TPU v7x, 128 devices: a whole 4x4x4 slice. The times are simulated.
128 devices in a mesh: dp: 4 (over y), label: 32 (over z, x, core).
Axes of the slice: x: 4, y: 4, z: 4, core: 2. Of those that a mesh axis runs over, the one named last changes fastest.
Arguments:
- queries: bfloat16 [32768, 768], P(('dp', 'label')), may hold values from -6 to 6
- weights: bfloat16 [32, 4096, 768], P('label'), as said below
- beam: int32 [256, 4], P(('dp', 'label')), may hold values from -1 to 31, as said below
- positives: int32 [32768], P(('dp', 'label')), may hold values from 0 to 131071, as said below
- owner: int32 [32], replicated, may hold values from 0 to 31, each once
Outputs:
- loss: float32 [32768], P(('dp', 'label'))
- grad_queries: float32 [32768, 768], P(('dp', 'label'))
- grad_weights: float32 [32, 4096, 768], P('label', 'dp')
Inputs may be any that keep to these rules, and one draw needn't show every extreme that they name: `beam`: each row lists 3 or 4 distinct block ids, then -1 entries. The query blocks of one device list pairwise different ids. Within each aligned group of 64 rows (the query blocks of one dp index) no id stands in more than 8 rows, and some id stands in exactly 8 rows. `positives`: the positive label id of query n lies in a block listed in the beam row of n // 128. `weights`: entries lie within -18 / sqrt(768) to 18 / sqrt(768).
All inputs are finite; a program needn't handle non-finite values.
Results may differ from a plain program's by a relative error of at most 0.013.
Values may be sent and summed in bfloat16 or wider, within the bound.
No kernel may reach another device: no remote copies, remote signals or barrier semaphores. Data moves between devices by JAX's collectives and lax.ppermute only.
A program may use at most 128 MiB of HBM per device.

v0:
```python
import functools

import jax
import jax.numpy as jnp
from jax import lax
from jax.experimental import pallas as pl
from jax.experimental.pallas import tpu as pltpu
from jax.sharding import PartitionSpec as P

F32 = jnp.float32
BF16 = jnp.bfloat16
NDEV = 32
SLOTS = 8
ROWS = 128
FEAT = 768
HALF = 384
LABELS = 4096
TILE = 512
BIG_TILE = 1024
PART_TILE = 256
NEG = -1e30
BIG = 1e30
LIMIT = 24

def iota(shape, dim):
    return lax.broadcasted_iota(jnp.int32, shape, dim)

def dot(a, b, dims):
    return lax.dot_general(a, b, (dims, ((), ())), preferred_element_type=F32)

def ones_where(mask):
    return jnp.where(mask, 1.0, 0.0).astype(BF16)

def slot_table(meta, held):
    n = held.shape[0]
    r = iota((256, 64), 0)
    q = iota((256, 64), 1)
    pick = ones_where((r // 8 == q % 32) & (r % 8 == 6 + q // 32))
    beams = dot(meta, pick, ((0,), (0,)))
    hit = held == beams[0:1, :]
    for k in range(1, 4):
        hit = hit | (held == beams[k : k + 1, :])
    hit = hit & (iota((n, 64), 1) >= 0)
    before = ones_where(iota((64, 64), 0) < iota((64, 64), 1))
    rank = dot(ones_where(hit), before, ((1,), (0,)))
    slot = (iota((n, 64), 0) % SLOTS).astype(F32)
    return jnp.where(hit & (rank == slot), 1.0, 0.0)

def piece_matrix(table):
    e = iota((64, 512), 1)
    spread = ones_where(iota((64, 512), 0) == e // 8)
    wide = dot(table.astype(BF16), spread, ((1,), (0,)))
    full = jnp.broadcast_to(wide[:, None, :], (256, 8, 512))
    same = iota((256, 8, 512), 1) == iota((256, 8, 512), 2) % 8
    return jnp.where(same, full, 0.0).reshape(2048, 512).astype(BF16)

def route_kernel(got_ref, held_ref, out_ref):
    got = got_ref[...]
    table = slot_table(got[:, FEAT:], held_ref[...][:, :1])
    m = piece_matrix(table)
    out = dot(m[:, :256], got[:, :HALF], ((1,), (0,)))
    out += dot(m[:, 256:], got[:, HALF:FEAT], ((1,), (0,)))
    out_ref[...] = out.astype(BF16)

def table_kernel(got_ref, held_ref, mine_ref, sel_ref, mask_ref, col_ref, slots_ref):
    meta = got_ref[...][:, FEAT:]
    table = slot_table(meta, held_ref[...][:, :1])
    sel_ref[...] = piece_matrix(table).T
    mine = mine_ref[...]
    own = slot_table(meta, mine[:, 0:1])
    row = iota((16, 64), 0)
    q = iota((16, 64), 1).astype(F32)
    home = jnp.where(q == (row.astype(F32) - 8.0) * 32.0 + mine[:, 1:2], 1.0, 0.0)
    own = jnp.where(row < 8, own, jnp.where(row < 10, home, 0.0)).astype(BF16)
    mask = dot(table.astype(BF16), own, ((1,), (1,)))
    mask_ref[...] = jnp.concatenate([mask, jnp.zeros((256, 112), F32)], axis=1)
    qq = iota((64, 256), 0)
    rr = iota((64, 256), 1)
    part = []
    for c in range(3):
        pick = ones_where((rr // 8 == qq % 32) & (rr % 8 == 3 * (qq // 32) + c))
        where_c = dot(own, pick, ((1,), (0,))).astype(BF16)
        part.append(dot(where_c, meta, ((1,), (0,))))
    inside = part[0] == mine[:, 0:1] + 1.0
    col = jnp.where(inside, part[1] * 64.0 + part[2], -1.0)
    slots_ref[...] = col[:SLOTS]
    for s in range(SLOTS):
        piece = col[s : s + 1].astype(jnp.int32)
        col_ref[:, s * ROWS : (s + 1) * ROWS] = jnp.broadcast_to(piece, (8, ROWS))

def start(copies):
    for c in copies:
        c.start()
    return copies

def pieces_kernel(q_hbm, pos_hbm, beam_hbm, out_ref, q_ref, pos_ref, beam_ref, sems):
    small = start(
        [
            pltpu.make_async_copy(pos_hbm, pos_ref, sems.at[0]),
            pltpu.make_async_copy(beam_hbm, beam_ref, sems.at[1]),
        ]
    )
    large = start(
        [
            pltpu.make_async_copy(q_hbm.at[:, pl.ds(8 * i, 8)], q_ref.at[:, pl.ds(8 * i, 8)], sems.at[2 + i])
            for i in range(2)
        ]
    )
    for c in small:
        c.wait()
    pos = pos_ref[...]
    beam = beam_ref[...]
    high, low = (pos >> 12) + 1, pos & (LABELS - 1)
    codes = (high, low >> 6, low & 63)
    row = iota((8, ROWS), 0)
    lane = iota((8, ROWS), 1)
    meta = jnp.full((8, ROWS), -1, jnp.int32)
    for b in range(2):
        for c in range(3):
            meta = jnp.where(row == 3 * b + c, codes[c][b : b + 1, :], meta)
        for k in range(beam.shape[1]):
            meta = jnp.where((row == 6 + b) & (lane == k), beam[b : b + 1, k : k + 1], meta)
    meta = meta.astype(F32).astype(BF16)
    out_ref[:, :, :, FEAT:] = jnp.broadcast_to(meta[None, None], (16, 2, 8, ROWS))
    for i in range(2):
        large[i].wait()
        g = slice(8 * i, 8 * i + 8)
        for h in range(2):
            for b in range(2):
                out_ref[g, h, :, b * HALF : (b + 1) * HALF] = q_ref[b, g, :, h * HALF : (h + 1) * HALF]

def by_slot(lanes):
    row = iota((SLOTS, ROWS), 0)
    out = jnp.zeros((SLOTS, ROWS), F32)
    for s in range(SLOTS):
        out = jnp.where(row == s, lanes[:, s * ROWS : (s + 1) * ROWS], out)
    return out

def scores_kernel(got_ref, col_ref, w_ref, p_ref, q_ref, top_ref, stat_ref, row_ref, s_ref, high, total, found):
    step = pl.program_id(0)
    rows = s_ref.shape[1]

    @pl.when(step == 0)
    def _():
        for g in range(16):
            for h in range(2):
                for s in range(SLOTS):
                    here = slice(s * ROWS + g * 8, s * ROWS + g * 8 + 8)
                    q_ref[here, h * HALF : (h + 1) * HALF] = got_ref[g, h, s]
        high[...] = jnp.full_like(high, NEG)
        total[...] = jnp.zeros_like(total)
        found[...] = jnp.zeros_like(found)

    n = BIG_TILE // PART_TILE
    top, tot, pick = high[...], total[...], found[...]
    for k in range(n + 1):
        if k < n:
            here = slice(k * PART_TILE, (k + 1) * PART_TILE)
            s_ref[here, :] = dot(w_ref[here, :], q_ref[...], ((1,), (1,)))
        if k > 0:
            here = slice((k - 1) * PART_TILE, k * PART_TILE)
            s = s_ref[here, :]
            target = iota(s.shape, 0) + (step * BIG_TILE + (k - 1) * PART_TILE) == col_ref[0:1, :]
            pick += jnp.sum(jnp.where(target, s, 0.0).reshape(PART_TILE // 8, 8, rows), axis=0)
            best = jnp.max(jnp.max(s.reshape(PART_TILE // 8, 8, rows), axis=0), axis=0, keepdims=True)
            best = jnp.broadcast_to(best, (8, rows))
            e = jnp.exp(s - best[0:1, :])
            p_ref[here, :] = jnp.where(target, 0.0, e).astype(BF16)
            new = jnp.maximum(top, best)
            add = jnp.sum(e.reshape(PART_TILE // 8, 8, rows), axis=0)
            tot = tot * jnp.exp(top - new) + add * jnp.exp(best - new)
            top = new
            top_ref[k - 1] = best
    high[...], total[...], found[...] = top, tot, pick

    @pl.when(step == pl.num_programs(0) - 1)
    def _():
        lse = top[0:1, :] + jnp.log(jnp.sum(tot, axis=0, keepdims=True))
        row_ref[...] = jnp.broadcast_to(lse, (8, rows))
        chosen = jnp.sum(pick, axis=0, keepdims=True)
        stat_ref[:, :SLOTS, :] = jnp.broadcast_to(by_slot(lse)[None], (NDEV, SLOTS, ROWS))
        stat_ref[:, SLOTS:, :] = jnp.broadcast_to(by_slot(chosen)[None], (NDEV, SLOTS, ROWS))


def normal_kernel(stat_ref, mask_ref, norm_ref, rest_ref, slots_ref, loss_ref):
    lse = stat_ref[:, :SLOTS, :].reshape(NDEV * SLOTS, ROWS)
    found = stat_ref[:, SLOTS:, :].reshape(NDEV * SLOTS, ROWS)
    mask = mask_ref[...]
    for s in range(SLOTS + 2):
        use = mask[:, s : s + 1] > 0.5
        kept = jnp.where(use, lse, NEG)
        high = jnp.max(kept, axis=0, keepdims=True)
        tot = jnp.sum(jnp.where(use, jnp.exp(kept - high), 0.0), axis=0, keepdims=True)
        value = jnp.where(high > 0.5 * NEG, high + jnp.log(tot), BIG)
        positive = jnp.sum(jnp.where(use, found, 0.0), axis=0, keepdims=True)
        if s < SLOTS:
            here = slice(s * ROWS, (s + 1) * ROWS)
            norm_ref[:, here] = jnp.broadcast_to(value, (8, ROWS))
            rest_ref[:, here] = jnp.broadcast_to(jnp.exp(positive - value) - 1.0, (8, ROWS))
            slots_ref[s : s + 1, :] = value
        else:
            loss_ref[s - SLOTS : s - SLOTS + 1, :] = value - positive


def rows_from(acc, out_ref):
    for s in range(SLOTS):
        here = slice(s * ROWS, (s + 1) * ROWS)
        out_ref[here, :] = acc[:, here].T.astype(out_ref.dtype)


def add_to(acc, term, first):
    @pl.when(first)
    def _():
        acc[...] = term

    @pl.when(jnp.logical_not(first))
    def _():
        acc[...] += term


def positive_kernel(col_ref, w_ref, out_ref, acc):
    step = pl.program_id(0)
    target = iota((BIG_TILE, acc.shape[1]), 0) + step * BIG_TILE == col_ref[0:1, :]
    add_to(acc, dot(w_ref[...], ones_where(target), ((0,), (0,))), step == 0)

    @pl.when(step == pl.num_programs(0) - 1)
    def _():
        rows_from(acc, out_ref)


def others_kernel(top_ref, row_ref, w_ref, p_ref, out_ref, acc):
    step = pl.program_id(0)
    term = None
    for k in range(0, BIG_TILE // PART_TILE, 2):
        pair = []
        for i in (k, k + 1):
            scale = jnp.exp(top_ref[i][0:1, :] - row_ref[0:1, :])
            here = slice(i * PART_TILE, (i + 1) * PART_TILE)
            pair.append((p_ref[here, :].astype(F32) * scale).astype(BF16))
        here = slice(k * PART_TILE, (k + 2) * PART_TILE)
        one = dot(w_ref[here, :], jnp.concatenate(pair, axis=0), ((0,), (0,)))
        term = one if term is None else term + one
    add_to(acc, term, step == 0)

    @pl.when(step == pl.num_programs(0) - 1)
    def _():
        rows_from(acc, out_ref)


def part_kernel(u_ref, r_ref, stat_ref, norm_ref, col_ref, out_ref):
    norm = norm_ref[...]
    scale = jnp.exp(stat_ref[0, :SLOTS, :] - norm).T
    rest = jnp.where(col_ref[...] >= 0.0, jnp.exp(stat_ref[0, SLOTS:, :] - norm) - 1.0, 0.0).T
    for s in range(SLOTS):
        u = u_ref[s * ROWS : (s + 1) * ROWS, :].astype(F32)
        r = r_ref[s * ROWS : (s + 1) * ROWS, :].astype(F32)
        part = (scale[:, s : s + 1] * u + rest[:, s : s + 1] * r).astype(BF16).reshape(16, 8, FEAT)
        for h in range(2):
            out_ref[:, h, s * 8 : (s + 1) * 8, :] = part[:, :, h * HALF : (h + 1) * HALF]


def table_grad_kernel(base, tiles_ref, q_ref, top_ref, norm_ref, rest_ref, col_ref, p_ref, *out_refs):
    step = pl.program_id(0)
    first = tiles_ref[base + step] * TILE
    for k in range(TILE // PART_TILE):
        here = slice(k * PART_TILE, (k + 1) * PART_TILE)
        scale = jnp.exp(top_ref[tiles_ref[base + step] * (TILE // PART_TILE) + k][0:1, :] - norm_ref[0:1, :])
        p = p_ref[here, :].astype(F32)
        target = iota(p.shape, 0) + (first + k * PART_TILE) == col_ref[0:1, :]
        slope = jnp.where(target, rest_ref[0:1, :], p * scale).astype(BF16)
        value = dot(slope, q_ref[...], ((1,), (0,)))
        for i, ref in enumerate(out_refs):

            @pl.when(step == i)
            def _(ref=ref):
                ref[here, :] = value.astype(ref.dtype)


def sum_kernel(sel_ref, parts_ref, out_ref):
    out = dot(sel_ref[...], parts_ref[...], ((1,), (0,))).astype(BF16)
    for b in range(2):
        out_ref[:, :, b * HALF : (b + 1) * HALF] = out[b * 256 : (b + 1) * 256].reshape(NDEV, 8, HALF)

def home_kernel(got_ref, out_ref):
    for h in range(2):
        for b in range(2):
            out_ref[b, :, :, h * HALF : (h + 1) * HALF] = got_ref[:, h, :, b * HALF : (b + 1) * HALF].astype(F32)

def relay_kernel(up_ref, down_ref, got_up_ref, got_down_ref, out_up_ref, out_down_ref):
    out_up_ref[...] = (up_ref[...] + got_up_ref[...].astype(F32)).astype(BF16)
    out_down_ref[...] = (down_ref[...] + got_down_ref[...].astype(F32)).astype(BF16)


def base_kernel(own_a_ref, own_b_ref, a_ref, b_ref, out_ref):
    out_ref[:TILE, :] = own_a_ref[...] + a_ref[...].astype(F32)
    out_ref[TILE:, :] = own_b_ref[...] + b_ref[...].astype(F32)


def finish_kernel(base_ref, a_ref, b_ref, out_hbm, out_v, out_sems):
    copies = []
    for i, ref in enumerate((a_ref, b_ref)):
        here = pl.ds(i * TILE, TILE)
        out_v[i * TILE : (i + 1) * TILE, :] = base_ref[i * TILE : (i + 1) * TILE, :] + ref[...].astype(F32)
        c = pltpu.make_async_copy(out_v.at[here], out_hbm.at[here], out_sems.at[i])
        c.start()
        copies.append(c)
    for c in copies:
        c.wait()


def shape(dims, dtype):
    return jax.ShapeDtypeStruct(dims, dtype)

def whole(kernel, out, *args, hbm=(), smem=(), hbm_out=(), limit=60, cost=1024, scratch=()):
    def place(i, far, scalar=()):
        space = pltpu.HBM if i in far else pltpu.SMEM if i in scalar else pltpu.VMEM
        return pl.BlockSpec(memory_space=space)

    single = not isinstance(out, tuple)
    outs = (out,) if single else out
    results = pl.pallas_call(
        kernel,
        out_shape=outs,
        in_specs=[place(i, hbm, smem) for i in range(len(args))],
        out_specs=tuple(place(i, hbm_out) for i in range(len(outs))),
        scratch_shapes=list(scratch),
        compiler_params=pltpu.CompilerParams(vmem_limit_bytes=limit << 20),
        cost_estimate=pl.CostEstimate(flops=cost, transcendentals=0, bytes_accessed=1024),
    )(*args)
    return results[0] if single else results

def fixed(dims):
    return pl.BlockSpec(dims, lambda *_: (0,) * len(dims))


def tiled(dims):
    return pl.BlockSpec(dims, lambda i, *_: (i,) + (0,) * (len(dims) - 1))


def stepped(kernel, grid, in_specs, outs, out_specs, scratch, *args, limit=LIMIT, scalars=0, cost=1024):
    spec = pltpu.PrefetchScalarGridSpec(
        num_scalar_prefetch=scalars,
        grid=(grid,),
        in_specs=in_specs,
        out_specs=out_specs,
        scratch_shapes=list(scratch),
    )
    return pl.pallas_call(
        kernel,
        grid_spec=spec,
        out_shape=outs,
        compiler_params=pltpu.CompilerParams(vmem_limit_bytes=limit << 20),
        cost_estimate=pl.CostEstimate(flops=cost, transcendentals=0, bytes_accessed=1024),
    )(*args)


def sems(n):
    return pltpu.SemaphoreType.DMA((n,))


def per_device(queries, weights, beam, positives, owner):
    me = lax.axis_index("label")
    y = lax.axis_index("dp")
    rows = SLOTS * ROWS
    ranker = pltpu.with_memory_space_constraint(weights[0], pltpu.HBM)

    def swap(x):
        return lax.all_to_all(x, "label", split_axis=0, concat_axis=0, tiled=True)

    ids = jnp.arange(NDEV, dtype=jnp.int32)
    held = jnp.sum(jnp.where(owner[None, :] == ids[:, None], ids[None, :], 0), axis=1).astype(F32)
    held_rows = jnp.broadcast_to(held[:, None, None], (NDEV, SLOTS, 128)).reshape(256, 128)
    my_block = jnp.sum(jnp.where(owner == me, ids, 0)).astype(F32)
    mine = jnp.where(iota((16, 128), 1) == 0, my_block, me.astype(F32))

    pieces = whole(
        pieces_kernel,
        shape((16, 2, 8, FEAT + ROWS), BF16),
        queries.reshape(2, 16, 8, FEAT),
        positives.reshape(2, ROWS),
        beam,
        hbm=(0, 1, 2),
        scratch=(
            pltpu.VMEM((2, 16, 8, FEAT), BF16),
            pltpu.VMEM((2, ROWS), jnp.int32),
            pltpu.VMEM(beam.shape, jnp.int32),
            sems(4),
        ),
    )
    got = swap(pieces.reshape(NDEV, 8, FEAT + ROWS)).reshape(256, FEAT + ROWS)

    sent = whole(route_kernel, shape((2048, HALF), BF16), got, held_rows, limit=16)
    arrived = swap(sent.reshape(NDEV, 64, HALF))
    sel, mask, col, col_slots = whole(
        table_kernel,
        (
            shape((512, 2048), BF16),
            shape((256, 128), F32),
            shape((8, rows), jnp.int32),
            shape((SLOTS, ROWS), F32),
        ),
        got,
        held_rows,
        mine,
    )
    steps = LABELS // BIG_TILE
    w_spec = tiled((BIG_TILE, FEAT))
    lanes = shape((8, rows), F32)
    positive_rows = stepped(
        positive_kernel,
        steps,
        [fixed((8, rows)), w_spec],
        shape((rows, FEAT), BF16),
        fixed((rows, FEAT)),
        (pltpu.VMEM((FEAT, rows), F32),),
        col,
        ranker,
    )
    arrived, positive_rows, col = lax.optimization_barrier((arrived, positive_rows, col))

    parts_each = BIG_TILE // PART_TILE
    p, q, tops, stats, lse_row = stepped(
        scores_kernel,
        steps,
        [fixed((16, 2, SLOTS, 8, HALF)), fixed((8, rows)), w_spec],
        (
            pltpu.HBM((LABELS, rows), BF16),
            shape((rows, FEAT), BF16),
            shape((LABELS // PART_TILE, 8, rows), F32),
            shape((NDEV, 2 * SLOTS, ROWS), F32),
            lanes,
        ),
        (
            tiled((BIG_TILE, rows)),
            fixed((rows, FEAT)),
            tiled((parts_each, 8, rows)),
            fixed((NDEV, 2 * SLOTS, ROWS)),
            fixed((8, rows)),
        ),
        (
            pltpu.VMEM((BIG_TILE, rows), F32),
            pltpu.VMEM((8, rows), F32),
            pltpu.VMEM((8, rows), F32),
            pltpu.VMEM((8, rows), F32),
        ),
        pltpu.with_memory_space_constraint(arrived.reshape(16, 2, SLOTS, 8, HALF), pltpu.HBM),
        col,
        ranker,
    )
    all_stats = swap(stats)
    p = pltpu.with_memory_space_constraint(p, pltpu.HBM)
    others = stepped(
        others_kernel,
        steps,
        [tiled((parts_each, 8, rows)), fixed((8, rows)), w_spec, tiled((BIG_TILE, rows))],
        pltpu.HBM((rows, FEAT), BF16),
        fixed((rows, FEAT)),
        (pltpu.VMEM((FEAT, rows), F32),),
        tops,
        lse_row,
        ranker,
        p,
    )
    all_stats, others = lax.optimization_barrier((all_stats, others))
    norm, rest, norm_slots, loss = whole(
        normal_kernel,
        (lanes, lanes, shape((SLOTS, ROWS), F32), shape((2, ROWS), F32)),
        all_stats,
        mask,
        limit=16,
    )

    up = [(i, (i + 1) % 4) for i in range(4)]
    down = [(i, (i + 3) % 4) for i in range(4)]
    across, ahead, behind = (y + 2) % 4 * 2, (y + 1) % 4 * 2, (y + 3) % 4 * 2
    tiles = jnp.stack([across, across + 1, ahead + 1, behind, ahead, behind + 1, y * 2, y * 2 + 1])
    tiles = tiles.astype(jnp.int32)

    def table_grads(first, norm, dtypes):
        n = len(dtypes)
        return stepped(
            functools.partial(table_grad_kernel, first),
            n,
            [
                fixed((rows, FEAT)),
                fixed((LABELS // PART_TILE, 8, rows)),
                fixed((8, rows)),
                fixed((8, rows)),
                fixed((8, rows)),
                pl.BlockSpec((TILE, rows), lambda i, t: (t[first + i], 0)),
            ],
            tuple(pltpu.HBM((TILE, FEAT), d) for d in dtypes),
            tuple(fixed((TILE, FEAT)) for _ in dtypes),
            (),
            tiles,
            q,
            tops,
            norm,
            rest,
            col,
            p,
            scalars=1,
        )

    far_a, far_b = table_grads(0, norm, (BF16, BF16))
    far_a, far_b, norm_slots, norm = lax.optimization_barrier((far_a, far_b, norm_slots, norm))
    via_up = lax.ppermute(far_a, "dp", up)
    via_down = lax.ppermute(far_b, "dp", down)
    part = whole(
        part_kernel,
        pltpu.HBM((16, 2, 64, HALF), BF16),
        others,
        positive_rows,
        stats,
        norm_slots,
        col_slots,
        limit=16,
    )
    part, norm = lax.optimization_barrier((part, norm))
    parts = swap(part.reshape(NDEV, 64, HALF)).reshape(2048, HALF)
    next_b, prev_a = table_grads(2, norm, (BF16, BF16))
    next_b, prev_a, norm = lax.optimization_barrier((next_b, prev_a, norm))
    from_prev_b = lax.ppermute(next_b, "dp", up)
    from_next_a = lax.ppermute(prev_a, "dp", down)
    next_a, prev_b, own_a, own_b = table_grads(4, norm, (F32, F32, F32, F32))

    relay_up, relay_down = whole(
        relay_kernel,
        (shape((TILE, FEAT), BF16), shape((TILE, FEAT), BF16)),
        next_a,
        prev_b,
        via_up,
        via_down,
        limit=16,
        cost=50_000_000_000,
    )
    from_prev_a = lax.ppermute(relay_up, "dp", up)
    from_next_b = lax.ppermute(relay_down, "dp", down)

    homeward = whole(sum_kernel, shape((NDEV, 8, FEAT), BF16), sel, parts, limit=16)
    home = swap(homeward).reshape(16, 2, 8, FEAT)
    grad_queries = whole(home_kernel, shape((2, 16, 8, FEAT), F32), home, limit=16).reshape(256, FEAT)
    base = whole(
        base_kernel,
        shape((2 * TILE, FEAT), F32),
        own_a,
        own_b,
        from_next_a,
        from_prev_b,
        limit=16,
    )
    base, grad_queries = lax.optimization_barrier((base, grad_queries))
    grad_table = whole(
        finish_kernel,
        shape((2 * TILE, FEAT), F32),
        base,
        from_prev_a,
        from_next_b,
        hbm_out=(0,),
        limit=16,
        scratch=(pltpu.VMEM((2 * TILE, FEAT), F32), sems(2)),
    )
    return loss.reshape(256), grad_queries, grad_table[None]

def solution(mesh):
    placed = (
        P(("dp", "label"), None),
        P("label", None, None),
        P(("dp", "label"), None),
        P(("dp", "label")),
        P(),
    )
    return jax.shard_map(
        per_device,
        mesh=mesh,
        in_specs=placed,
        out_specs=(P(("dp", "label")), P(("dp", "label"), None), P("label", "dp", None)),
        check_vma=False,
    )
```

profile of v0, /device:TPU:2, one launch (start us, length us, event | category | flops | bytes accessed | tf_op | source)
XLA Modules:
  0.0 164.1 jit_solution(8901929886616444700)
XLA Ops:
  0.6 1.9 %shard_map.76 = bf16[16,2,8,896]{3,2,1,0:T(8,128)(2,1)} custom-call(bf16[2,16,8,768]{3,2,1,0:T(8,128)(2,1)} %bitcast.32, s32[2,128]{1,0:T(2,128)} %bitcast.33, s32[2,4]{1,0:T(2,128)} %beam_hbm.1), custom_call_target="tpu_custom_call" | custom-call | flops 1024 | bytes 1024 | tf_op jit(solution)/shard_map/pallas_call | solution.py:321
  2.5 8.5 %all-to-all-start = ((bf16[32,8,896]{2,1,0:T(8,128)(2,1)}), bf16[32,8,896]{2,1,0:T(8,128)(2,1)S(1)}, u32[]{:S(2)}, u32[]{:S(2)}) async-start(bf16[32,8,896]{2,1,0:T(8,128)(2,1)} %bitcast.30), calls=%async_computation | async-start | bytes 917504 | tf_op jit(solution)/shard_map/all_to_all | solution.py:368
  11.0 0.1 select_reduce_fusion
  11.1 0.1 broadcast_in_dim.42
  11.2 0.1 broadcast_in_dim.43
  11.3 9.5 %all-to-all-done = bf16[32,8,896]{2,1,0:T(8,128)(2,1)S(1)} async-done(((bf16[32,8,896]{2,1,0:T(8,128)(2,1)}), bf16[32,8,896]{2,1,0:T(8,128)(2,1)S(1)}, u32[]{:S(2)}, u32[]{:S(2)}) %all-to-all-start) | async-done | bytes 458784 | tf_op jit(solution)/shard_map/all_to_all | solution.py:368
  20.8 0.1 broadcast_in_dim.44.held_ref
  20.9 2.9 %shard_map.77 = bf16[2048,384]{1,0:T(8,128)(2,1)} custom-call(bf16[256,896]{1,0:T(8,128)(2,1)S(1)} %bitcast.21, f32[256,128]{1,0:T(8,128)S(1)} %broadcast_in_dim.44.held_ref), custom_call_target="tpu_custom_call" | custom-call | flops 1024 | bytes 1024 | tf_op jit(solution)/shard_map/pallas_call | solution.py:321
  23.8 5.1 %all-to-all-start.1 = ((bf16[32,64,384]{2,1,0:T(8,128)(2,1)}), bf16[32,64,384]{2,1,0:T(8,128)(2,1)S(1)}, u32[]{:S(2)}, u32[]{:S(2)}) async-start(bf16[32,64,384]{2,1,0:T(8,128)(2,1)} %bitcast.4), calls=%async_computation.1 | async-start | bytes 3145728 | tf_op jit(solution)/shard_map/all_to_all | solution.py:368
  28.9 0.6 fusion
  30.2 0.6 iota.17.mine_ref
  30.8 3.7 %shard_map.78 = (bf16[512,2048]{1,0:T(8,128)(2,1)}, f32[256,128]{1,0:T(8,128)}, s32[8,1024]{1,0:T(8,128)}, f32[8,128]{1,0:T(8,128)}) custom-call(bf16[256,896]{1,0:T(8,128)(2,1)} %bitcast.22, f32[256,128]{1,0:T(8,128)} %copy-done.7, f32[16,128]{1,0:T(8,128)} %iota.17.mine_ref), custom_call_target="tpu_custom_call" | custom-call | flops 1024 | bytes 1024 | tf_op jit(solution)/shard_map/pallas_call | solution.py:321
  34.5 0.8 copy-done.8
  35.2 10.4 %shard_map.79.r_ref = bf16[1024,768]{1,0:T(8,128)(2,1)S(1)} custom-call(s32[8,1024]{1,0:T(8,128)S(1)} %copy-done.8, bf16[4096,768]{1,0:T(8,128)(2,1)} %bitcast.24), custom_call_target="tpu_custom_call" | custom-call | flops 1024 | bytes 1024 | tf_op jit(solution)/shard_map/pallas_call | solution.py:348
  45.6 1.2 copy-done.1
  46.8 4.3 %all-to-all-done.1 = bf16[32,64,384]{2,1,0:T(8,128)(2,1)S(1)} async-done(((bf16[32,64,384]{2,1,0:T(8,128)(2,1)}), bf16[32,64,384]{2,1,0:T(8,128)(2,1)S(1)}, u32[]{:S(2)}, u32[]{:S(2)}) %all-to-all-start.1) | async-done | bytes 1572896 | tf_op jit(solution)/shard_map/all_to_all | solution.py:368
  51.1 1.1 copy-done.16
  52.2 13.5 %shard_map.80 = (bf16[4096,1024]{1,0:T(8,128)(2,1)}, bf16[1024,768]{1,0:T(8,128)(2,1)S(1)}, f32[16,8,1024]{2,1,0:T(8,128)S(1)}, f32[32,16,128]{2,1,0:T(8,128)}, f32[8,1024]{1,0:T(8,128)S(1)}) custom-call(bf16[16,2,8,8,384]{4,3,2,1,0:T(8,128)(2,1)} %bitcast.28, s32[8,1024]{1,0:T(8,128)S(1)} %copy-done.9, bf16[4096,768]{1,0:T(8,128)(2,1)} %bitcast.25), custom_call_target="tpu_custom_call" | custom-call | flops 1024 | bytes 1024 | tf_op jit(solution)/shard_map/pallas_call | solution.py:348
  65.7 5.7 %all-to-all-start.2 = ((f32[32,16,128]{2,1,0:T(8,128)}), f32[32,16,128]{2,1,0:T(8,128)S(1)}, u32[]{:S(2)}, u32[]{:S(2)}) async-start(f32[32,16,128]{2,1,0:T(8,128)} %get-tuple-element.45.stat_ref), calls=%async_computation.2 | async-start | bytes 524288 | tf_op jit(solution)/shard_map/all_to_all | solution.py:368
  71.4 0.1 stack.35.tiles_ref
  71.5 12.2 %shard_map.81.u_ref = bf16[1024,768]{1,0:T(8,128)(2,1)} custom-call(f32[16,8,1024]{2,1,0:T(8,128)S(1)} %get-tuple-element.46.top_ref, f32[8,1024]{1,0:T(8,128)S(1)} %get-tuple-element.47.row_ref, bf16[4096,768]{1,0:T(8,128)(2,1)} %bitcast.26, bf16[4096,1024]{1,0:T(8,128)(2,1)} %get-tuple-element.48.p_ref), custom_call_target="tpu_custom_call" | custom-call | flops 1024 | bytes 1024 | tf_op jit(solution)/shard_map/pallas_call | solution.py:348
  83.8 1.2 shard_map.82
  85.0 6.2 %shard_map.83 = (bf16[512,768]{1,0:T(8,128)(2,1)}, bf16[512,768]{1,0:T(8,128)(2,1)}) custom-call(s32[8]{0:T(128)S(1)} %stack.35.tiles_ref, bf16[1024,768]{1,0:T(8,128)(2,1)S(1)} %get-tuple-element.52.q_ref, f32[16,8,1024]{2,1,0:T(8,128)S(1)} %get-tuple-element.46.top_ref, f32[8,1024]{1,0:T(8,128)S(1)} %get-tuple-element.66.norm_ref, ...), custom_call_target="tpu_custom_call" | custom-call | flops 1024 | bytes 1024 | tf_op jit(solution)/shard_map/pallas_call | solution.py:348
  91.1 1.6 collective-permute-start.2
  92.7 1.7 %collective-permute-start.3 = (bf16[512,768]{1,0:T(8,128)(2,1)}, bf16[512,768]{1,0:T(8,128)(2,1)}, u32[]{:S(2)}, u32[]{:S(2)}) collective-permute-start(bf16[512,768]{1,0:T(8,128)(2,1)} %get-tuple-element.78), channel_id=1, source_target_pairs={{0,96},{32,0},{64,32},{96,64},{1,97},{33,1},{65,33},{97,65},{2,98}... | collective-permute-start | bytes 2359304 | tf_op jit(solution)/shard_map/ppermute | solution.py:508
  94.4 2.9 %shard_map.84 = bf16[16,2,64,384]{3,2,1,0:T(8,128)(2,1)} custom-call(bf16[1024,768]{1,0:T(8,128)(2,1)S(1)} %copy-done, bf16[1024,768]{1,0:T(8,128)(2,1)S(1)} %copy-done.2, f32[32,16,128]{2,1,0:T(8,128)} %get-tuple-element.45.stat_ref, f32[8,128]{1,0:T(8,128)S(1)} %get-tuple-element.60.norm_ref, f32[8,128]{1,0:T(8,128)S(1)} %copy-done.13), custom_call_target="tpu_custom_call" | custom-call | flops 1024 | bytes 1024 | tf_op jit(solution)/shard_map/pallas_call | solution.py:321
  97.3 7.5 %all-to-all-start.3 = ((bf16[32,64,384]{2,1,0:T(8,128)(2,1)}), bf16[32,64,384]{2,1,0:T(8,128)(2,1)}, u32[]{:S(2)}, u32[]{:S(2)}) async-start(bf16[32,64,384]{2,1,0:T(8,128)(2,1)} %bitcast.27), calls=%async_computation.3 | async-start | bytes 3145728 | tf_op jit(solution)/shard_map/all_to_all | solution.py:368
  104.8 5.9 %shard_map.85 = (bf16[512,768]{1,0:T(8,128)(2,1)}, bf16[512,768]{1,0:T(8,128)(2,1)}) custom-call(s32[8]{0:T(128)S(1)} %stack.35.tiles_ref, bf16[1024,768]{1,0:T(8,128)(2,1)S(1)} %get-tuple-element.52.q_ref, f32[16,8,1024]{2,1,0:T(8,128)S(1)} %get-tuple-element.46.top_ref, f32[8,1024]{1,0:T(8,128)S(1)} %get-tuple-element.66.norm_ref, ...), custom_call_target="tpu_custom_call" | custom-call | flops 1024 | bytes 1024 | tf_op jit(solution)/shard_map/pallas_call | solution.py:348
  110.7 10.5 %shard_map.86 = (f32[512,768]{1,0:T(8,128)}, f32[512,768]{1,0:T(8,128)}, f32[512,768]{1,0:T(8,128)}, f32[512,768]{1,0:T(8,128)}) custom-call(s32[8]{0:T(128)S(1)} %stack.35.tiles_ref, bf16[1024,768]{1,0:T(8,128)(2,1)S(1)} %get-tuple-element.52.q_ref, f32[16,8,1024]{2,1,0:T(8,128)S(1)} %get-tuple-element.46.top_ref, ...), custom_call_target="tpu_custom_call" | custom-call | flops 1024 | bytes 1024 | tf_op jit(solution)/shard_map/pallas_call | solution.py:348
  121.2 1.8 %collective-permute-start = (bf16[512,768]{1,0:T(8,128)(2,1)}, bf16[512,768]{1,0:T(8,128)(2,1)S(1)}, u32[]{:S(2)}, u32[]{:S(2)}) collective-permute-start(bf16[512,768]{1,0:T(8,128)(2,1)} %get-tuple-element.69), channel_id=1, source_target_pairs={{0,96},{32,0},{64,32},{96,64},{1,97},{33,1},{65,33},{97,65},{2,98}... | collective-permute-start | bytes 2359304 | tf_op jit(solution)/shard_map/ppermute | solution.py:524
  123.0 0.2 collective-permute-start.1
  123.3 1.4 copy-done.14
  124.7 1.4 copy-done.15
  126.1 2.9 %shard_map.90 = (bf16[512,768]{1,0:T(8,128)(2,1)}, bf16[512,768]{1,0:T(8,128)(2,1)}) custom-call(f32[512,768]{1,0:T(8,128)S(1)} %copy-done.14, f32[512,768]{1,0:T(8,128)S(1)} %copy-done.15, bf16[512,768]{1,0:T(8,128)(2,1)} %collective-permute-done.2.got_up_ref, bf16[512,768]{1,0:T(8,128)(2,1)} %collective-permute-done.3.got_down_ref), custom_call_target="tpu_custom_call" | custom-call | flops 49999998976 | bytes 1024 | tf_op jit(solution)/shard_map/pallas_call | solution.py:321
  129.0 0.4 collective-permute-start.4
  129.3 2.9 %collective-permute-start.5 = (bf16[512,768]{1,0:T(8,128)(2,1)}, bf16[512,768]{1,0:T(8,128)(2,1)}, u32[]{:S(2)}, u32[]{:S(2)}) collective-permute-start(bf16[512,768]{1,0:T(8,128)(2,1)} %get-tuple-element.80), channel_id=1, source_target_pairs={{0,96},{32,0},{64,32},{96,64},{1,97},{33,1},{65,33},{97,65},{2,98}... | collective-permute-start | bytes 2359304 | tf_op jit(solution)/shard_map/ppermute | solution.py:538
  132.2 3.4 %shard_map.88 = bf16[32,8,768]{2,1,0:T(8,128)(2,1)} custom-call(bf16[512,2048]{1,0:T(8,128)(2,1)S(1)} %copy-done.4, bf16[2048,384]{1,0:T(8,128)(2,1)} %bitcast.17.parts_ref), custom_call_target="tpu_custom_call" | custom-call | flops 1024 | bytes 1024 | tf_op jit(solution)/shard_map/pallas_call | solution.py:321
  135.6 7.4 %all-to-all-start.4 = ((bf16[32,8,768]{2,1,0:T(8,128)(2,1)}), bf16[32,8,768]{2,1,0:T(8,128)(2,1)S(1)}, u32[]{:S(2)}, u32[]{:S(2)}) async-start(bf16[32,8,768]{2,1,0:T(8,128)(2,1)} %shard_map.88), calls=%async_computation.4 | async-start | bytes 786432 | tf_op jit(solution)/shard_map/all_to_all | solution.py:368
  143.0 0.9 copy-done.10
  143.9 1.1 collective-permute-done.1.b_ref
  145.0 1.4 copy-done.5
  146.4 1.4 copy-done.6
  147.8 1.1 copy-done.11
  148.9 1.4 shard_map.87.base_ref
  150.3 1.8 %all-to-all-done.4 = bf16[32,8,768]{2,1,0:T(8,128)(2,1)S(1)} async-done(((bf16[32,8,768]{2,1,0:T(8,128)(2,1)}), bf16[32,8,768]{2,1,0:T(8,128)(2,1)S(1)}, u32[]{:S(2)}, u32[]{:S(2)}) %all-to-all-start.4) | async-done | bytes 393248 | tf_op jit(solution)/shard_map/all_to_all | solution.py:368
  152.1 0.9 shard_map.89
  153.0 7.7 %collective-permute-done.4.a_ref = bf16[512,768]{1,0:T(8,128)(2,1)} collective-permute-done((bf16[512,768]{1,0:T(8,128)(2,1)}, bf16[512,768]{1,0:T(8,128)(2,1)}, u32[]{:S(2)}, u32[]{:S(2)}) %collective-permute-start.4) | collective-permute-done | bytes 786464 | tf_op jit(solution)/shard_map/ppermute | solution.py:537
  160.7 3.2 %shard_map.91 = f32[1024,768]{1,0:T(8,128)} custom-call(f32[1024,768]{1,0:T(8,128)S(1)} %shard_map.87.base_ref, bf16[512,768]{1,0:T(8,128)(2,1)} %collective-permute-done.4.a_ref, bf16[512,768]{1,0:T(8,128)(2,1)} %collective-permute-done.5.b_ref), custom_call_target="tpu_custom_call" | custom-call | flops 1024 | bytes 1024 | tf_op jit(solution)/shard_map/pallas_call | solution.py:321
  (35 shorter events, 0.1 us)
Async XLA Ops:
  0.6 10.4 %copy-start.17 = (s32[32]{0:T(128)S(1)}, s32[32]{0:T(128)}, u32[]{:S(2)}) copy-start(s32[32]{0:T(128)} %param.9) | copy-start | bytes 388
  2.5 18.3 %all-to-all-start = ((bf16[32,8,896]{2,1,0:T(8,128)(2,1)}), bf16[32,8,896]{2,1,0:T(8,128)(2,1)S(1)}, u32[]{:S(2)}, u32[]{:S(2)}) async-start(bf16[32,8,896]{2,1,0:T(8,128)(2,1)} %bitcast.30), calls=%async_computation | async-start | bytes 917504 | tf_op jit(solution)/shard_map/all_to_all | solution.py:368
  20.8 3.0 %copy-start.3 = (bf16[32,8,896]{2,1,0:T(8,128)(2,1)}, bf16[32,8,896]{2,1,0:T(8,128)(2,1)S(1)}, u32[]{:S(2)}) copy-start(bf16[32,8,896]{2,1,0:T(8,128)(2,1)S(1)} %all-to-all-done) | copy-start | bytes 1376260
  20.9 2.9 %copy-start.7 = (f32[256,128]{1,0:T(8,128)}, f32[256,128]{1,0:T(8,128)S(1)}, u32[]{:S(2)}) copy-start(f32[256,128]{1,0:T(8,128)S(1)} %broadcast_in_dim.44.held_ref) | copy-start | bytes 393220
  23.8 27.2 %all-to-all-start.1 = ((bf16[32,64,384]{2,1,0:T(8,128)(2,1)}), bf16[32,64,384]{2,1,0:T(8,128)(2,1)S(1)}, u32[]{:S(2)}, u32[]{:S(2)}) async-start(bf16[32,64,384]{2,1,0:T(8,128)(2,1)} %bitcast.4), calls=%async_computation.1 | async-start | bytes 3145728 | tf_op jit(solution)/shard_map/all_to_all | solution.py:368
  34.5 0.8 copy-start.8
  35.2 17.0 %copy-start.9 = (s32[8,1024]{1,0:T(8,128)S(1)}, s32[8,1024]{1,0:T(8,128)}, u32[]{:S(2)}) copy-start(s32[8,1024]{1,0:T(8,128)} %get-tuple-element.44.col_ref) | copy-start | bytes 98308
  45.6 1.2 copy-start.1
  51.1 1.1 copy-start.16
  65.7 18.0 %all-to-all-start.2 = ((f32[32,16,128]{2,1,0:T(8,128)}), f32[32,16,128]{2,1,0:T(8,128)S(1)}, u32[]{:S(2)}, u32[]{:S(2)}) async-start(f32[32,16,128]{2,1,0:T(8,128)} %get-tuple-element.45.stat_ref), calls=%async_computation.2 | async-start | bytes 524288 | tf_op jit(solution)/shard_map/all_to_all | solution.py:368
  71.5 12.3 %copy-start.12 = (f32[256,128]{1,0:T(8,128)S(1)}, f32[256,128]{1,0:T(8,128)}, u32[]{:S(2)}) copy-start(f32[256,128]{1,0:T(8,128)} %get-tuple-element.50.mask_ref) | copy-start | bytes 393220
  84.9 9.4 %copy-start = (bf16[1024,768]{1,0:T(8,128)(2,1)S(1)}, bf16[1024,768]{1,0:T(8,128)(2,1)}, u32[]{:S(2)}) copy-start(bf16[1024,768]{1,0:T(8,128)(2,1)} %shard_map.81.u_ref) | copy-start | bytes 4718596
  84.9 9.4 %copy-start.2 = (bf16[1024,768]{1,0:T(8,128)(2,1)S(1)}, bf16[1024,768]{1,0:T(8,128)(2,1)}, u32[]{:S(2)}) copy-start(bf16[1024,768]{1,0:T(8,128)(2,1)} %copy-done.1) | copy-start | bytes 4718596
  84.9 9.4 %copy-start.13 = (f32[8,128]{1,0:T(8,128)S(1)}, f32[8,128]{1,0:T(8,128)}, u32[]{:S(2)}) copy-start(f32[8,128]{1,0:T(8,128)} %get-tuple-element.61.col_ref) | copy-start | bytes 12292
  91.1 32.1 %collective-permute-start.2 = (bf16[512,768]{1,0:T(8,128)(2,1)}, bf16[512,768]{1,0:T(8,128)(2,1)}, u32[]{:S(2)}, u32[]{:S(2)}) collective-permute-start(bf16[512,768]{1,0:T(8,128)(2,1)} %get-tuple-element.77), channel_id=1, source_target_pairs={{0,32},{32,64},{64,96},{96,0},{1,33},{33,65},{65,97},{97,1},{2,34}... | collective-permute-start | bytes 2359304 | tf_op jit(solution)/shard_map/ppermute | solution.py:507
  92.7 30.6 %collective-permute-start.3 = (bf16[512,768]{1,0:T(8,128)(2,1)}, bf16[512,768]{1,0:T(8,128)(2,1)}, u32[]{:S(2)}, u32[]{:S(2)}) collective-permute-start(bf16[512,768]{1,0:T(8,128)(2,1)} %get-tuple-element.78), channel_id=1, source_target_pairs={{0,96},{32,0},{64,32},{96,64},{1,97},{33,1},{65,33},{97,65},{2,98}... | collective-permute-start | bytes 2359304 | tf_op jit(solution)/shard_map/ppermute | solution.py:508
  97.3 34.9 %all-to-all-start.3 = ((bf16[32,64,384]{2,1,0:T(8,128)(2,1)}), bf16[32,64,384]{2,1,0:T(8,128)(2,1)}, u32[]{:S(2)}, u32[]{:S(2)}) async-start(bf16[32,64,384]{2,1,0:T(8,128)(2,1)} %bitcast.27), calls=%async_computation.3 | async-start | bytes 3145728 | tf_op jit(solution)/shard_map/all_to_all | solution.py:368
  121.2 21.8 %collective-permute-start = (bf16[512,768]{1,0:T(8,128)(2,1)}, bf16[512,768]{1,0:T(8,128)(2,1)S(1)}, u32[]{:S(2)}, u32[]{:S(2)}) collective-permute-start(bf16[512,768]{1,0:T(8,128)(2,1)} %get-tuple-element.69), channel_id=1, source_target_pairs={{0,96},{32,0},{64,32},{96,64},{1,97},{33,1},{65,33},{97,65},{2,98}... | collective-permute-start | bytes 2359304 | tf_op jit(solution)/shard_map/ppermute | solution.py:524
  123.0 22.0 %collective-permute-start.1 = (bf16[512,768]{1,0:T(8,128)(2,1)}, bf16[512,768]{1,0:T(8,128)(2,1)}, u32[]{:S(2)}, u32[]{:S(2)}) collective-permute-start(bf16[512,768]{1,0:T(8,128)(2,1)} %get-tuple-element.70), channel_id=1, source_target_pairs={{0,32},{32,64},{64,96},{96,0},{1,33},{33,65},{65,97},{97,1},{2,34}... | collective-permute-start | bytes 2359304 | tf_op jit(solution)/shard_map/ppermute | solution.py:523
  123.3 1.4 copy-start.14
  124.7 1.4 copy-start.15
  126.1 6.1 %copy-start.4 = (bf16[512,2048]{1,0:T(8,128)(2,1)S(1)}, bf16[512,2048]{1,0:T(8,128)(2,1)}, u32[]{:S(2)}) copy-start(bf16[512,2048]{1,0:T(8,128)(2,1)} %get-tuple-element.71.sel_ref) | copy-start | bytes 6291460
  129.0 31.8 %collective-permute-start.4 = (bf16[512,768]{1,0:T(8,128)(2,1)}, bf16[512,768]{1,0:T(8,128)(2,1)}, u32[]{:S(2)}, u32[]{:S(2)}) collective-permute-start(bf16[512,768]{1,0:T(8,128)(2,1)} %get-tuple-element.79), channel_id=1, source_target_pairs={{0,32},{32,64},{64,96},{96,0},{1,33},{33,65},{65,97},{97,1},{2,34}... | collective-permute-start | bytes 2359304 | tf_op jit(solution)/shard_map/ppermute | solution.py:537
  129.3 31.4 %collective-permute-start.5 = (bf16[512,768]{1,0:T(8,128)(2,1)}, bf16[512,768]{1,0:T(8,128)(2,1)}, u32[]{:S(2)}, u32[]{:S(2)}) collective-permute-start(bf16[512,768]{1,0:T(8,128)(2,1)} %get-tuple-element.80), channel_id=1, source_target_pairs={{0,96},{32,0},{64,32},{96,64},{1,97},{33,1},{65,33},{97,65},{2,98}... | collective-permute-start | bytes 2359304 | tf_op jit(solution)/shard_map/ppermute | solution.py:538
  135.6 16.5 %all-to-all-start.4 = ((bf16[32,8,768]{2,1,0:T(8,128)(2,1)}), bf16[32,8,768]{2,1,0:T(8,128)(2,1)S(1)}, u32[]{:S(2)}, u32[]{:S(2)}) async-start(bf16[32,8,768]{2,1,0:T(8,128)(2,1)} %shard_map.88), calls=%async_computation.4 | async-start | bytes 786432 | tf_op jit(solution)/shard_map/all_to_all | solution.py:368
  143.0 0.9 copy-start.10
  145.0 1.4 copy-start.5
  146.4 1.4 copy-start.6
  147.8 1.1 copy-start.11
where the time goes:
time: 165 us; the launch traced here: 164 us
  Pallas kernels  83 us (50%)
  starting transfers between devices  42.6 us (26%)
  waiting for transfers between devices  24.4 us (15%)
  local copies, waits for them, and re-layouts  11.7 us (7%)
    pallas_call x6, Pallas kernels, stepped(): pl.pallas_call(kernel, grid_spec=spec, out_shape=outs, compiler_params=pl...  58.6 us
    all_to_all x5, starting transfers between devices, swap(): return lax.all_to_all(x, 'label', split_axis=0, concat_axis=0, tiled=True)  34.1 us
    pallas_call x10, Pallas kernels, whole(): pl.pallas_call(kernel, out_shape=outs, in_specs=[place(i, hbm, smem) for...  24.3 us
    all_to_all x5, waiting for transfers between devices, swap(): return lax.all_to_all(x, 'label', split_axis=0, concat_axis=0, tiled=True)  15.6 us
    unnamed x36, local copies, waits for them, and re-layouts  10.7 us
    ppermute x1, waiting for transfers between devices, per_device(): from_prev_a = lax.ppermute(relay_up, 'dp', up)  7.69 us
  transfers between devices with their start and end apart: 11, of which 5 were waited for; matrix products, arithmetic and copies ran while one was open for 1% of the time, Pallas kernels for 33%

commit v1 on v0

--- a/solution.py
+++ b/solution.py
@@ -136,7 +136,7 @@
         out = jnp.where(row == s, lanes[:, s * ROWS : (s + 1) * ROWS], out)
     return out
 
-def scores_kernel(got_ref, col_ref, w_ref, p_ref, q_ref, top_ref, stat_ref, row_ref, s_ref, high, total, found):
+def scores_kernel(got_ref, col_ref, w_ref, r_ref, p_ref, q_ref, top_ref, stat_ref, row_ref, s_ref, high, total, found):
     step = pl.program_id(0)
     rows = s_ref.shape[1]
 
@@ -149,10 +149,9 @@
                     q_ref[here, h * HALF : (h + 1) * HALF] = got_ref[g, h, s]
         high[...] = jnp.full_like(high, NEG)
         total[...] = jnp.zeros_like(total)
-        found[...] = jnp.zeros_like(found)
 
     n = BIG_TILE // PART_TILE
-    top, tot, pick = high[...], total[...], found[...]
+    top, tot = high[...], total[...]
     for k in range(n + 1):
         if k < n:
             here = slice(k * PART_TILE, (k + 1) * PART_TILE)
@@ -160,26 +159,35 @@
         if k > 0:
             here = slice((k - 1) * PART_TILE, k * PART_TILE)
             s = s_ref[here, :]
-            target = iota(s.shape, 0) + (step * BIG_TILE + (k - 1) * PART_TILE) == col_ref[0:1, :]
-            pick += jnp.sum(jnp.where(target, s, 0.0).reshape(PART_TILE // 8, 8, rows), axis=0)
             best = jnp.max(jnp.max(s.reshape(PART_TILE // 8, 8, rows), axis=0), axis=0, keepdims=True)
             best = jnp.broadcast_to(best, (8, rows))
             e = jnp.exp(s - best[0:1, :])
+            target = iota(s.shape, 0) == col_ref[0:1, :] - (step * BIG_TILE + (k - 1) * PART_TILE)
             p_ref[here, :] = jnp.where(target, 0.0, e).astype(BF16)
             new = jnp.maximum(top, best)
             add = jnp.sum(e.reshape(PART_TILE // 8, 8, rows), axis=0)
             tot = tot * jnp.exp(top - new) + add * jnp.exp(best - new)
             top = new
             top_ref[k - 1] = best
-    high[...], total[...], found[...] = top, tot, pick
+    high[...], total[...] = top, tot
+
+    two = 2 * ROWS
+    mine = q_ref[pl.ds(pl.multiple_of(step * two, two), two), :].astype(F32) * r_ref[...].astype(F32)
+    folded = mine[:, :ROWS]
+    for c in range(1, FEAT // ROWS):
+        folded += mine[:, c * ROWS : (c + 1) * ROWS]
+    for i in range(2):
+        one = jnp.sum(folded[i * ROWS : (i + 1) * ROWS].T, axis=0, keepdims=True)
+        found[step, i : i + 1, :] = one
 
     @pl.when(step == pl.num_programs(0) - 1)
     def _():
         lse = top[0:1, :] + jnp.log(jnp.sum(tot, axis=0, keepdims=True))
         row_ref[...] = jnp.broadcast_to(lse, (8, rows))
-        chosen = jnp.sum(pick, axis=0, keepdims=True)
         stat_ref[:, :SLOTS, :] = jnp.broadcast_to(by_slot(lse)[None], (NDEV, SLOTS, ROWS))
-        stat_ref[:, SLOTS:, :] = jnp.broadcast_to(by_slot(chosen)[None], (NDEV, SLOTS, ROWS))
+        for i in range(SLOTS // 2):
+            here = slice(SLOTS + 2 * i, SLOTS + 2 * i + 2)
+            stat_ref[:, here, :] = jnp.broadcast_to(found[i][None], (NDEV, 2, ROWS))
 
 
 def normal_kernel(stat_ref, mask_ref, norm_ref, rest_ref, slots_ref, loss_ref):
@@ -228,19 +236,13 @@
         rows_from(acc, out_ref)
 
 
-def others_kernel(top_ref, row_ref, w_ref, p_ref, out_ref, acc):
+def others_kernel(top_ref, row_ref, w_ref, p_ref, out_ref, acc, scaled):
     step = pl.program_id(0)
-    term = None
-    for k in range(0, BIG_TILE // PART_TILE, 2):
-        pair = []
-        for i in (k, k + 1):
-            scale = jnp.exp(top_ref[i][0:1, :] - row_ref[0:1, :])
-            here = slice(i * PART_TILE, (i + 1) * PART_TILE)
-            pair.append((p_ref[here, :].astype(F32) * scale).astype(BF16))
-        here = slice(k * PART_TILE, (k + 2) * PART_TILE)
-        one = dot(w_ref[here, :], jnp.concatenate(pair, axis=0), ((0,), (0,)))
-        term = one if term is None else term + one
-    add_to(acc, term, step == 0)
+    for i in range(BIG_TILE // PART_TILE):
+        scale = jnp.exp(top_ref[i][0:1, :] - row_ref[0:1, :])
+        here = slice(i * PART_TILE, (i + 1) * PART_TILE)
+        scaled[here, :] = (p_ref[here, :].astype(F32) * scale).astype(BF16)
+    add_to(acc, dot(w_ref[...], scaled[...], ((0,), (0,))), step == 0)
 
     @pl.when(step == pl.num_programs(0) - 1)
     def _():
@@ -259,21 +261,18 @@
             out_ref[:, h, s * 8 : (s + 1) * 8, :] = part[:, :, h * HALF : (h + 1) * HALF]
 
 
-def table_grad_kernel(base, tiles_ref, q_ref, top_ref, norm_ref, rest_ref, col_ref, p_ref, *out_refs):
-    step = pl.program_id(0)
-    first = tiles_ref[base + step] * TILE
-    for k in range(TILE // PART_TILE):
-        here = slice(k * PART_TILE, (k + 1) * PART_TILE)
-        scale = jnp.exp(top_ref[tiles_ref[base + step] * (TILE // PART_TILE) + k][0:1, :] - norm_ref[0:1, :])
-        p = p_ref[here, :].astype(F32)
-        target = iota(p.shape, 0) + (first + k * PART_TILE) == col_ref[0:1, :]
-        slope = jnp.where(target, rest_ref[0:1, :], p * scale).astype(BF16)
-        value = dot(slope, q_ref[...], ((1,), (0,)))
-        for i, ref in enumerate(out_refs):
-
-            @pl.when(step == i)
-            def _(ref=ref):
-                ref[here, :] = value.astype(ref.dtype)
+def table_grad_kernel(base, tiles_ref, q_ref, top_ref, norm_ref, rest_ref, col_ref, *refs):
+    n = len(refs) // 2
+    for i in range(n):
+        p_ref, out_ref = refs[i], refs[n + i]
+        tile = tiles_ref[base + i]
+        for k in range(TILE // PART_TILE):
+            here = slice(k * PART_TILE, (k + 1) * PART_TILE)
+            scale = jnp.exp(top_ref[tile * (TILE // PART_TILE) + k][0:1, :] - norm_ref[0:1, :])
+            p = p_ref[here, :].astype(F32)
+            target = iota(p.shape, 0) == col_ref[0:1, :] - (tile * TILE + k * PART_TILE)
+            slope = jnp.where(target, rest_ref[0:1, :], p * scale).astype(BF16)
+            out_ref[here, :] = dot(slope, q_ref[...], ((1,), (0,))).astype(out_ref.dtype)
 
 
 def sum_kernel(sel_ref, parts_ref, out_ref):
@@ -422,11 +421,11 @@
     p, q, tops, stats, lse_row = stepped(
         scores_kernel,
         steps,
-        [fixed((16, 2, SLOTS, 8, HALF)), fixed((8, rows)), w_spec],
+        [fixed((16, 2, SLOTS, 8, HALF)), fixed((8, rows)), w_spec, tiled((2 * ROWS, FEAT))],
         (
             pltpu.HBM((LABELS, rows), BF16),
             shape((rows, FEAT), BF16),
-            shape((LABELS // PART_TILE, 8, rows), F32),
+            pltpu.HBM((LABELS // PART_TILE, 8, rows), F32),
             shape((NDEV, 2 * SLOTS, ROWS), F32),
             lanes,
         ),
@@ -441,21 +440,23 @@
             pltpu.VMEM((BIG_TILE, rows), F32),
             pltpu.VMEM((8, rows), F32),
             pltpu.VMEM((8, rows), F32),
-            pltpu.VMEM((8, rows), F32),
+            pltpu.VMEM((SLOTS // 2, 2, ROWS), F32),
         ),
         pltpu.with_memory_space_constraint(arrived.reshape(16, 2, SLOTS, 8, HALF), pltpu.HBM),
         col,
         ranker,
+        positive_rows,
     )
     all_stats = swap(stats)
     p = pltpu.with_memory_space_constraint(p, pltpu.HBM)
+    tops = pltpu.with_memory_space_constraint(tops, pltpu.HBM)
     others = stepped(
         others_kernel,
         steps,
         [tiled((parts_each, 8, rows)), fixed((8, rows)), w_spec, tiled((BIG_TILE, rows))],
         pltpu.HBM((rows, FEAT), BF16),
         fixed((rows, FEAT)),
-        (pltpu.VMEM((FEAT, rows), F32),),
+        (pltpu.VMEM((FEAT, rows), F32), pltpu.VMEM((BIG_TILE, rows), BF16)),
         tops,
         lse_row,
         ranker,
@@ -476,20 +477,20 @@
     tiles = jnp.stack([across, across + 1, ahead + 1, behind, ahead, behind + 1, y * 2, y * 2 + 1])
     tiles = tiles.astype(jnp.int32)
 
-    def table_grads(first, norm, dtypes):
+    def table_grads(first, norm, dtypes, place=pltpu.HBM):
         n = len(dtypes)
         return stepped(
             functools.partial(table_grad_kernel, first),
-            n,
+            1,
             [
                 fixed((rows, FEAT)),
                 fixed((LABELS // PART_TILE, 8, rows)),
                 fixed((8, rows)),
                 fixed((8, rows)),
                 fixed((8, rows)),
-                pl.BlockSpec((TILE, rows), lambda i, t: (t[first + i], 0)),
+                *(pl.BlockSpec((TILE, rows), lambda _, t, i=i: (t[first + i], 0)) for i in range(n)),
             ],
-            tuple(pltpu.HBM((TILE, FEAT), d) for d in dtypes),
+            tuple(place((TILE, FEAT), d) for d in dtypes),
             tuple(fixed((TILE, FEAT)) for _ in dtypes),
             (),
             tiles,
@@ -498,7 +499,7 @@
             norm,
             rest,
             col,
-            p,
+            *([p] * n),
             scalars=1,
         )
 
@@ -522,7 +523,9 @@
     next_b, prev_a, norm = lax.optimization_barrier((next_b, prev_a, norm))
     from_prev_b = lax.ppermute(next_b, "dp", up)
     from_next_a = lax.ppermute(prev_a, "dp", down)
-    next_a, prev_b, own_a, own_b = table_grads(4, norm, (F32, F32, F32, F32))
+    next_a, prev_b = table_grads(4, norm, (F32, F32), shape)
+    next_a, prev_b, norm = lax.optimization_barrier((next_a, prev_b, norm))
+    own_a, own_b = table_grads(6, norm, (F32, F32))
 
     relay_up, relay_down = whole(
         relay_kernel,
@@ -548,6 +551,7 @@
         from_next_a,
         from_prev_b,
         limit=16,
+        cost=50_000_000_000,
     )
     base, grad_queries = lax.optimization_barrier((base, grad_queries))
     grad_table = whole(

time: 165 us -> 156 us (0.945)
  local copies, waits for them, and re-layouts: 11.7 us -> 7.02 us
  waiting for transfers between devices: 24.4 us -> 20.4 us
  Pallas kernels: 83 us -> 80.7 us
    ppermute x1, waiting for transfers between devices: 7.69 us -> 0.79 us  [per_device(): from_prev_a = lax.ppermute(relay_up, 'dp', up)]
    unnamed x36 -> x22, local copies, waits for them, and re-layouts: 10.7 us -> 6.09 us
    all_to_all x5, waiting for transfers between devices: 15.6 us -> 19.6 us  [swap(): return lax.all_to_all(x, 'label', split_axis=0, concat_axis=0, tiled=True)]
    pallas_call x6 -> x7, Pallas kernels: 58.6 us -> 57.6 us  [stepped(): pl.pallas_call(kernel, grid_spec=spec, out_shape=outs, compiler_params=pl...]
  transfers between devices with their start and end apart: 11 -> 11, of which waited for: 5 -> 4; matrix products, arithmetic and copies ran while one was open for 1% -> 1% of each run, Pallas kernels for 33% -> 33%
where the time goes in v1:
time: 156 us; the launch traced here: 154 us
  Pallas kernels  80.7 us (52%)
  starting transfers between devices  43.2 us (28%)
  waiting for transfers between devices  20.4 us (13%)
  local copies, waits for them, and re-layouts  7.02 us (4%)
  between operations  1.66 us (1%)
    pallas_call x7, Pallas kernels, stepped(): pl.pallas_call(kernel, grid_spec=spec, out_shape=outs, compiler_params=pl...  57.6 us
    all_to_all x5, starting transfers between devices, swap(): return lax.all_to_all(x, 'label', split_axis=0, concat_axis=0, tiled=True)  34.7 us
    pallas_call x10, Pallas kernels, whole(): pl.pallas_call(kernel, out_shape=outs, in_specs=[place(i, hbm, smem) for...  23.1 us
    all_to_all x5, waiting for transfers between devices, swap(): return lax.all_to_all(x, 'label', split_axis=0, concat_axis=0, tiled=True)  19.6 us
    unnamed x22, local copies, waits for them, and re-layouts  6.09 us
  transfers between devices with their start and end apart: 11, of which 4 were waited for; matrix products, arithmetic and copies ran while one was open for 1% of the time, Pallas kernels for 33%

profile of v1, /device:TPU:2, one launch (start us, length us, event | category | flops | bytes accessed | tf_op | source)
XLA Modules:
  0.0 153.8 jit_solution(12911443430704079380)
XLA Ops:
  0.6 1.9 %shard_map.76 = bf16[16,2,8,896]{3,2,1,0:T(8,128)(2,1)} custom-call(bf16[2,16,8,768]{3,2,1,0:T(8,128)(2,1)} %bitcast.32, s32[2,128]{1,0:T(2,128)} %bitcast.33, s32[2,4]{1,0:T(2,128)} %beam_hbm.1), custom_call_target="tpu_custom_call" | custom-call | flops 1024 | bytes 1024 | tf_op jit(solution)/shard_map/pallas_call | solution.py:320
  2.5 8.5 %all-to-all-start = ((bf16[32,8,896]{2,1,0:T(8,128)(2,1)}), bf16[32,8,896]{2,1,0:T(8,128)(2,1)S(1)}, u32[]{:S(2)}, u32[]{:S(2)}) async-start(bf16[32,8,896]{2,1,0:T(8,128)(2,1)} %bitcast.30), calls=%async_computation | async-start | bytes 917504 | tf_op jit(solution)/shard_map/all_to_all | solution.py:367
  11.0 0.1 select_reduce_fusion
  11.1 0.1 broadcast_in_dim.42
  11.2 0.1 broadcast_in_dim.43
  11.3 9.5 %all-to-all-done = bf16[32,8,896]{2,1,0:T(8,128)(2,1)S(1)} async-done(((bf16[32,8,896]{2,1,0:T(8,128)(2,1)}), bf16[32,8,896]{2,1,0:T(8,128)(2,1)S(1)}, u32[]{:S(2)}, u32[]{:S(2)}) %all-to-all-start) | async-done | bytes 458784 | tf_op jit(solution)/shard_map/all_to_all | solution.py:367
  20.8 0.1 broadcast_in_dim.44.held_ref
  20.9 2.9 %shard_map.77 = bf16[2048,384]{1,0:T(8,128)(2,1)} custom-call(bf16[256,896]{1,0:T(8,128)(2,1)S(1)} %bitcast.22, f32[256,128]{1,0:T(8,128)S(1)} %broadcast_in_dim.44.held_ref), custom_call_target="tpu_custom_call" | custom-call | flops 1024 | bytes 1024 | tf_op jit(solution)/shard_map/pallas_call | solution.py:320
  23.8 5.8 %all-to-all-start.1 = ((bf16[32,64,384]{2,1,0:T(8,128)(2,1)}), bf16[32,64,384]{2,1,0:T(8,128)(2,1)}, u32[]{:S(2)}, u32[]{:S(2)}) async-start(bf16[32,64,384]{2,1,0:T(8,128)(2,1)} %bitcast.4), calls=%async_computation.1 | async-start | bytes 3145728 | tf_op jit(solution)/shard_map/all_to_all | solution.py:367
  29.6 0.6 fusion
  30.9 0.6 iota.17.mine_ref
  31.5 3.7 %shard_map.78 = (bf16[512,2048]{1,0:T(8,128)(2,1)}, f32[256,128]{1,0:T(8,128)}, s32[8,1024]{1,0:T(8,128)}, f32[8,128]{1,0:T(8,128)}) custom-call(bf16[256,896]{1,0:T(8,128)(2,1)} %bitcast.23, f32[256,128]{1,0:T(8,128)} %copy-done.5, f32[16,128]{1,0:T(8,128)} %iota.17.mine_ref), custom_call_target="tpu_custom_call" | custom-call | flops 1024 | bytes 1024 | tf_op jit(solution)/shard_map/pallas_call | solution.py:320
  35.2 0.8 copy-done.3
  35.9 10.4 %shard_map.79.r_ref = bf16[1024,768]{1,0:T(8,128)(2,1)S(1)} custom-call(s32[8,1024]{1,0:T(8,128)S(1)} %copy-done.3, bf16[4096,768]{1,0:T(8,128)(2,1)} %bitcast.25), custom_call_target="tpu_custom_call" | custom-call | flops 1024 | bytes 1024 | tf_op jit(solution)/shard_map/pallas_call | solution.py:347
  46.3 5.5 %all-to-all-done.1 = bf16[32,64,384]{2,1,0:T(8,128)(2,1)} async-done(((bf16[32,64,384]{2,1,0:T(8,128)(2,1)}), bf16[32,64,384]{2,1,0:T(8,128)(2,1)}, u32[]{:S(2)}, u32[]{:S(2)}) %all-to-all-start.1) | async-done | bytes 1572896 | tf_op jit(solution)/shard_map/all_to_all | solution.py:367
  51.8 15.4 %shard_map.80 = (bf16[4096,1024]{1,0:T(8,128)(2,1)}, bf16[1024,768]{1,0:T(8,128)(2,1)S(1)}, f32[16,8,1024]{2,1,0:T(8,128)}, f32[32,16,128]{2,1,0:T(8,128)}, f32[8,1024]{1,0:T(8,128)S(1)}) custom-call(bf16[16,2,8,8,384]{4,3,2,1,0:T(8,128)(2,1)} %bitcast.6.got_ref, s32[8,1024]{1,0:T(8,128)S(1)} %copy-done.4, bf16[4096,768]{1,0:T(8,128)(2,1)} %bitcast.26, ...), custom_call_target="tpu_custom_call" | custom-call | flops 1024 | bytes 1024 | tf_op jit(solution)/shard_map/pallas_call | solution.py:347
  67.2 5.7 %all-to-all-start.2 = ((f32[32,16,128]{2,1,0:T(8,128)}), f32[32,16,128]{2,1,0:T(8,128)S(1)}, u32[]{:S(2)}, u32[]{:S(2)}) async-start(f32[32,16,128]{2,1,0:T(8,128)} %get-tuple-element.49.stat_ref), calls=%async_computation.2 | async-start | bytes 524288 | tf_op jit(solution)/shard_map/all_to_all | solution.py:367
  72.9 0.1 stack.35.tiles_ref
  73.0 12.3 %shard_map.81.u_ref = bf16[1024,768]{1,0:T(8,128)(2,1)} custom-call(f32[16,8,1024]{2,1,0:T(8,128)} %get-tuple-element.50.top_ref, f32[8,1024]{1,0:T(8,128)S(1)} %get-tuple-element.51.row_ref, bf16[4096,768]{1,0:T(8,128)(2,1)} %bitcast.27, bf16[4096,1024]{1,0:T(8,128)(2,1)} %get-tuple-element.52.p_ref.refs_0_.refs_1_), custom_call_target="tpu_custom_call" | custom-call | flops 1024 | bytes 1024 | tf_op jit(solution)/shard_map/pallas_call | solution.py:347
  85.3 0.0 all-to-all-done.2.stat_ref
  85.3 0.9 copy-done.6
  86.2 1.2 shard_map.82
  87.4 5.0 %shard_map.83 = (bf16[512,768]{1,0:T(8,128)(2,1)}, bf16[512,768]{1,0:T(8,128)(2,1)}) custom-call(s32[8]{0:T(128)S(1)} %stack.35.tiles_ref, bf16[1024,768]{1,0:T(8,128)(2,1)S(1)} %get-tuple-element.56.q_ref, f32[16,8,1024]{2,1,0:T(8,128)} %get-tuple-element.50.top_ref, f32[8,1024]{1,0:T(8,128)S(1)} %get-tuple-element.72.norm_ref, ...), custom_call_target="tpu_custom_call" | custom-call | flops 1024 | bytes 1024 | tf_op jit(solution)/shard_map/pallas_call | solution.py:347
  92.4 1.6 %collective-permute-start.2 = (bf16[512,768]{1,0:T(8,128)(2,1)}, bf16[512,768]{1,0:T(8,128)(2,1)}, u32[]{:S(2)}, u32[]{:S(2)}) collective-permute-start(bf16[512,768]{1,0:T(8,128)(2,1)} %get-tuple-element.83), channel_id=1, source_target_pairs={{0,32},{32,64},{64,96},{96,0},{1,33},{33,65},{65,97},{97,1},{2,34}... | collective-permute-start | bytes 2359304 | tf_op jit(solution)/shard_map/ppermute | solution.py:508
  93.9 1.7 %collective-permute-start.3 = (bf16[512,768]{1,0:T(8,128)(2,1)}, bf16[512,768]{1,0:T(8,128)(2,1)}, u32[]{:S(2)}, u32[]{:S(2)}) collective-permute-start(bf16[512,768]{1,0:T(8,128)(2,1)} %get-tuple-element.84), channel_id=1, source_target_pairs={{0,96},{32,0},{64,32},{96,64},{1,97},{33,1},{65,33},{97,65},{2,98}... | collective-permute-start | bytes 2359304 | tf_op jit(solution)/shard_map/ppermute | solution.py:509
  95.6 2.9 %shard_map.84 = bf16[16,2,64,384]{3,2,1,0:T(8,128)(2,1)} custom-call(bf16[1024,768]{1,0:T(8,128)(2,1)S(1)} %copy-done, bf16[1024,768]{1,0:T(8,128)(2,1)S(1)} %shard_map.79.r_ref, f32[32,16,128]{2,1,0:T(8,128)} %get-tuple-element.49.stat_ref, f32[8,128]{1,0:T(8,128)S(1)} %get-tuple-element.63.norm_ref, f32[8,128]{1,0:T(8,128)S(1)} %copy-done.7), custom_call_target="tpu_custom_call" | custom-call | flops 1024 | bytes 1024 | tf_op jit(solution)/shard_map/pallas_call | solution.py:320
  98.5 7.5 %all-to-all-start.3 = ((bf16[32,64,384]{2,1,0:T(8,128)(2,1)}), bf16[32,64,384]{2,1,0:T(8,128)(2,1)S(1)}, u32[]{:S(2)}, u32[]{:S(2)}) async-start(bf16[32,64,384]{2,1,0:T(8,128)(2,1)} %bitcast.28), calls=%async_computation.3 | async-start | bytes 3145728 | tf_op jit(solution)/shard_map/all_to_all | solution.py:367
  106.0 5.0 %shard_map.85 = (bf16[512,768]{1,0:T(8,128)(2,1)}, bf16[512,768]{1,0:T(8,128)(2,1)}) custom-call(s32[8]{0:T(128)S(1)} %stack.35.tiles_ref, bf16[1024,768]{1,0:T(8,128)(2,1)S(1)} %get-tuple-element.56.q_ref, f32[16,8,1024]{2,1,0:T(8,128)} %get-tuple-element.50.top_ref, f32[8,1024]{1,0:T(8,128)S(1)} %get-tuple-element.72.norm_ref, ...), custom_call_target="tpu_custom_call" | custom-call | flops 1024 | bytes 1024 | tf_op jit(solution)/shard_map/pallas_call | solution.py:347
  111.0 1.8 %collective-permute-start = (bf16[512,768]{1,0:T(8,128)(2,1)}, bf16[512,768]{1,0:T(8,128)(2,1)}, u32[]{:S(2)}, u32[]{:S(2)}) collective-permute-start(bf16[512,768]{1,0:T(8,128)(2,1)} %get-tuple-element.75), channel_id=1, source_target_pairs={{0,96},{32,0},{64,32},{96,64},{1,97},{33,1},{65,33},{97,65},{2,98}... | collective-permute-start | bytes 2359304 | tf_op jit(solution)/shard_map/ppermute | solution.py:525
  112.8 0.3 collective-permute-start.1
  113.0 4.0 %shard_map.86 = (f32[512,768]{1,0:T(8,128)S(1)}, f32[512,768]{1,0:T(8,128)S(1)}) custom-call(s32[8]{0:T(128)S(1)} %stack.35.tiles_ref, bf16[1024,768]{1,0:T(8,128)(2,1)S(1)} %get-tuple-element.56.q_ref, f32[16,8,1024]{2,1,0:T(8,128)} %get-tuple-element.50.top_ref, f32[8,1024]{1,0:T(8,128)S(1)} %get-tuple-element.72.norm_ref, ...), custom_call_target="tpu_custom_call" | custom-call | flops 1024 | bytes 1024 | tf_op jit(solution)/shard_map/pallas_call | solution.py:347
  117.1 5.6 %shard_map.87 = (f32[512,768]{1,0:T(8,128)}, f32[512,768]{1,0:T(8,128)}) custom-call(s32[8]{0:T(128)S(1)} %stack.35.tiles_ref, bf16[1024,768]{1,0:T(8,128)(2,1)S(1)} %get-tuple-element.56.q_ref, f32[16,8,1024]{2,1,0:T(8,128)} %get-tuple-element.50.top_ref, f32[8,1024]{1,0:T(8,128)S(1)} %get-tuple-element.72.norm_ref, ...), custom_call_target="tpu_custom_call" | custom-call | flops 1024 | bytes 1024 | tf_op jit(solution)/shard_map/pallas_call | solution.py:347
  122.6 0.0 collective-permute-done.2.got_up_ref
  122.6 0.0 collective-permute-done.3.got_down_ref
  122.7 2.8 %shard_map.91 = (bf16[512,768]{1,0:T(8,128)(2,1)}, bf16[512,768]{1,0:T(8,128)(2,1)}) custom-call(f32[512,768]{1,0:T(8,128)S(1)} %get-tuple-element.81.up_ref, f32[512,768]{1,0:T(8,128)S(1)} %get-tuple-element.82.down_ref, bf16[512,768]{1,0:T(8,128)(2,1)} %collective-permute-done.2.got_up_ref, bf16[512,768]{1,0:T(8,128)(2,1)} %collective-permute-done.3.got_down_ref), custom_call_target="tpu_custom_call" | custom-call | flops 49999998976 | bytes 1024 | tf_op jit(solution)/shard_map/pallas_call | solution.py:320
  125.4 0.4 collective-permute-start.4
  125.8 2.9 %collective-permute-start.5 = (bf16[512,768]{1,0:T(8,128)(2,1)}, bf16[512,768]{1,0:T(8,128)(2,1)}, u32[]{:S(2)}, u32[]{:S(2)}) collective-permute-start(bf16[512,768]{1,0:T(8,128)(2,1)} %get-tuple-element.86), channel_id=1, source_target_pairs={{0,96},{32,0},{64,32},{96,64},{1,97},{33,1},{65,33},{97,65},{2,98}... | collective-permute-start | bytes 2359304 | tf_op jit(solution)/shard_map/ppermute | solution.py:541
  128.7 1.6 %copy-done.2 = bf16[512,2048]{1,0:T(8,128)(2,1)S(1)} copy-done((bf16[512,2048]{1,0:T(8,128)(2,1)S(1)}, bf16[512,2048]{1,0:T(8,128)(2,1)}, u32[]{:S(2)}) %copy-start.2) | copy-done | bytes 2097176
  130.2 2.0 %shard_map.89 = bf16[32,8,768]{2,1,0:T(8,128)(2,1)} custom-call(bf16[512,2048]{1,0:T(8,128)(2,1)S(1)} %copy-done.2, bf16[2048,384]{1,0:T(8,128)(2,1)S(1)} %bitcast.21), custom_call_target="tpu_custom_call" | custom-call | flops 1024 | bytes 1024 | tf_op jit(solution)/shard_map/pallas_call | solution.py:320
  132.2 7.4 %all-to-all-start.4 = ((bf16[32,8,768]{2,1,0:T(8,128)(2,1)}), bf16[32,8,768]{2,1,0:T(8,128)(2,1)S(1)}, u32[]{:S(2)}, u32[]{:S(2)}) async-start(bf16[32,8,768]{2,1,0:T(8,128)(2,1)} %shard_map.89), calls=%async_computation.4 | async-start | bytes 786432 | tf_op jit(solution)/shard_map/all_to_all | solution.py:367
  139.6 0.0 collective-permute-done.a_ref
  139.7 1.4 copy-done.8
  141.1 1.4 copy-done.9
  142.5 1.6 %shard_map.88.base_ref = f32[1024,768]{1,0:T(8,128)S(1)} custom-call(f32[512,768]{1,0:T(8,128)S(1)} %copy-done.8, f32[512,768]{1,0:T(8,128)S(1)} %copy-done.9, bf16[512,768]{1,0:T(8,128)(2,1)} %collective-permute-done.a_ref, bf16[512,768]{1,0:T(8,128)(2,1)} %collective-permute-done.1.b_ref), custom_call_target="tpu_custom_call" | custom-call | flops 49999998976 | bytes 1024 | tf_op jit(solution)/shard_map/pallas_call | solution.py:320
  144.1 4.6 %all-to-all-done.4 = bf16[32,8,768]{2,1,0:T(8,128)(2,1)S(1)} async-done(((bf16[32,8,768]{2,1,0:T(8,128)(2,1)}), bf16[32,8,768]{2,1,0:T(8,128)(2,1)S(1)}, u32[]{:S(2)}, u32[]{:S(2)}) %all-to-all-start.4) | async-done | bytes 393248 | tf_op jit(solution)/shard_map/all_to_all | solution.py:367
  148.7 0.9 shard_map.90
  149.7 0.8 collective-permute-done.4.a_ref
  150.5 3.2 %shard_map.92 = f32[1024,768]{1,0:T(8,128)} custom-call(f32[1024,768]{1,0:T(8,128)S(1)} %shard_map.88.base_ref, bf16[512,768]{1,0:T(8,128)(2,1)} %collective-permute-done.4.a_ref, bf16[512,768]{1,0:T(8,128)(2,1)} %collective-permute-done.5.b_ref), custom_call_target="tpu_custom_call" | custom-call | flops 1024 | bytes 1024 | tf_op jit(solution)/shard_map/pallas_call | solution.py:320
  (22 shorter events, 0.0 us)
Async XLA Ops:
  0.6 10.4 %copy-start.10 = (s32[32]{0:T(128)S(1)}, s32[32]{0:T(128)}, u32[]{:S(2)}) copy-start(s32[32]{0:T(128)} %param.9) | copy-start | bytes 388
  2.5 18.3 %all-to-all-start = ((bf16[32,8,896]{2,1,0:T(8,128)(2,1)}), bf16[32,8,896]{2,1,0:T(8,128)(2,1)S(1)}, u32[]{:S(2)}, u32[]{:S(2)}) async-start(bf16[32,8,896]{2,1,0:T(8,128)(2,1)} %bitcast.30), calls=%async_computation | async-start | bytes 917504 | tf_op jit(solution)/shard_map/all_to_all | solution.py:367
  20.8 3.0 %copy-start.1 = (bf16[32,8,896]{2,1,0:T(8,128)(2,1)}, bf16[32,8,896]{2,1,0:T(8,128)(2,1)S(1)}, u32[]{:S(2)}) copy-start(bf16[32,8,896]{2,1,0:T(8,128)(2,1)S(1)} %all-to-all-done) | copy-start | bytes 1376260
  20.9 2.9 %copy-start.5 = (f32[256,128]{1,0:T(8,128)}, f32[256,128]{1,0:T(8,128)S(1)}, u32[]{:S(2)}) copy-start(f32[256,128]{1,0:T(8,128)S(1)} %broadcast_in_dim.44.held_ref) | copy-start | bytes 393220
  23.8 28.0 %all-to-all-start.1 = ((bf16[32,64,384]{2,1,0:T(8,128)(2,1)}), bf16[32,64,384]{2,1,0:T(8,128)(2,1)}, u32[]{:S(2)}, u32[]{:S(2)}) async-start(bf16[32,64,384]{2,1,0:T(8,128)(2,1)} %bitcast.4), calls=%async_computation.1 | async-start | bytes 3145728 | tf_op jit(solution)/shard_map/all_to_all | solution.py:367
  35.2 0.8 copy-start.3
  35.9 15.9 %copy-start.4 = (s32[8,1024]{1,0:T(8,128)S(1)}, s32[8,1024]{1,0:T(8,128)}, u32[]{:S(2)}) copy-start(s32[8,1024]{1,0:T(8,128)} %get-tuple-element.47.col_ref) | copy-start | bytes 98308
  67.2 18.1 %all-to-all-start.2 = ((f32[32,16,128]{2,1,0:T(8,128)}), f32[32,16,128]{2,1,0:T(8,128)S(1)}, u32[]{:S(2)}, u32[]{:S(2)}) async-start(f32[32,16,128]{2,1,0:T(8,128)} %get-tuple-element.49.stat_ref), calls=%async_computation.2 | async-start | bytes 524288 | tf_op jit(solution)/shard_map/all_to_all | solution.py:367
  85.3 0.9 copy-start.6
  87.4 8.2 %copy-start = (bf16[1024,768]{1,0:T(8,128)(2,1)S(1)}, bf16[1024,768]{1,0:T(8,128)(2,1)}, u32[]{:S(2)}) copy-start(bf16[1024,768]{1,0:T(8,128)(2,1)} %shard_map.81.u_ref) | copy-start | bytes 4718596
  87.4 8.2 %copy-start.7 = (f32[8,128]{1,0:T(8,128)S(1)}, f32[8,128]{1,0:T(8,128)}, u32[]{:S(2)}) copy-start(f32[8,128]{1,0:T(8,128)} %get-tuple-element.64.col_ref) | copy-start | bytes 12292
  92.4 30.3 %collective-permute-start.2 = (bf16[512,768]{1,0:T(8,128)(2,1)}, bf16[512,768]{1,0:T(8,128)(2,1)}, u32[]{:S(2)}, u32[]{:S(2)}) collective-permute-start(bf16[512,768]{1,0:T(8,128)(2,1)} %get-tuple-element.83), channel_id=1, source_target_pairs={{0,32},{32,64},{64,96},{96,0},{1,33},{33,65},{65,97},{97,1},{2,34}... | collective-permute-start | bytes 2359304 | tf_op jit(solution)/shard_map/ppermute | solution.py:508
  93.9 28.7 %collective-permute-start.3 = (bf16[512,768]{1,0:T(8,128)(2,1)}, bf16[512,768]{1,0:T(8,128)(2,1)}, u32[]{:S(2)}, u32[]{:S(2)}) collective-permute-start(bf16[512,768]{1,0:T(8,128)(2,1)} %get-tuple-element.84), channel_id=1, source_target_pairs={{0,96},{32,0},{64,32},{96,64},{1,97},{33,1},{65,33},{97,65},{2,98}... | collective-permute-start | bytes 2359304 | tf_op jit(solution)/shard_map/ppermute | solution.py:509
  98.5 30.1 %all-to-all-start.3 = ((bf16[32,64,384]{2,1,0:T(8,128)(2,1)}), bf16[32,64,384]{2,1,0:T(8,128)(2,1)S(1)}, u32[]{:S(2)}, u32[]{:S(2)}) async-start(bf16[32,64,384]{2,1,0:T(8,128)(2,1)} %bitcast.28), calls=%async_computation.3 | async-start | bytes 3145728 | tf_op jit(solution)/shard_map/all_to_all | solution.py:367
  111.0 28.7 %collective-permute-start = (bf16[512,768]{1,0:T(8,128)(2,1)}, bf16[512,768]{1,0:T(8,128)(2,1)}, u32[]{:S(2)}, u32[]{:S(2)}) collective-permute-start(bf16[512,768]{1,0:T(8,128)(2,1)} %get-tuple-element.75), channel_id=1, source_target_pairs={{0,96},{32,0},{64,32},{96,64},{1,97},{33,1},{65,33},{97,65},{2,98}... | collective-permute-start | bytes 2359304 | tf_op jit(solution)/shard_map/ppermute | solution.py:525
  112.8 26.9 %collective-permute-start.1 = (bf16[512,768]{1,0:T(8,128)(2,1)}, bf16[512,768]{1,0:T(8,128)(2,1)}, u32[]{:S(2)}, u32[]{:S(2)}) collective-permute-start(bf16[512,768]{1,0:T(8,128)(2,1)} %get-tuple-element.76), channel_id=1, source_target_pairs={{0,32},{32,64},{64,96},{96,0},{1,33},{33,65},{65,97},{97,1},{2,34}... | collective-permute-start | bytes 2359304 | tf_op jit(solution)/shard_map/ppermute | solution.py:524
  125.4 25.0 %collective-permute-start.4 = (bf16[512,768]{1,0:T(8,128)(2,1)}, bf16[512,768]{1,0:T(8,128)(2,1)}, u32[]{:S(2)}, u32[]{:S(2)}) collective-permute-start(bf16[512,768]{1,0:T(8,128)(2,1)} %get-tuple-element.85), channel_id=1, source_target_pairs={{0,32},{32,64},{64,96},{96,0},{1,33},{33,65},{65,97},{97,1},{2,34}... | collective-permute-start | bytes 2359304 | tf_op jit(solution)/shard_map/ppermute | solution.py:540
  125.8 24.7 %collective-permute-start.5 = (bf16[512,768]{1,0:T(8,128)(2,1)}, bf16[512,768]{1,0:T(8,128)(2,1)}, u32[]{:S(2)}, u32[]{:S(2)}) collective-permute-start(bf16[512,768]{1,0:T(8,128)(2,1)} %get-tuple-element.86), channel_id=1, source_target_pairs={{0,96},{32,0},{64,32},{96,64},{1,97},{33,1},{65,33},{97,65},{2,98}... | collective-permute-start | bytes 2359304 | tf_op jit(solution)/shard_map/ppermute | solution.py:541
  128.6 1.6 %copy-start.2 = (bf16[512,2048]{1,0:T(8,128)(2,1)S(1)}, bf16[512,2048]{1,0:T(8,128)(2,1)}, u32[]{:S(2)}) copy-start(bf16[512,2048]{1,0:T(8,128)(2,1)} %get-tuple-element.77.sel_ref) | copy-start | bytes 6291460
  132.2 16.5 %all-to-all-start.4 = ((bf16[32,8,768]{2,1,0:T(8,128)(2,1)}), bf16[32,8,768]{2,1,0:T(8,128)(2,1)S(1)}, u32[]{:S(2)}, u32[]{:S(2)}) async-start(bf16[32,8,768]{2,1,0:T(8,128)(2,1)} %shard_map.89), calls=%async_computation.4 | async-start | bytes 786432 | tf_op jit(solution)/shard_map/all_to_all | solution.py:367
  139.7 1.4 copy-start.8
  141.1 1.4 copy-start.9

commit v2 on v1

--- a/solution.py
+++ b/solution.py
@@ -129,6 +129,10 @@
             for b in range(2):
                 out_ref[g, h, :, b * HALF : (b + 1) * HALF] = q_ref[b, g, :, h * HALF : (h + 1) * HALF]
 
+def label_iota(rows):
+    return iota((PART_TILE, rows), 0).reshape(PART_TILE // 8, 8, rows)
+
+
 def by_slot(lanes):
     row = iota((SLOTS, ROWS), 0)
     out = jnp.zeros((SLOTS, ROWS), F32)
@@ -158,15 +162,14 @@
             s_ref[here, :] = dot(w_ref[here, :], q_ref[...], ((1,), (1,)))
         if k > 0:
             here = slice((k - 1) * PART_TILE, k * PART_TILE)
-            s = s_ref[here, :]
-            best = jnp.max(jnp.max(s.reshape(PART_TILE // 8, 8, rows), axis=0), axis=0, keepdims=True)
+            s = s_ref[here, :].reshape(PART_TILE // 8, 8, rows)
+            best = jnp.max(jnp.max(s, axis=0), axis=0, keepdims=True)
             best = jnp.broadcast_to(best, (8, rows))
-            e = jnp.exp(s - best[0:1, :])
-            target = iota(s.shape, 0) == col_ref[0:1, :] - (step * BIG_TILE + (k - 1) * PART_TILE)
-            p_ref[here, :] = jnp.where(target, 0.0, e).astype(BF16)
+            e = jnp.exp(s - best[None])
+            target = label_iota(rows) == (col_ref[...] - (step * BIG_TILE + (k - 1) * PART_TILE))[None]
+            p_ref[here, :] = jnp.where(target, 0.0, e).reshape(PART_TILE, rows).astype(BF16)
             new = jnp.maximum(top, best)
-            add = jnp.sum(e.reshape(PART_TILE // 8, 8, rows), axis=0)
-            tot = tot * jnp.exp(top - new) + add * jnp.exp(best - new)
+            tot = tot * jnp.exp(top - new) + jnp.sum(e, axis=0) * jnp.exp(best - new)
             top = new
             top_ref[k - 1] = best
     high[...], total[...] = top, tot
@@ -239,9 +242,10 @@
 def others_kernel(top_ref, row_ref, w_ref, p_ref, out_ref, acc, scaled):
     step = pl.program_id(0)
     for i in range(BIG_TILE // PART_TILE):
-        scale = jnp.exp(top_ref[i][0:1, :] - row_ref[0:1, :])
+        scale = jnp.exp(top_ref[i] - row_ref[...])
         here = slice(i * PART_TILE, (i + 1) * PART_TILE)
-        scaled[here, :] = (p_ref[here, :].astype(F32) * scale).astype(BF16)
+        p = p_ref[here, :].astype(F32).reshape(PART_TILE // 8, 8, scale.shape[1])
+        scaled[here, :] = (p * scale[None]).reshape(PART_TILE, scale.shape[1]).astype(BF16)
     add_to(acc, dot(w_ref[...], scaled[...], ((0,), (0,))), step == 0)
 
     @pl.when(step == pl.num_programs(0) - 1)
@@ -268,10 +272,12 @@
         tile = tiles_ref[base + i]
         for k in range(TILE // PART_TILE):
             here = slice(k * PART_TILE, (k + 1) * PART_TILE)
-            scale = jnp.exp(top_ref[tile * (TILE // PART_TILE) + k][0:1, :] - norm_ref[0:1, :])
-            p = p_ref[here, :].astype(F32)
-            target = iota(p.shape, 0) == col_ref[0:1, :] - (tile * TILE + k * PART_TILE)
-            slope = jnp.where(target, rest_ref[0:1, :], p * scale).astype(BF16)
+            scale = jnp.exp(top_ref[tile * (TILE // PART_TILE) + k] - norm_ref[...])
+            rows = scale.shape[1]
+            p = p_ref[here, :].astype(F32).reshape(PART_TILE // 8, 8, rows)
+            target = label_iota(rows) == (col_ref[...] - (tile * TILE + k * PART_TILE))[None]
+            slope = jnp.where(target, rest_ref[...][None], p * scale[None])
+            slope = slope.reshape(PART_TILE, rows).astype(BF16)
             out_ref[here, :] = dot(slope, q_ref[...], ((1,), (0,))).astype(out_ref.dtype)
 
 
@@ -393,8 +399,8 @@
     sel, mask, col, col_slots = whole(
         table_kernel,
         (
-            shape((512, 2048), BF16),
-            shape((256, 128), F32),
+            pltpu.HBM((512, 2048), BF16),
+            pltpu.HBM((256, 128), F32),
             shape((8, rows), jnp.int32),
             shape((SLOTS, ROWS), F32),
         ),
@@ -467,7 +473,7 @@
         normal_kernel,
         (lanes, lanes, shape((SLOTS, ROWS), F32), shape((2, ROWS), F32)),
         all_stats,
-        mask,
+        pltpu.with_memory_space_constraint(mask, pltpu.HBM),
         limit=16,
     )
 
@@ -524,8 +530,6 @@
     from_prev_b = lax.ppermute(next_b, "dp", up)
     from_next_a = lax.ppermute(prev_a, "dp", down)
     next_a, prev_b = table_grads(4, norm, (F32, F32), shape)
-    next_a, prev_b, norm = lax.optimization_barrier((next_a, prev_b, norm))
-    own_a, own_b = table_grads(6, norm, (F32, F32))
 
     relay_up, relay_down = whole(
         relay_kernel,
@@ -537,12 +541,14 @@
         limit=16,
         cost=50_000_000_000,
     )
+    relay_up, relay_down, norm = lax.optimization_barrier((relay_up, relay_down, norm))
+    own_a, own_b = table_grads(6, norm, (F32, F32))
     from_prev_a = lax.ppermute(relay_up, "dp", up)
     from_next_b = lax.ppermute(relay_down, "dp", down)
 
+    sel = pltpu.with_memory_space_constraint(sel, pltpu.HBM)
     homeward = whole(sum_kernel, shape((NDEV, 8, FEAT), BF16), sel, parts, limit=16)
-    home = swap(homeward).reshape(16, 2, 8, FEAT)
-    grad_queries = whole(home_kernel, shape((2, 16, 8, FEAT), F32), home, limit=16).reshape(256, FEAT)
+    home = swap(homeward)
     base = whole(
         base_kernel,
         shape((2 * TILE, FEAT), F32),
@@ -551,9 +557,8 @@
         from_next_a,
         from_prev_b,
         limit=16,
-        cost=50_000_000_000,
-    )
-    base, grad_queries = lax.optimization_barrier((base, grad_queries))
+        cost=8_000_000_000,
+    )
     grad_table = whole(
         finish_kernel,
         shape((2 * TILE, FEAT), F32),
@@ -564,6 +569,10 @@
         limit=16,
         scratch=(pltpu.VMEM((2 * TILE, FEAT), F32), sems(2)),
     )
+    home, grad_table = lax.optimization_barrier((home, grad_table))
+    grad_queries = whole(
+        home_kernel, shape((2, 16, 8, FEAT), F32), home.reshape(16, 2, 8, FEAT), limit=16
+    ).reshape(256, FEAT)
     return loss.reshape(256), grad_queries, grad_table[None]
 
 def solution(mesh):

time: 156 us -> 156 us (level)
  local copies, waits for them, and re-layouts: 7.02 us -> 4.53 us
  Pallas kernels: 80.7 us -> 83.1 us
    ppermute x1, waiting for transfers between devices: 0.79 us -> 6.46 us  [per_device(): from_prev_a = lax.ppermute(relay_up, 'dp', up)]
    all_to_all x5, waiting for transfers between devices: 19.6 us -> 15 us  [swap(): return lax.all_to_all(x, 'label', split_axis=0, concat_axis=0, tiled=True)]
    unnamed x22 -> x18, local copies, waits for them, and re-layouts: 6.09 us -> 3.59 us
    pallas_call x10, Pallas kernels: 23.1 us -> 25.5 us  [whole(): pl.pallas_call(kernel, out_shape=outs, in_specs=[place(i, hbm, smem) for...]
  transfers between devices with their start and end apart: 11 -> 11, of which waited for: 4 -> 3; matrix products, arithmetic and copies ran while one was open for 1% -> 1% of each run, Pallas kernels for 33% -> 35%
where the time goes in v2:
time: 156 us; the launch traced here: 155 us
  Pallas kernels  83.1 us (53%)
  starting transfers between devices  43.2 us (28%)
  waiting for transfers between devices  21.5 us (14%)
  local copies, waits for them, and re-layouts  4.53 us (3%)
    pallas_call x7, Pallas kernels, stepped(): pl.pallas_call(kernel, grid_spec=spec, out_shape=outs, compiler_params=pl...  57.6 us
    all_to_all x5, starting transfers between devices, swap(): return lax.all_to_all(x, 'label', split_axis=0, concat_axis=0, tiled=True)  34.7 us
    pallas_call x10, Pallas kernels, whole(): pl.pallas_call(kernel, out_shape=outs, in_specs=[place(i, hbm, smem) for...  25.5 us
    all_to_all x5, waiting for transfers between devices, swap(): return lax.all_to_all(x, 'label', split_axis=0, concat_axis=0, tiled=True)  15 us
    ppermute x1, waiting for transfers between devices, per_device(): from_prev_a = lax.ppermute(relay_up, 'dp', up)  6.46 us
    unnamed x18, local copies, waits for them, and re-layouts  3.59 us
  transfers between devices with their start and end apart: 11, of which 3 were waited for; matrix products, arithmetic and copies ran while one was open for 1% of the time, Pallas kernels for 35%

profile of v2, /device:TPU:2, one launch (start us, length us, event | category | flops | bytes accessed | tf_op | source)
XLA Modules:
  0.0 154.7 jit_solution(4558757016886866236)
XLA Ops:
  0.6 1.9 %shard_map.76 = bf16[16,2,8,896]{3,2,1,0:T(8,128)(2,1)} custom-call(bf16[2,16,8,768]{3,2,1,0:T(8,128)(2,1)} %bitcast.32, s32[2,128]{1,0:T(2,128)} %bitcast.33, s32[2,4]{1,0:T(2,128)} %beam_hbm.1), custom_call_target="tpu_custom_call" | custom-call | flops 1024 | bytes 1024 | tf_op jit(solution)/shard_map/pallas_call | solution.py:326
  2.5 8.5 %all-to-all-start = ((bf16[32,8,896]{2,1,0:T(8,128)(2,1)}), bf16[32,8,896]{2,1,0:T(8,128)(2,1)S(1)}, u32[]{:S(2)}, u32[]{:S(2)}) async-start(bf16[32,8,896]{2,1,0:T(8,128)(2,1)} %bitcast.30), calls=%async_computation | async-start | bytes 917504 | tf_op jit(solution)/shard_map/all_to_all | solution.py:373
  11.0 0.1 select_reduce_fusion
  11.1 0.1 broadcast_in_dim.42
  11.2 0.1 broadcast_in_dim.43
  11.3 9.5 %all-to-all-done = bf16[32,8,896]{2,1,0:T(8,128)(2,1)S(1)} async-done(((bf16[32,8,896]{2,1,0:T(8,128)(2,1)}), bf16[32,8,896]{2,1,0:T(8,128)(2,1)S(1)}, u32[]{:S(2)}, u32[]{:S(2)}) %all-to-all-start) | async-done | bytes 458784 | tf_op jit(solution)/shard_map/all_to_all | solution.py:373
  20.8 0.1 broadcast_in_dim.44.held_ref
  20.9 2.9 %shard_map.77 = bf16[2048,384]{1,0:T(8,128)(2,1)} custom-call(bf16[256,896]{1,0:T(8,128)(2,1)S(1)} %bitcast.22, f32[256,128]{1,0:T(8,128)S(1)} %broadcast_in_dim.44.held_ref), custom_call_target="tpu_custom_call" | custom-call | flops 1024 | bytes 1024 | tf_op jit(solution)/shard_map/pallas_call | solution.py:326
  23.8 5.7 %all-to-all-start.1 = ((bf16[32,64,384]{2,1,0:T(8,128)(2,1)}), bf16[32,64,384]{2,1,0:T(8,128)(2,1)}, u32[]{:S(2)}, u32[]{:S(2)}) async-start(bf16[32,64,384]{2,1,0:T(8,128)(2,1)} %bitcast.4), calls=%async_computation.1 | async-start | bytes 3145728 | tf_op jit(solution)/shard_map/all_to_all | solution.py:373
  29.6 0.6 fusion
  30.9 0.6 iota.17.mine_ref
  31.5 3.7 %shard_map.78 = (bf16[512,2048]{1,0:T(8,128)(2,1)}, f32[256,128]{1,0:T(8,128)}, s32[8,1024]{1,0:T(8,128)}, f32[8,128]{1,0:T(8,128)}) custom-call(bf16[256,896]{1,0:T(8,128)(2,1)} %bitcast.23, f32[256,128]{1,0:T(8,128)} %copy-done.4, f32[16,128]{1,0:T(8,128)} %iota.17.mine_ref), custom_call_target="tpu_custom_call" | custom-call | flops 1024 | bytes 1024 | tf_op jit(solution)/shard_map/pallas_call | solution.py:326
  35.2 0.8 copy-done.2
  35.9 10.4 %shard_map.79.r_ref = bf16[1024,768]{1,0:T(8,128)(2,1)S(1)} custom-call(s32[8,1024]{1,0:T(8,128)S(1)} %copy-done.2, bf16[4096,768]{1,0:T(8,128)(2,1)} %bitcast.25), custom_call_target="tpu_custom_call" | custom-call | flops 1024 | bytes 1024 | tf_op jit(solution)/shard_map/pallas_call | solution.py:353
  46.3 5.5 %all-to-all-done.1 = bf16[32,64,384]{2,1,0:T(8,128)(2,1)} async-done(((bf16[32,64,384]{2,1,0:T(8,128)(2,1)}), bf16[32,64,384]{2,1,0:T(8,128)(2,1)}, u32[]{:S(2)}, u32[]{:S(2)}) %all-to-all-start.1) | async-done | bytes 1572896 | tf_op jit(solution)/shard_map/all_to_all | solution.py:373
  51.8 15.4 %shard_map.80 = (bf16[4096,1024]{1,0:T(8,128)(2,1)}, bf16[1024,768]{1,0:T(8,128)(2,1)S(1)}, f32[16,8,1024]{2,1,0:T(8,128)}, f32[32,16,128]{2,1,0:T(8,128)}, f32[8,1024]{1,0:T(8,128)S(1)}) custom-call(bf16[16,2,8,8,384]{4,3,2,1,0:T(8,128)(2,1)} %bitcast.6.got_ref, s32[8,1024]{1,0:T(8,128)S(1)} %copy-done.3, bf16[4096,768]{1,0:T(8,128)(2,1)} %bitcast.26, ...), custom_call_target="tpu_custom_call" | custom-call | flops 1024 | bytes 1024 | tf_op jit(solution)/shard_map/pallas_call | solution.py:353
  67.2 5.7 %all-to-all-start.2 = ((f32[32,16,128]{2,1,0:T(8,128)}), f32[32,16,128]{2,1,0:T(8,128)S(1)}, u32[]{:S(2)}, u32[]{:S(2)}) async-start(f32[32,16,128]{2,1,0:T(8,128)} %get-tuple-element.49.stat_ref), calls=%async_computation.2 | async-start | bytes 524288 | tf_op jit(solution)/shard_map/all_to_all | solution.py:373
  72.9 0.1 stack.35.tiles_ref
  73.0 12.2 %shard_map.81.u_ref = bf16[1024,768]{1,0:T(8,128)(2,1)} custom-call(f32[16,8,1024]{2,1,0:T(8,128)} %get-tuple-element.50.top_ref, f32[8,1024]{1,0:T(8,128)S(1)} %get-tuple-element.51.row_ref, bf16[4096,768]{1,0:T(8,128)(2,1)} %bitcast.27, bf16[4096,1024]{1,0:T(8,128)(2,1)} %get-tuple-element.52.p_ref.refs_0_.refs_1_), custom_call_target="tpu_custom_call" | custom-call | flops 1024 | bytes 1024 | tf_op jit(solution)/shard_map/pallas_call | solution.py:353
  85.2 0.0 all-to-all-done.2.stat_ref
  85.3 2.1 %shard_map.82 = (f32[8,1024]{1,0:T(8,128)S(1)}, f32[8,1024]{1,0:T(8,128)S(1)}, f32[8,128]{1,0:T(8,128)S(1)}, f32[2,128]{1,0:T(2,128)}) custom-call(f32[32,16,128]{2,1,0:T(8,128)S(1)} %all-to-all-done.2.stat_ref, f32[256,128]{1,0:T(8,128)} %get-tuple-element.54.mask_ref), custom_call_target="tpu_custom_call" | custom-call | flops 1024 | bytes 1024 | tf_op jit(solution)/shard_map/pallas_call | solution.py:326
  87.3 5.0 %shard_map.83 = (bf16[512,768]{1,0:T(8,128)(2,1)}, bf16[512,768]{1,0:T(8,128)(2,1)}) custom-call(s32[8]{0:T(128)S(1)} %stack.35.tiles_ref, bf16[1024,768]{1,0:T(8,128)(2,1)S(1)} %get-tuple-element.58.q_ref, f32[16,8,1024]{2,1,0:T(8,128)} %get-tuple-element.50.top_ref, f32[8,1024]{1,0:T(8,128)S(1)} %get-tuple-element.78.norm_ref, ...), custom_call_target="tpu_custom_call" | custom-call | flops 1024 | bytes 1024 | tf_op jit(solution)/shard_map/pallas_call | solution.py:353
  92.4 1.6 %collective-permute-start = (bf16[512,768]{1,0:T(8,128)(2,1)}, bf16[512,768]{1,0:T(8,128)(2,1)}, u32[]{:S(2)}, u32[]{:S(2)}) collective-permute-start(bf16[512,768]{1,0:T(8,128)(2,1)} %get-tuple-element.74), channel_id=1, source_target_pairs={{0,32},{32,64},{64,96},{96,0},{1,33},{33,65},{65,97},{97,1},{2,34}... | collective-permute-start | bytes 2359304 | tf_op jit(solution)/shard_map/ppermute | solution.py:514
  93.9 1.7 %collective-permute-start.1 = (bf16[512,768]{1,0:T(8,128)(2,1)}, bf16[512,768]{1,0:T(8,128)(2,1)}, u32[]{:S(2)}, u32[]{:S(2)}) collective-permute-start(bf16[512,768]{1,0:T(8,128)(2,1)} %get-tuple-element.75), channel_id=1, source_target_pairs={{0,96},{32,0},{64,32},{96,64},{1,97},{33,1},{65,33},{97,65},{2,98}... | collective-permute-start | bytes 2359304 | tf_op jit(solution)/shard_map/ppermute | solution.py:515
  95.6 3.0 %shard_map.84 = bf16[16,2,64,384]{3,2,1,0:T(8,128)(2,1)} custom-call(bf16[1024,768]{1,0:T(8,128)(2,1)S(1)} %copy-done, bf16[1024,768]{1,0:T(8,128)(2,1)S(1)} %shard_map.79.r_ref, f32[32,16,128]{2,1,0:T(8,128)} %get-tuple-element.49.stat_ref, f32[8,128]{1,0:T(8,128)S(1)} %get-tuple-element.64.norm_ref, f32[8,128]{1,0:T(8,128)S(1)} %copy-done.5), custom_call_target="tpu_custom_call" | custom-call | flops 1024 | bytes 1024 | tf_op jit(solution)/shard_map/pallas_call | solution.py:326
  98.6 7.5 %all-to-all-start.3 = ((bf16[32,64,384]{2,1,0:T(8,128)(2,1)}), bf16[32,64,384]{2,1,0:T(8,128)(2,1)S(1)}, u32[]{:S(2)}, u32[]{:S(2)}) async-start(bf16[32,64,384]{2,1,0:T(8,128)(2,1)} %bitcast.28), calls=%async_computation.3 | async-start | bytes 3145728 | tf_op jit(solution)/shard_map/all_to_all | solution.py:373
  106.1 5.0 %shard_map.86 = (bf16[512,768]{1,0:T(8,128)(2,1)}, bf16[512,768]{1,0:T(8,128)(2,1)}) custom-call(s32[8]{0:T(128)S(1)} %stack.35.tiles_ref, bf16[1024,768]{1,0:T(8,128)(2,1)S(1)} %get-tuple-element.58.q_ref, f32[16,8,1024]{2,1,0:T(8,128)} %get-tuple-element.50.top_ref, f32[8,1024]{1,0:T(8,128)S(1)} %get-tuple-element.78.norm_ref, ...), custom_call_target="tpu_custom_call" | custom-call | flops 1024 | bytes 1024 | tf_op jit(solution)/shard_map/pallas_call | solution.py:353
  111.0 1.8 %collective-permute-start.2 = (bf16[512,768]{1,0:T(8,128)(2,1)}, bf16[512,768]{1,0:T(8,128)(2,1)}, u32[]{:S(2)}, u32[]{:S(2)}) collective-permute-start(bf16[512,768]{1,0:T(8,128)(2,1)} %get-tuple-element.81), channel_id=1, source_target_pairs={{0,96},{32,0},{64,32},{96,64},{1,97},{33,1},{65,33},{97,65},{2,98}... | collective-permute-start | bytes 2359304 | tf_op jit(solution)/shard_map/ppermute | solution.py:531
  112.8 0.2 collective-permute-start.3
  113.1 4.0 %shard_map.87 = (f32[512,768]{1,0:T(8,128)S(1)}, f32[512,768]{1,0:T(8,128)S(1)}) custom-call(s32[8]{0:T(128)S(1)} %stack.35.tiles_ref, bf16[1024,768]{1,0:T(8,128)(2,1)S(1)} %get-tuple-element.58.q_ref, f32[16,8,1024]{2,1,0:T(8,128)} %get-tuple-element.50.top_ref, f32[8,1024]{1,0:T(8,128)S(1)} %get-tuple-element.78.norm_ref, ...), custom_call_target="tpu_custom_call" | custom-call | flops 1024 | bytes 1024 | tf_op jit(solution)/shard_map/pallas_call | solution.py:353
  117.1 0.0 collective-permute-done.got_up_ref
  117.1 0.0 collective-permute-done.1.got_down_ref
  117.1 2.7 %shard_map.88 = (bf16[512,768]{1,0:T(8,128)(2,1)}, bf16[512,768]{1,0:T(8,128)(2,1)}) custom-call(f32[512,768]{1,0:T(8,128)S(1)} %get-tuple-element.72.up_ref, f32[512,768]{1,0:T(8,128)S(1)} %get-tuple-element.73.down_ref, bf16[512,768]{1,0:T(8,128)(2,1)} %collective-permute-done.got_up_ref, bf16[512,768]{1,0:T(8,128)(2,1)} %collective-permute-done.1.got_down_ref), custom_call_target="tpu_custom_call" | custom-call | flops 49999998976 | bytes 1024 | tf_op jit(solution)/shard_map/pallas_call | solution.py:326
  119.9 0.4 collective-permute-start.4
  120.2 2.9 %collective-permute-start.5 = (bf16[512,768]{1,0:T(8,128)(2,1)}, bf16[512,768]{1,0:T(8,128)(2,1)}, u32[]{:S(2)}, u32[]{:S(2)}) collective-permute-start(bf16[512,768]{1,0:T(8,128)(2,1)} %get-tuple-element.84), channel_id=1, source_target_pairs={{0,96},{32,0},{64,32},{96,64},{1,97},{33,1},{65,33},{97,65},{2,98}... | collective-permute-start | bytes 2359304 | tf_op jit(solution)/shard_map/ppermute | solution.py:547
  123.1 5.5 %shard_map.89 = (f32[512,768]{1,0:T(8,128)}, f32[512,768]{1,0:T(8,128)}) custom-call(s32[8]{0:T(128)S(1)} %stack.35.tiles_ref, bf16[1024,768]{1,0:T(8,128)(2,1)S(1)} %get-tuple-element.58.q_ref, f32[16,8,1024]{2,1,0:T(8,128)} %get-tuple-element.50.top_ref, f32[8,1024]{1,0:T(8,128)S(1)} %get-tuple-element.78.norm_ref, ...), custom_call_target="tpu_custom_call" | custom-call | flops 1024 | bytes 1024 | tf_op jit(solution)/shard_map/pallas_call | solution.py:353
  128.6 0.0 all-to-all-done.3
  128.6 3.6 %shard_map.85 = bf16[32,8,768]{2,1,0:T(8,128)(2,1)} custom-call(bf16[512,2048]{1,0:T(8,128)(2,1)} %get-tuple-element.56.sel_ref, bf16[2048,384]{1,0:T(8,128)(2,1)S(1)} %bitcast.21), custom_call_target="tpu_custom_call" | custom-call | flops 1024 | bytes 1024 | tf_op jit(solution)/shard_map/pallas_call | solution.py:326
  132.2 7.4 %all-to-all-start.4 = ((bf16[32,8,768]{2,1,0:T(8,128)(2,1)}), bf16[32,8,768]{2,1,0:T(8,128)(2,1)S(1)}, u32[]{:S(2)}, u32[]{:S(2)}) async-start(bf16[32,8,768]{2,1,0:T(8,128)(2,1)} %shard_map.85), calls=%async_computation.4 | async-start | bytes 786432 | tf_op jit(solution)/shard_map/all_to_all | solution.py:373
  139.6 0.0 collective-permute-done.2.a_ref
  139.6 1.4 copy-done.6
  141.0 1.4 copy-done.7
  142.4 1.6 %shard_map.90.base_ref = f32[1024,768]{1,0:T(8,128)S(1)} custom-call(f32[512,768]{1,0:T(8,128)S(1)} %copy-done.6, f32[512,768]{1,0:T(8,128)S(1)} %copy-done.7, bf16[512,768]{1,0:T(8,128)(2,1)} %collective-permute-done.2.a_ref, bf16[512,768]{1,0:T(8,128)(2,1)} %collective-permute-done.3.b_ref), custom_call_target="tpu_custom_call" | custom-call | flops 8000000000 | bytes 1024 | tf_op jit(solution)/shard_map/pallas_call | solution.py:326
  144.1 6.5 %collective-permute-done.4.a_ref = bf16[512,768]{1,0:T(8,128)(2,1)} collective-permute-done((bf16[512,768]{1,0:T(8,128)(2,1)}, bf16[512,768]{1,0:T(8,128)(2,1)}, u32[]{:S(2)}, u32[]{:S(2)}) %collective-permute-start.4) | collective-permute-done | bytes 786464 | tf_op jit(solution)/shard_map/ppermute | solution.py:546
  150.5 0.0 collective-permute-done.5.b_ref
  150.5 3.2 %shard_map.91 = f32[1024,768]{1,0:T(8,128)} custom-call(f32[1024,768]{1,0:T(8,128)S(1)} %shard_map.90.base_ref, bf16[512,768]{1,0:T(8,128)(2,1)} %collective-permute-done.4.a_ref, bf16[512,768]{1,0:T(8,128)(2,1)} %collective-permute-done.5.b_ref), custom_call_target="tpu_custom_call" | custom-call | flops 1024 | bytes 1024 | tf_op jit(solution)/shard_map/pallas_call | solution.py:326
  153.7 0.0 all-to-all-done.4
  153.7 0.9 shard_map.92
  (18 shorter events, 0.0 us)
Async XLA Ops:
  0.6 10.4 %copy-start.8 = (s32[32]{0:T(128)S(1)}, s32[32]{0:T(128)}, u32[]{:S(2)}) copy-start(s32[32]{0:T(128)} %param.9) | copy-start | bytes 388
  2.5 18.3 %all-to-all-start = ((bf16[32,8,896]{2,1,0:T(8,128)(2,1)}), bf16[32,8,896]{2,1,0:T(8,128)(2,1)S(1)}, u32[]{:S(2)}, u32[]{:S(2)}) async-start(bf16[32,8,896]{2,1,0:T(8,128)(2,1)} %bitcast.30), calls=%async_computation | async-start | bytes 917504 | tf_op jit(solution)/shard_map/all_to_all | solution.py:373
  20.8 3.0 %copy-start.1 = (bf16[32,8,896]{2,1,0:T(8,128)(2,1)}, bf16[32,8,896]{2,1,0:T(8,128)(2,1)S(1)}, u32[]{:S(2)}) copy-start(bf16[32,8,896]{2,1,0:T(8,128)(2,1)S(1)} %all-to-all-done) | copy-start | bytes 1376260
  20.9 2.9 %copy-start.4 = (f32[256,128]{1,0:T(8,128)}, f32[256,128]{1,0:T(8,128)S(1)}, u32[]{:S(2)}) copy-start(f32[256,128]{1,0:T(8,128)S(1)} %broadcast_in_dim.44.held_ref) | copy-start | bytes 393220
  23.8 28.0 %all-to-all-start.1 = ((bf16[32,64,384]{2,1,0:T(8,128)(2,1)}), bf16[32,64,384]{2,1,0:T(8,128)(2,1)}, u32[]{:S(2)}, u32[]{:S(2)}) async-start(bf16[32,64,384]{2,1,0:T(8,128)(2,1)} %bitcast.4), calls=%async_computation.1 | async-start | bytes 3145728 | tf_op jit(solution)/shard_map/all_to_all | solution.py:373
  35.2 0.8 copy-start.2
  35.9 15.9 %copy-start.3 = (s32[8,1024]{1,0:T(8,128)S(1)}, s32[8,1024]{1,0:T(8,128)}, u32[]{:S(2)}) copy-start(s32[8,1024]{1,0:T(8,128)} %get-tuple-element.47.col_ref) | copy-start | bytes 98308
  67.2 18.0 %all-to-all-start.2 = ((f32[32,16,128]{2,1,0:T(8,128)}), f32[32,16,128]{2,1,0:T(8,128)S(1)}, u32[]{:S(2)}, u32[]{:S(2)}) async-start(f32[32,16,128]{2,1,0:T(8,128)} %get-tuple-element.49.stat_ref), calls=%async_computation.2 | async-start | bytes 524288 | tf_op jit(solution)/shard_map/all_to_all | solution.py:373
  87.3 8.3 %copy-start = (bf16[1024,768]{1,0:T(8,128)(2,1)S(1)}, bf16[1024,768]{1,0:T(8,128)(2,1)}, u32[]{:S(2)}) copy-start(bf16[1024,768]{1,0:T(8,128)(2,1)} %shard_map.81.u_ref) | copy-start | bytes 4718596
  87.3 8.3 %copy-start.5 = (f32[8,128]{1,0:T(8,128)S(1)}, f32[8,128]{1,0:T(8,128)}, u32[]{:S(2)}) copy-start(f32[8,128]{1,0:T(8,128)} %get-tuple-element.65.col_ref) | copy-start | bytes 12292
  92.4 24.7 %collective-permute-start = (bf16[512,768]{1,0:T(8,128)(2,1)}, bf16[512,768]{1,0:T(8,128)(2,1)}, u32[]{:S(2)}, u32[]{:S(2)}) collective-permute-start(bf16[512,768]{1,0:T(8,128)(2,1)} %get-tuple-element.74), channel_id=1, source_target_pairs={{0,32},{32,64},{64,96},{96,0},{1,33},{33,65},{65,97},{97,1},{2,34}... | collective-permute-start | bytes 2359304 | tf_op jit(solution)/shard_map/ppermute | solution.py:514
  93.9 23.2 %collective-permute-start.1 = (bf16[512,768]{1,0:T(8,128)(2,1)}, bf16[512,768]{1,0:T(8,128)(2,1)}, u32[]{:S(2)}, u32[]{:S(2)}) collective-permute-start(bf16[512,768]{1,0:T(8,128)(2,1)} %get-tuple-element.75), channel_id=1, source_target_pairs={{0,96},{32,0},{64,32},{96,64},{1,97},{33,1},{65,33},{97,65},{2,98}... | collective-permute-start | bytes 2359304 | tf_op jit(solution)/shard_map/ppermute | solution.py:515
  98.6 30.0 %all-to-all-start.3 = ((bf16[32,64,384]{2,1,0:T(8,128)(2,1)}), bf16[32,64,384]{2,1,0:T(8,128)(2,1)S(1)}, u32[]{:S(2)}, u32[]{:S(2)}) async-start(bf16[32,64,384]{2,1,0:T(8,128)(2,1)} %bitcast.28), calls=%async_computation.3 | async-start | bytes 3145728 | tf_op jit(solution)/shard_map/all_to_all | solution.py:373
  111.0 28.6 %collective-permute-start.2 = (bf16[512,768]{1,0:T(8,128)(2,1)}, bf16[512,768]{1,0:T(8,128)(2,1)}, u32[]{:S(2)}, u32[]{:S(2)}) collective-permute-start(bf16[512,768]{1,0:T(8,128)(2,1)} %get-tuple-element.81), channel_id=1, source_target_pairs={{0,96},{32,0},{64,32},{96,64},{1,97},{33,1},{65,33},{97,65},{2,98}... | collective-permute-start | bytes 2359304 | tf_op jit(solution)/shard_map/ppermute | solution.py:531
  112.8 26.8 %collective-permute-start.3 = (bf16[512,768]{1,0:T(8,128)(2,1)}, bf16[512,768]{1,0:T(8,128)(2,1)}, u32[]{:S(2)}, u32[]{:S(2)}) collective-permute-start(bf16[512,768]{1,0:T(8,128)(2,1)} %get-tuple-element.82), channel_id=1, source_target_pairs={{0,32},{32,64},{64,96},{96,0},{1,33},{33,65},{65,97},{97,1},{2,34}... | collective-permute-start | bytes 2359304 | tf_op jit(solution)/shard_map/ppermute | solution.py:530
  119.9 30.7 %collective-permute-start.4 = (bf16[512,768]{1,0:T(8,128)(2,1)}, bf16[512,768]{1,0:T(8,128)(2,1)}, u32[]{:S(2)}, u32[]{:S(2)}) collective-permute-start(bf16[512,768]{1,0:T(8,128)(2,1)} %get-tuple-element.83), channel_id=1, source_target_pairs={{0,32},{32,64},{64,96},{96,0},{1,33},{33,65},{65,97},{97,1},{2,34}... | collective-permute-start | bytes 2359304 | tf_op jit(solution)/shard_map/ppermute | solution.py:546
  120.2 30.3 %collective-permute-start.5 = (bf16[512,768]{1,0:T(8,128)(2,1)}, bf16[512,768]{1,0:T(8,128)(2,1)}, u32[]{:S(2)}, u32[]{:S(2)}) collective-permute-start(bf16[512,768]{1,0:T(8,128)(2,1)} %get-tuple-element.84), channel_id=1, source_target_pairs={{0,96},{32,0},{64,32},{96,64},{1,97},{33,1},{65,33},{97,65},{2,98}... | collective-permute-start | bytes 2359304 | tf_op jit(solution)/shard_map/ppermute | solution.py:547
  132.2 21.5 %all-to-all-start.4 = ((bf16[32,8,768]{2,1,0:T(8,128)(2,1)}), bf16[32,8,768]{2,1,0:T(8,128)(2,1)S(1)}, u32[]{:S(2)}, u32[]{:S(2)}) async-start(bf16[32,8,768]{2,1,0:T(8,128)(2,1)} %shard_map.85), calls=%async_computation.4 | async-start | bytes 786432 | tf_op jit(solution)/shard_map/all_to_all | solution.py:373
  139.6 1.4 copy-start.6
  141.0 1.4 copy-start.7

commit v3 on v2

--- a/solution.py
+++ b/solution.py
@@ -140,7 +140,7 @@
         out = jnp.where(row == s, lanes[:, s * ROWS : (s + 1) * ROWS], out)
     return out
 
-def scores_kernel(got_ref, col_ref, w_ref, r_ref, p_ref, q_ref, top_ref, stat_ref, row_ref, s_ref, high, total, found):
+def scores_kernel(got_ref, col_ref, w_ref, p_ref, q_ref, top_ref, stat_ref, row_ref, s_ref, high, total, found):
     step = pl.program_id(0)
     rows = s_ref.shape[1]
 
@@ -153,44 +153,37 @@
                     q_ref[here, h * HALF : (h + 1) * HALF] = got_ref[g, h, s]
         high[...] = jnp.full_like(high, NEG)
         total[...] = jnp.zeros_like(total)
+        found[...] = jnp.zeros_like(found)
 
     n = BIG_TILE // PART_TILE
-    top, tot = high[...], total[...]
+    top, tot, pick = high[...], total[...], found[...]
     for k in range(n + 1):
         if k < n:
             here = slice(k * PART_TILE, (k + 1) * PART_TILE)
             s_ref[here, :] = dot(w_ref[here, :], q_ref[...], ((1,), (1,)))
         if k > 0:
             here = slice((k - 1) * PART_TILE, k * PART_TILE)
-            s = s_ref[here, :].reshape(PART_TILE // 8, 8, rows)
-            best = jnp.max(jnp.max(s, axis=0), axis=0, keepdims=True)
+            s = s_ref[here, :]
+            target = iota(s.shape, 0) + (step * BIG_TILE + (k - 1) * PART_TILE) == col_ref[0:1, :]
+            pick += jnp.sum(jnp.where(target, s, 0.0).reshape(PART_TILE // 8, 8, rows), axis=0)
+            best = jnp.max(jnp.max(s.reshape(PART_TILE // 8, 8, rows), axis=0), axis=0, keepdims=True)
             best = jnp.broadcast_to(best, (8, rows))
-            e = jnp.exp(s - best[None])
-            target = label_iota(rows) == (col_ref[...] - (step * BIG_TILE + (k - 1) * PART_TILE))[None]
-            p_ref[here, :] = jnp.where(target, 0.0, e).reshape(PART_TILE, rows).astype(BF16)
+            e = jnp.exp(s - best[0:1, :])
+            p_ref[here, :] = jnp.where(target, 0.0, e).astype(BF16)
             new = jnp.maximum(top, best)
-            tot = tot * jnp.exp(top - new) + jnp.sum(e, axis=0) * jnp.exp(best - new)
+            add = jnp.sum(e.reshape(PART_TILE // 8, 8, rows), axis=0)
+            tot = tot * jnp.exp(top - new) + add * jnp.exp(best - new)
             top = new
             top_ref[k - 1] = best
-    high[...], total[...] = top, tot
-
-    two = 2 * ROWS
-    mine = q_ref[pl.ds(pl.multiple_of(step * two, two), two), :].astype(F32) * r_ref[...].astype(F32)
-    folded = mine[:, :ROWS]
-    for c in range(1, FEAT // ROWS):
-        folded += mine[:, c * ROWS : (c + 1) * ROWS]
-    for i in range(2):
-        one = jnp.sum(folded[i * ROWS : (i + 1) * ROWS].T, axis=0, keepdims=True)
-        found[step, i : i + 1, :] = one
+    high[...], total[...], found[...] = top, tot, pick
 
     @pl.when(step == pl.num_programs(0) - 1)
     def _():
         lse = top[0:1, :] + jnp.log(jnp.sum(tot, axis=0, keepdims=True))
         row_ref[...] = jnp.broadcast_to(lse, (8, rows))
+        chosen = jnp.sum(pick, axis=0, keepdims=True)
         stat_ref[:, :SLOTS, :] = jnp.broadcast_to(by_slot(lse)[None], (NDEV, SLOTS, ROWS))
-        for i in range(SLOTS // 2):
-            here = slice(SLOTS + 2 * i, SLOTS + 2 * i + 2)
-            stat_ref[:, here, :] = jnp.broadcast_to(found[i][None], (NDEV, 2, ROWS))
+        stat_ref[:, SLOTS:, :] = jnp.broadcast_to(by_slot(chosen)[None], (NDEV, SLOTS, ROWS))
 
 
 def normal_kernel(stat_ref, mask_ref, norm_ref, rest_ref, slots_ref, loss_ref):
@@ -239,40 +232,52 @@
         rows_from(acc, out_ref)
 
 
-def others_kernel(top_ref, row_ref, w_ref, p_ref, out_ref, acc, scaled):
-    step = pl.program_id(0)
+def scaled_tile(p_ref, top_ref, row_ref, out_ref):
+    rows = out_ref.shape[1]
     for i in range(BIG_TILE // PART_TILE):
         scale = jnp.exp(top_ref[i] - row_ref[...])
         here = slice(i * PART_TILE, (i + 1) * PART_TILE)
-        p = p_ref[here, :].astype(F32).reshape(PART_TILE // 8, 8, scale.shape[1])
-        scaled[here, :] = (p * scale[None]).reshape(PART_TILE, scale.shape[1]).astype(BF16)
-    add_to(acc, dot(w_ref[...], scaled[...], ((0,), (0,))), step == 0)
+        p = p_ref[here, :].astype(F32).reshape(PART_TILE // 8, 8, rows)
+        out_ref[here, :] = (p * scale[None]).reshape(PART_TILE, rows).astype(BF16)
+
+
+def others_kernel(top_ref, row_ref, w_ref, p_ref, acc_ref, scaled):
+    scaled_tile(p_ref, top_ref, row_ref, scaled)
+    add_to(acc_ref, dot(w_ref[...], scaled[...], ((0,), (0,))), pl.program_id(0) == 0)
+
+
+def part_kernel(top_ref, row_ref, w_ref, p_ref, half_ref, r_ref, stat_ref, norm_ref, col_ref, out_ref, acc, scaled):
+    step = pl.program_id(0)
+
+    @pl.when(step == 0)
+    def _():
+        acc[...] = half_ref[...]
+
+    scaled_tile(p_ref, top_ref, row_ref, scaled)
+    acc[...] += dot(w_ref[...], scaled[...], ((0,), (0,)))
 
     @pl.when(step == pl.num_programs(0) - 1)
     def _():
-        rows_from(acc, out_ref)
-
-
-def part_kernel(u_ref, r_ref, stat_ref, norm_ref, col_ref, out_ref):
-    norm = norm_ref[...]
-    scale = jnp.exp(stat_ref[0, :SLOTS, :] - norm).T
-    rest = jnp.where(col_ref[...] >= 0.0, jnp.exp(stat_ref[0, SLOTS:, :] - norm) - 1.0, 0.0).T
-    for s in range(SLOTS):
-        u = u_ref[s * ROWS : (s + 1) * ROWS, :].astype(F32)
-        r = r_ref[s * ROWS : (s + 1) * ROWS, :].astype(F32)
-        part = (scale[:, s : s + 1] * u + rest[:, s : s + 1] * r).astype(BF16).reshape(16, 8, FEAT)
-        for h in range(2):
-            out_ref[:, h, s * 8 : (s + 1) * 8, :] = part[:, :, h * HALF : (h + 1) * HALF]
-
-
-def table_grad_kernel(base, tiles_ref, q_ref, top_ref, norm_ref, rest_ref, col_ref, *refs):
-    n = len(refs) // 2
+        norm = norm_ref[...]
+        scale = jnp.exp(stat_ref[0, :SLOTS, :] - norm).T
+        rest = jnp.where(col_ref[...] >= 0.0, jnp.exp(stat_ref[0, SLOTS:, :] - norm) - 1.0, 0.0).T
+        for s in range(SLOTS):
+            here = slice(s * ROWS, (s + 1) * ROWS)
+            u = acc[:, here].T
+            r = r_ref[here, :].astype(F32)
+            part = (scale[:, s : s + 1] * u + rest[:, s : s + 1] * r).astype(BF16).reshape(16, 8, FEAT)
+            for h in range(2):
+                out_ref[:, h, s * 8 : (s + 1) * 8, :] = part[:, :, h * HALF : (h + 1) * HALF]
+
+
+def table_grad_kernel(base, tiles_ref, q_ref, norm_ref, rest_ref, col_ref, *refs):
+    n = len(refs) // 3
     for i in range(n):
-        p_ref, out_ref = refs[i], refs[n + i]
+        p_ref, top_ref, out_ref = refs[i], refs[n + i], refs[2 * n + i]
         tile = tiles_ref[base + i]
         for k in range(TILE // PART_TILE):
             here = slice(k * PART_TILE, (k + 1) * PART_TILE)
-            scale = jnp.exp(top_ref[tile * (TILE // PART_TILE) + k] - norm_ref[...])
+            scale = jnp.exp(top_ref[k] - norm_ref[...])
             rows = scale.shape[1]
             p = p_ref[here, :].astype(F32).reshape(PART_TILE // 8, 8, rows)
             target = label_iota(rows) == (col_ref[...] - (tile * TILE + k * PART_TILE))[None]
@@ -415,7 +420,7 @@
         positive_kernel,
         steps,
         [fixed((8, rows)), w_spec],
-        shape((rows, FEAT), BF16),
+        pltpu.HBM((rows, FEAT), BF16),
         fixed((rows, FEAT)),
         (pltpu.VMEM((FEAT, rows), F32),),
         col,
@@ -427,7 +432,7 @@
     p, q, tops, stats, lse_row = stepped(
         scores_kernel,
         steps,
-        [fixed((16, 2, SLOTS, 8, HALF)), fixed((8, rows)), w_spec, tiled((2 * ROWS, FEAT))],
+        [fixed((16, 2, SLOTS, 8, HALF)), fixed((8, rows)), w_spec],
         (
             pltpu.HBM((LABELS, rows), BF16),
             shape((rows, FEAT), BF16),
@@ -446,29 +451,33 @@
             pltpu.VMEM((BIG_TILE, rows), F32),
             pltpu.VMEM((8, rows), F32),
             pltpu.VMEM((8, rows), F32),
-            pltpu.VMEM((SLOTS // 2, 2, ROWS), F32),
+            pltpu.VMEM((8, rows), F32),
         ),
         pltpu.with_memory_space_constraint(arrived.reshape(16, 2, SLOTS, 8, HALF), pltpu.HBM),
         col,
         ranker,
-        positive_rows,
     )
     all_stats = swap(stats)
     p = pltpu.with_memory_space_constraint(p, pltpu.HBM)
     tops = pltpu.with_memory_space_constraint(tops, pltpu.HBM)
-    others = stepped(
+    later = steps // 2
+
+    def shifted(dims):
+        return pl.BlockSpec(dims, lambda i, *_: (i + later,) + (0,) * (len(dims) - 1))
+
+    half_sum = stepped(
         others_kernel,
-        steps,
+        later,
         [tiled((parts_each, 8, rows)), fixed((8, rows)), w_spec, tiled((BIG_TILE, rows))],
-        pltpu.HBM((rows, FEAT), BF16),
-        fixed((rows, FEAT)),
-        (pltpu.VMEM((FEAT, rows), F32), pltpu.VMEM((BIG_TILE, rows), BF16)),
+        pltpu.HBM((FEAT, rows), F32),
+        fixed((FEAT, rows)),
+        (pltpu.VMEM((BIG_TILE, rows), BF16),),
         tops,
         lse_row,
         ranker,
         p,
     )
-    all_stats, others = lax.optimization_barrier((all_stats, others))
+    all_stats, half_sum = lax.optimization_barrier((all_stats, half_sum))
     norm, rest, norm_slots, loss = whole(
         normal_kernel,
         (lanes, lanes, shape((SLOTS, ROWS), F32), shape((2, ROWS), F32)),
@@ -490,22 +499,25 @@
             1,
             [
                 fixed((rows, FEAT)),
-                fixed((LABELS // PART_TILE, 8, rows)),
                 fixed((8, rows)),
                 fixed((8, rows)),
                 fixed((8, rows)),
                 *(pl.BlockSpec((TILE, rows), lambda _, t, i=i: (t[first + i], 0)) for i in range(n)),
+                *(
+                    pl.BlockSpec((TILE // PART_TILE, 8, rows), lambda _, t, i=i: (t[first + i], 0, 0))
+                    for i in range(n)
+                ),
             ],
             tuple(place((TILE, FEAT), d) for d in dtypes),
             tuple(fixed((TILE, FEAT)) for _ in dtypes),
             (),
             tiles,
             q,
-            tops,
             norm,
             rest,
             col,
             *([p] * n),
+            *([tops] * n),
             scalars=1,
         )
 
@@ -513,15 +525,33 @@
     far_a, far_b, norm_slots, norm = lax.optimization_barrier((far_a, far_b, norm_slots, norm))
     via_up = lax.ppermute(far_a, "dp", up)
     via_down = lax.ppermute(far_b, "dp", down)
-    part = whole(
+    part = stepped(
         part_kernel,
+        later,
+        [
+            shifted((parts_each, 8, rows)),
+            fixed((8, rows)),
+            shifted((BIG_TILE, FEAT)),
+            shifted((BIG_TILE, rows)),
+            fixed((FEAT, rows)),
+            fixed((rows, FEAT)),
+            fixed(stats.shape),
+            fixed((SLOTS, ROWS)),
+            fixed((SLOTS, ROWS)),
+        ],
         pltpu.HBM((16, 2, 64, HALF), BF16),
-        others,
-        positive_rows,
+        fixed((16, 2, 64, HALF)),
+        (pltpu.VMEM((FEAT, rows), F32), pltpu.VMEM((BIG_TILE, rows), BF16)),
+        tops,
+        lse_row,
+        ranker,
+        p,
+        pltpu.with_memory_space_constraint(half_sum, pltpu.HBM),
+        pltpu.with_memory_space_constraint(positive_rows, pltpu.HBM),
         stats,
         norm_slots,
         col_slots,
-        limit=16,
+        limit=36,
     )
     part, norm = lax.optimization_barrier((part, norm))
     parts = swap(part.reshape(NDEV, 64, HALF)).reshape(2048, HALF)

time: 156 us -> 157 us (level)
  Pallas kernels: 83.1 us -> 85 us
    pallas_call x7 -> x8, Pallas kernels: 57.6 us -> 62.4 us  [stepped(): pl.pallas_call(kernel, grid_spec=spec, out_shape=outs, compiler_params=pl...]
    pallas_call x10 -> x9, Pallas kernels: 25.5 us -> 22.6 us  [whole(): pl.pallas_call(kernel, out_shape=outs, in_specs=[place(i, hbm, smem) for...]
  transfers between devices with their start and end apart: 11 -> 11, of which waited for: 3 -> 3; matrix products, arithmetic and copies ran while one was open for 1% -> 1% of each run, Pallas kernels for 35% -> 38%
where the time goes in v3:
time: 157 us; the launch traced here: 156 us
  Pallas kernels  85 us (54%)
  starting transfers between devices  42.6 us (27%)
  waiting for transfers between devices  20.6 us (13%)
  local copies, waits for them, and re-layouts  5.66 us (4%)
    pallas_call x8, Pallas kernels, stepped(): pl.pallas_call(kernel, grid_spec=spec, out_shape=outs, compiler_params=pl...  62.4 us
    all_to_all x5, starting transfers between devices, swap(): return lax.all_to_all(x, 'label', split_axis=0, concat_axis=0, tiled=True)  34.1 us
    pallas_call x9, Pallas kernels, whole(): pl.pallas_call(kernel, out_shape=outs, in_specs=[place(i, hbm, smem) for...  22.6 us
    all_to_all x5, waiting for transfers between devices, swap(): return lax.all_to_all(x, 'label', split_axis=0, concat_axis=0, tiled=True)  13.8 us
    ppermute x1, waiting for transfers between devices, per_device(): from_prev_a = lax.ppermute(relay_up, 'dp', up)  6.8 us
    unnamed x18, local copies, waits for them, and re-layouts  4.73 us
  transfers between devices with their start and end apart: 11, of which 3 were waited for; matrix products, arithmetic and copies ran while one was open for 1% of the time, Pallas kernels for 38%

profile of v3, /device:TPU:2, one launch (start us, length us, event | category | flops | bytes accessed | tf_op | source)
XLA Modules:
  0.0 156.1 jit_solution(6289242505894261768)
XLA Ops:
  0.6 1.9 %shard_map.76 = bf16[16,2,8,896]{3,2,1,0:T(8,128)(2,1)} custom-call(bf16[2,16,8,768]{3,2,1,0:T(8,128)(2,1)} %bitcast.34, s32[2,128]{1,0:T(2,128)} %bitcast.35, s32[2,4]{1,0:T(2,128)} %beam_hbm.1), custom_call_target="tpu_custom_call" | custom-call | flops 1024 | bytes 1024 | tf_op jit(solution)/shard_map/pallas_call | solution.py:331
  2.5 8.5 %all-to-all-start = ((bf16[32,8,896]{2,1,0:T(8,128)(2,1)}), bf16[32,8,896]{2,1,0:T(8,128)(2,1)S(1)}, u32[]{:S(2)}, u32[]{:S(2)}) async-start(bf16[32,8,896]{2,1,0:T(8,128)(2,1)} %bitcast.32), calls=%async_computation | async-start | bytes 917504 | tf_op jit(solution)/shard_map/all_to_all | solution.py:378
  11.0 0.1 select_reduce_fusion
  11.1 0.1 broadcast_in_dim.42
  11.2 0.1 broadcast_in_dim.43
  11.3 9.5 %all-to-all-done = bf16[32,8,896]{2,1,0:T(8,128)(2,1)S(1)} async-done(((bf16[32,8,896]{2,1,0:T(8,128)(2,1)}), bf16[32,8,896]{2,1,0:T(8,128)(2,1)S(1)}, u32[]{:S(2)}, u32[]{:S(2)}) %all-to-all-start) | async-done | bytes 458784 | tf_op jit(solution)/shard_map/all_to_all | solution.py:378
  20.8 0.1 broadcast_in_dim.44.held_ref
  20.9 2.9 %shard_map.77 = bf16[2048,384]{1,0:T(8,128)(2,1)} custom-call(bf16[256,896]{1,0:T(8,128)(2,1)S(1)} %bitcast.22, f32[256,128]{1,0:T(8,128)S(1)} %broadcast_in_dim.44.held_ref), custom_call_target="tpu_custom_call" | custom-call | flops 1024 | bytes 1024 | tf_op jit(solution)/shard_map/pallas_call | solution.py:331
  23.8 5.1 %all-to-all-start.1 = ((bf16[32,64,384]{2,1,0:T(8,128)(2,1)}), bf16[32,64,384]{2,1,0:T(8,128)(2,1)S(1)}, u32[]{:S(2)}, u32[]{:S(2)}) async-start(bf16[32,64,384]{2,1,0:T(8,128)(2,1)} %bitcast.4), calls=%async_computation.1 | async-start | bytes 3145728 | tf_op jit(solution)/shard_map/all_to_all | solution.py:378
  28.9 0.6 fusion
  30.2 0.6 iota.17.mine_ref
  30.8 3.7 %shard_map.78 = (bf16[512,2048]{1,0:T(8,128)(2,1)}, f32[256,128]{1,0:T(8,128)}, s32[8,1024]{1,0:T(8,128)}, f32[8,128]{1,0:T(8,128)}) custom-call(bf16[256,896]{1,0:T(8,128)(2,1)} %bitcast.23, f32[256,128]{1,0:T(8,128)} %copy-done.3, f32[16,128]{1,0:T(8,128)} %iota.17.mine_ref), custom_call_target="tpu_custom_call" | custom-call | flops 1024 | bytes 1024 | tf_op jit(solution)/shard_map/pallas_call | solution.py:331
  34.5 0.8 copy-done.1
  35.3 11.5 %shard_map.79.r_ref = bf16[1024,768]{1,0:T(8,128)(2,1)} custom-call(s32[8,1024]{1,0:T(8,128)S(1)} %copy-done.1, bf16[4096,768]{1,0:T(8,128)(2,1)} %bitcast.25), custom_call_target="tpu_custom_call" | custom-call | flops 1024 | bytes 1024 | tf_op jit(solution)/shard_map/pallas_call | solution.py:358
  46.8 4.3 %all-to-all-done.1 = bf16[32,64,384]{2,1,0:T(8,128)(2,1)S(1)} async-done(((bf16[32,64,384]{2,1,0:T(8,128)(2,1)}), bf16[32,64,384]{2,1,0:T(8,128)(2,1)S(1)}, u32[]{:S(2)}, u32[]{:S(2)}) %all-to-all-start.1) | async-done | bytes 1572896 | tf_op jit(solution)/shard_map/all_to_all | solution.py:378
  51.0 1.1 copy-done.7
  52.2 13.5 %shard_map.80 = (bf16[4096,1024]{1,0:T(8,128)(2,1)}, bf16[1024,768]{1,0:T(8,128)(2,1)S(1)}, f32[16,8,1024]{2,1,0:T(8,128)}, f32[32,16,128]{2,1,0:T(8,128)}, f32[8,1024]{1,0:T(8,128)S(1)}) custom-call(bf16[16,2,8,8,384]{4,3,2,1,0:T(8,128)(2,1)} %bitcast.30, s32[8,1024]{1,0:T(8,128)S(1)} %copy-done.2, bf16[4096,768]{1,0:T(8,128)(2,1)} %bitcast.26), custom_call_target="tpu_custom_call" | custom-call | flops 1024 | bytes 1024 | tf_op jit(solution)/shard_map/pallas_call | solution.py:358
  65.7 5.7 %all-to-all-start.2 = ((f32[32,16,128]{2,1,0:T(8,128)}), f32[32,16,128]{2,1,0:T(8,128)S(1)}, u32[]{:S(2)}, u32[]{:S(2)}) async-start(f32[32,16,128]{2,1,0:T(8,128)} %get-tuple-element.48.stat_ref), calls=%async_computation.2 | async-start | bytes 524288 | tf_op jit(solution)/shard_map/all_to_all | solution.py:378
  71.4 0.1 stack.35.tiles_ref
  71.5 7.9 %shard_map.81.half_ref = f32[768,1024]{1,0:T(8,128)} custom-call(f32[16,8,1024]{2,1,0:T(8,128)} %get-tuple-element.49.top_ref.refs_2_.refs_3_, f32[8,1024]{1,0:T(8,128)S(1)} %get-tuple-element.50.row_ref, bf16[4096,768]{1,0:T(8,128)(2,1)} %bitcast.27, bf16[4096,1024]{1,0:T(8,128)(2,1)} %get-tuple-element.51.p_ref.refs_0_.refs_1_), custom_call_target="tpu_custom_call" | custom-call | flops 1024 | bytes 1024 | tf_op jit(solution)/shard_map/pallas_call | solution.py:358
  79.5 0.0 all-to-all-done.2.stat_ref
  79.5 2.1 %shard_map.82 = (f32[8,1024]{1,0:T(8,128)S(1)}, f32[8,1024]{1,0:T(8,128)S(1)}, f32[8,128]{1,0:T(8,128)S(1)}, f32[2,128]{1,0:T(2,128)}) custom-call(f32[32,16,128]{2,1,0:T(8,128)S(1)} %all-to-all-done.2.stat_ref, f32[256,128]{1,0:T(8,128)} %get-tuple-element.53.mask_ref), custom_call_target="tpu_custom_call" | custom-call | flops 1024 | bytes 1024 | tf_op jit(solution)/shard_map/pallas_call | solution.py:331
  81.5 4.8 %shard_map.83 = (bf16[512,768]{1,0:T(8,128)(2,1)}, bf16[512,768]{1,0:T(8,128)(2,1)}) custom-call(s32[8]{0:T(128)S(1)} %stack.35.tiles_ref, bf16[1024,768]{1,0:T(8,128)(2,1)S(1)} %get-tuple-element.58.q_ref, f32[8,1024]{1,0:T(8,128)S(1)} %get-tuple-element.78.norm_ref, f32[8,1024]{1,0:T(8,128)S(1)} %get-tuple-element.60.rest_ref, s32[8,1024]{1,0:T(8,128)S(1)} %copy-done.2, ...), custom_call_target="tpu_custom_call" | custom-call | flops 1024 | bytes 1024 | tf_op jit(solution)/shard_map/pallas_call | solution.py:358
  86.3 1.6 %collective-permute-start = (bf16[512,768]{1,0:T(8,128)(2,1)}, bf16[512,768]{1,0:T(8,128)(2,1)}, u32[]{:S(2)}, u32[]{:S(2)}) collective-permute-start(bf16[512,768]{1,0:T(8,128)(2,1)} %get-tuple-element.74), channel_id=1, source_target_pairs={{0,32},{32,64},{64,96},{96,0},{1,33},{33,65},{65,97},{97,1},{2,34}... | collective-permute-start | bytes 2359304 | tf_op jit(solution)/shard_map/ppermute | solution.py:526
  87.9 1.7 %collective-permute-start.1 = (bf16[512,768]{1,0:T(8,128)(2,1)}, bf16[512,768]{1,0:T(8,128)(2,1)}, u32[]{:S(2)}, u32[]{:S(2)}) collective-permute-start(bf16[512,768]{1,0:T(8,128)(2,1)} %get-tuple-element.75), channel_id=1, source_target_pairs={{0,96},{32,0},{64,32},{96,64},{1,97},{33,1},{65,33},{97,65},{2,98}... | collective-permute-start | bytes 2359304 | tf_op jit(solution)/shard_map/ppermute | solution.py:527
  89.6 10.6 %shard_map.84 = bf16[16,2,64,384]{3,2,1,0:T(8,128)(2,1)} custom-call(f32[16,8,1024]{2,1,0:T(8,128)} %get-tuple-element.49.top_ref.refs_2_.refs_3_, f32[8,1024]{1,0:T(8,128)S(1)} %get-tuple-element.50.row_ref, bf16[4096,768]{1,0:T(8,128)(2,1)} %bitcast.28, bf16[4096,1024]{1,0:T(8,128)(2,1)} %get-tuple-element.51.p_ref.refs_0_.refs_1_, ...), custom_call_target="tpu_custom_call" | custom-call | flops 1024 | bytes 1024 | tf_op jit(solution)/shard_map/pallas_call | solution.py:358
  100.2 7.5 %all-to-all-start.3 = ((bf16[32,64,384]{2,1,0:T(8,128)(2,1)}), bf16[32,64,384]{2,1,0:T(8,128)(2,1)S(1)}, u32[]{:S(2)}, u32[]{:S(2)}) async-start(bf16[32,64,384]{2,1,0:T(8,128)(2,1)} %bitcast.29), calls=%async_computation.3 | async-start | bytes 3145728 | tf_op jit(solution)/shard_map/all_to_all | solution.py:378
  107.7 4.8 %shard_map.86 = (bf16[512,768]{1,0:T(8,128)(2,1)}, bf16[512,768]{1,0:T(8,128)(2,1)}) custom-call(s32[8]{0:T(128)S(1)} %stack.35.tiles_ref, bf16[1024,768]{1,0:T(8,128)(2,1)S(1)} %get-tuple-element.58.q_ref, f32[8,1024]{1,0:T(8,128)S(1)} %get-tuple-element.78.norm_ref, f32[8,1024]{1,0:T(8,128)S(1)} %get-tuple-element.60.rest_ref, s32[8,1024]{1,0:T(8,128)S(1)} %copy-done.2, ...), custom_call_target="tpu_custom_call" | custom-call | flops 1024 | bytes 1024 | tf_op jit(solution)/shard_map/pallas_call | solution.py:358
  112.5 1.8 %collective-permute-start.2 = (bf16[512,768]{1,0:T(8,128)(2,1)}, bf16[512,768]{1,0:T(8,128)(2,1)}, u32[]{:S(2)}, u32[]{:S(2)}) collective-permute-start(bf16[512,768]{1,0:T(8,128)(2,1)} %get-tuple-element.81), channel_id=1, source_target_pairs={{0,96},{32,0},{64,32},{96,64},{1,97},{33,1},{65,33},{97,65},{2,98}... | collective-permute-start | bytes 2359304 | tf_op jit(solution)/shard_map/ppermute | solution.py:561
  114.3 0.2 collective-permute-start.3
  114.5 3.9 %shard_map.87 = (f32[512,768]{1,0:T(8,128)S(1)}, f32[512,768]{1,0:T(8,128)S(1)}) custom-call(s32[8]{0:T(128)S(1)} %stack.35.tiles_ref, bf16[1024,768]{1,0:T(8,128)(2,1)S(1)} %get-tuple-element.58.q_ref, f32[8,1024]{1,0:T(8,128)S(1)} %get-tuple-element.78.norm_ref, f32[8,1024]{1,0:T(8,128)S(1)} %get-tuple-element.60.rest_ref, s32[8,1024]{1,0:T(8,128)S(1)} %copy-done.2, ...), custom_call_target="tpu_custom_call" | custom-call | flops 1024 | bytes 1024 | tf_op jit(solution)/shard_map/pallas_call | solution.py:358
  118.4 0.0 collective-permute-done.got_up_ref
  118.5 0.0 collective-permute-done.1.got_down_ref
  118.5 2.7 %shard_map.88 = (bf16[512,768]{1,0:T(8,128)(2,1)}, bf16[512,768]{1,0:T(8,128)(2,1)}) custom-call(f32[512,768]{1,0:T(8,128)S(1)} %get-tuple-element.72.up_ref, f32[512,768]{1,0:T(8,128)S(1)} %get-tuple-element.73.down_ref, bf16[512,768]{1,0:T(8,128)(2,1)} %collective-permute-done.got_up_ref, bf16[512,768]{1,0:T(8,128)(2,1)} %collective-permute-done.1.got_down_ref), custom_call_target="tpu_custom_call" | custom-call | flops 49999998976 | bytes 1024 | tf_op jit(solution)/shard_map/pallas_call | solution.py:331
  121.2 0.3 collective-permute-start.4
  121.5 2.9 %collective-permute-start.5 = (bf16[512,768]{1,0:T(8,128)(2,1)}, bf16[512,768]{1,0:T(8,128)(2,1)}, u32[]{:S(2)}, u32[]{:S(2)}) collective-permute-start(bf16[512,768]{1,0:T(8,128)(2,1)} %get-tuple-element.84), channel_id=1, source_target_pairs={{0,96},{32,0},{64,32},{96,64},{1,97},{33,1},{65,33},{97,65},{2,98}... | collective-permute-start | bytes 2359304 | tf_op jit(solution)/shard_map/ppermute | solution.py:577
  124.4 5.3 %shard_map.89 = (f32[512,768]{1,0:T(8,128)}, f32[512,768]{1,0:T(8,128)}) custom-call(s32[8]{0:T(128)S(1)} %stack.35.tiles_ref, bf16[1024,768]{1,0:T(8,128)(2,1)S(1)} %get-tuple-element.58.q_ref, f32[8,1024]{1,0:T(8,128)S(1)} %get-tuple-element.78.norm_ref, f32[8,1024]{1,0:T(8,128)S(1)} %get-tuple-element.60.rest_ref, s32[8,1024]{1,0:T(8,128)S(1)} %copy-done.2, ...), custom_call_target="tpu_custom_call" | custom-call | flops 1024 | bytes 1024 | tf_op jit(solution)/shard_map/pallas_call | solution.py:358
  129.8 0.0 all-to-all-done.3
  129.8 3.6 %shard_map.85 = bf16[32,8,768]{2,1,0:T(8,128)(2,1)} custom-call(bf16[512,2048]{1,0:T(8,128)(2,1)} %get-tuple-element.55.sel_ref, bf16[2048,384]{1,0:T(8,128)(2,1)S(1)} %bitcast.21), custom_call_target="tpu_custom_call" | custom-call | flops 1024 | bytes 1024 | tf_op jit(solution)/shard_map/pallas_call | solution.py:331
  133.4 7.4 %all-to-all-start.4 = ((bf16[32,8,768]{2,1,0:T(8,128)(2,1)}), bf16[32,8,768]{2,1,0:T(8,128)(2,1)S(1)}, u32[]{:S(2)}, u32[]{:S(2)}) async-start(bf16[32,8,768]{2,1,0:T(8,128)(2,1)} %shard_map.85), calls=%async_computation.4 | async-start | bytes 786432 | tf_op jit(solution)/shard_map/all_to_all | solution.py:378
  140.7 0.0 collective-permute-done.2.a_ref
  140.8 0.0 copy-start.5
  140.8 1.4 copy-done.5
  142.2 1.4 copy-done.6
  143.6 1.6 %shard_map.90.base_ref = f32[1024,768]{1,0:T(8,128)S(1)} custom-call(f32[512,768]{1,0:T(8,128)S(1)} %copy-done.5, f32[512,768]{1,0:T(8,128)S(1)} %copy-done.6, bf16[512,768]{1,0:T(8,128)(2,1)} %collective-permute-done.2.a_ref, bf16[512,768]{1,0:T(8,128)(2,1)} %collective-permute-done.3.b_ref), custom_call_target="tpu_custom_call" | custom-call | flops 8000000000 | bytes 1024 | tf_op jit(solution)/shard_map/pallas_call | solution.py:331
  145.2 6.8 %collective-permute-done.4.a_ref = bf16[512,768]{1,0:T(8,128)(2,1)} collective-permute-done((bf16[512,768]{1,0:T(8,128)(2,1)}, bf16[512,768]{1,0:T(8,128)(2,1)}, u32[]{:S(2)}, u32[]{:S(2)}) %collective-permute-start.4) | collective-permute-done | bytes 786464 | tf_op jit(solution)/shard_map/ppermute | solution.py:576
  152.0 3.2 %shard_map.91 = f32[1024,768]{1,0:T(8,128)} custom-call(f32[1024,768]{1,0:T(8,128)S(1)} %shard_map.90.base_ref, bf16[512,768]{1,0:T(8,128)(2,1)} %collective-permute-done.4.a_ref, bf16[512,768]{1,0:T(8,128)(2,1)} %collective-permute-done.5.b_ref), custom_call_target="tpu_custom_call" | custom-call | flops 1024 | bytes 1024 | tf_op jit(solution)/shard_map/pallas_call | solution.py:331
  155.2 0.9 shard_map.92
  (18 shorter events, 0.0 us)
Async XLA Ops:
  0.6 10.4 %copy-start.8 = (s32[32]{0:T(128)S(1)}, s32[32]{0:T(128)}, u32[]{:S(2)}) copy-start(s32[32]{0:T(128)} %param.9) | copy-start | bytes 388
  2.5 18.3 %all-to-all-start = ((bf16[32,8,896]{2,1,0:T(8,128)(2,1)}), bf16[32,8,896]{2,1,0:T(8,128)(2,1)S(1)}, u32[]{:S(2)}, u32[]{:S(2)}) async-start(bf16[32,8,896]{2,1,0:T(8,128)(2,1)} %bitcast.32), calls=%async_computation | async-start | bytes 917504 | tf_op jit(solution)/shard_map/all_to_all | solution.py:378
  20.8 3.0 %copy-start = (bf16[32,8,896]{2,1,0:T(8,128)(2,1)}, bf16[32,8,896]{2,1,0:T(8,128)(2,1)S(1)}, u32[]{:S(2)}) copy-start(bf16[32,8,896]{2,1,0:T(8,128)(2,1)S(1)} %all-to-all-done) | copy-start | bytes 1376260
  20.9 2.9 %copy-start.3 = (f32[256,128]{1,0:T(8,128)}, f32[256,128]{1,0:T(8,128)S(1)}, u32[]{:S(2)}) copy-start(f32[256,128]{1,0:T(8,128)S(1)} %broadcast_in_dim.44.held_ref) | copy-start | bytes 393220
  23.8 27.2 %all-to-all-start.1 = ((bf16[32,64,384]{2,1,0:T(8,128)(2,1)}), bf16[32,64,384]{2,1,0:T(8,128)(2,1)S(1)}, u32[]{:S(2)}, u32[]{:S(2)}) async-start(bf16[32,64,384]{2,1,0:T(8,128)(2,1)} %bitcast.4), calls=%async_computation.1 | async-start | bytes 3145728 | tf_op jit(solution)/shard_map/all_to_all | solution.py:378
  34.5 0.8 copy-start.1
  35.3 16.9 %copy-start.2 = (s32[8,1024]{1,0:T(8,128)S(1)}, s32[8,1024]{1,0:T(8,128)}, u32[]{:S(2)}) copy-start(s32[8,1024]{1,0:T(8,128)} %get-tuple-element.47.col_ref) | copy-start | bytes 98308
  51.0 1.1 copy-start.7
  65.7 13.7 %all-to-all-start.2 = ((f32[32,16,128]{2,1,0:T(8,128)}), f32[32,16,128]{2,1,0:T(8,128)S(1)}, u32[]{:S(2)}, u32[]{:S(2)}) async-start(f32[32,16,128]{2,1,0:T(8,128)} %get-tuple-element.48.stat_ref), calls=%async_computation.2 | async-start | bytes 524288 | tf_op jit(solution)/shard_map/all_to_all | solution.py:378
  81.5 8.1 %copy-start.4 = (f32[8,128]{1,0:T(8,128)S(1)}, f32[8,128]{1,0:T(8,128)}, u32[]{:S(2)}) copy-start(f32[8,128]{1,0:T(8,128)} %get-tuple-element.65.col_ref) | copy-start | bytes 12292
  86.3 32.1 %collective-permute-start = (bf16[512,768]{1,0:T(8,128)(2,1)}, bf16[512,768]{1,0:T(8,128)(2,1)}, u32[]{:S(2)}, u32[]{:S(2)}) collective-permute-start(bf16[512,768]{1,0:T(8,128)(2,1)} %get-tuple-element.74), channel_id=1, source_target_pairs={{0,32},{32,64},{64,96},{96,0},{1,33},{33,65},{65,97},{97,1},{2,34}... | collective-permute-start | bytes 2359304 | tf_op jit(solution)/shard_map/ppermute | solution.py:526
  87.9 30.5 %collective-permute-start.1 = (bf16[512,768]{1,0:T(8,128)(2,1)}, bf16[512,768]{1,0:T(8,128)(2,1)}, u32[]{:S(2)}, u32[]{:S(2)}) collective-permute-start(bf16[512,768]{1,0:T(8,128)(2,1)} %get-tuple-element.75), channel_id=1, source_target_pairs={{0,96},{32,0},{64,32},{96,64},{1,97},{33,1},{65,33},{97,65},{2,98}... | collective-permute-start | bytes 2359304 | tf_op jit(solution)/shard_map/ppermute | solution.py:527
  100.2 29.6 %all-to-all-start.3 = ((bf16[32,64,384]{2,1,0:T(8,128)(2,1)}), bf16[32,64,384]{2,1,0:T(8,128)(2,1)S(1)}, u32[]{:S(2)}, u32[]{:S(2)}) async-start(bf16[32,64,384]{2,1,0:T(8,128)(2,1)} %bitcast.29), calls=%async_computation.3 | async-start | bytes 3145728 | tf_op jit(solution)/shard_map/all_to_all | solution.py:378
  112.5 28.2 %collective-permute-start.2 = (bf16[512,768]{1,0:T(8,128)(2,1)}, bf16[512,768]{1,0:T(8,128)(2,1)}, u32[]{:S(2)}, u32[]{:S(2)}) collective-permute-start(bf16[512,768]{1,0:T(8,128)(2,1)} %get-tuple-element.81), channel_id=1, source_target_pairs={{0,96},{32,0},{64,32},{96,64},{1,97},{33,1},{65,33},{97,65},{2,98}... | collective-permute-start | bytes 2359304 | tf_op jit(solution)/shard_map/ppermute | solution.py:561
  114.3 26.4 %collective-permute-start.3 = (bf16[512,768]{1,0:T(8,128)(2,1)}, bf16[512,768]{1,0:T(8,128)(2,1)}, u32[]{:S(2)}, u32[]{:S(2)}) collective-permute-start(bf16[512,768]{1,0:T(8,128)(2,1)} %get-tuple-element.82), channel_id=1, source_target_pairs={{0,32},{32,64},{64,96},{96,0},{1,33},{33,65},{65,97},{97,1},{2,34}... | collective-permute-start | bytes 2359304 | tf_op jit(solution)/shard_map/ppermute | solution.py:560
  121.2 30.8 %collective-permute-start.4 = (bf16[512,768]{1,0:T(8,128)(2,1)}, bf16[512,768]{1,0:T(8,128)(2,1)}, u32[]{:S(2)}, u32[]{:S(2)}) collective-permute-start(bf16[512,768]{1,0:T(8,128)(2,1)} %get-tuple-element.83), channel_id=1, source_target_pairs={{0,32},{32,64},{64,96},{96,0},{1,33},{33,65},{65,97},{97,1},{2,34}... | collective-permute-start | bytes 2359304 | tf_op jit(solution)/shard_map/ppermute | solution.py:576
  121.5 30.5 %collective-permute-start.5 = (bf16[512,768]{1,0:T(8,128)(2,1)}, bf16[512,768]{1,0:T(8,128)(2,1)}, u32[]{:S(2)}, u32[]{:S(2)}) collective-permute-start(bf16[512,768]{1,0:T(8,128)(2,1)} %get-tuple-element.84), channel_id=1, source_target_pairs={{0,96},{32,0},{64,32},{96,64},{1,97},{33,1},{65,33},{97,65},{2,98}... | collective-permute-start | bytes 2359304 | tf_op jit(solution)/shard_map/ppermute | solution.py:577
  133.4 21.8 %all-to-all-start.4 = ((bf16[32,8,768]{2,1,0:T(8,128)(2,1)}), bf16[32,8,768]{2,1,0:T(8,128)(2,1)S(1)}, u32[]{:S(2)}, u32[]{:S(2)}) async-start(bf16[32,8,768]{2,1,0:T(8,128)(2,1)} %shard_map.85), calls=%async_computation.4 | async-start | bytes 786432 | tf_op jit(solution)/shard_map/all_to_all | solution.py:378
  140.8 1.4 copy-start.5
  142.2 1.4 copy-start.6

commit v4 on v2

--- a/solution.py
+++ b/solution.py
@@ -140,7 +140,7 @@
         out = jnp.where(row == s, lanes[:, s * ROWS : (s + 1) * ROWS], out)
     return out
 
-def scores_kernel(got_ref, col_ref, w_ref, r_ref, p_ref, q_ref, top_ref, stat_ref, row_ref, s_ref, high, total, found):
+def scores_kernel(got_ref, col_ref, w_ref, p_ref, q_ref, top_ref, stat_ref, row_ref, s_ref, high, total, found):
     step = pl.program_id(0)
     rows = s_ref.shape[1]
 
@@ -153,44 +153,37 @@
                     q_ref[here, h * HALF : (h + 1) * HALF] = got_ref[g, h, s]
         high[...] = jnp.full_like(high, NEG)
         total[...] = jnp.zeros_like(total)
+        found[...] = jnp.zeros_like(found)
 
     n = BIG_TILE // PART_TILE
-    top, tot = high[...], total[...]
+    top, tot, pick = high[...], total[...], found[...]
     for k in range(n + 1):
         if k < n:
             here = slice(k * PART_TILE, (k + 1) * PART_TILE)
             s_ref[here, :] = dot(w_ref[here, :], q_ref[...], ((1,), (1,)))
         if k > 0:
             here = slice((k - 1) * PART_TILE, k * PART_TILE)
-            s = s_ref[here, :].reshape(PART_TILE // 8, 8, rows)
-            best = jnp.max(jnp.max(s, axis=0), axis=0, keepdims=True)
+            s = s_ref[here, :]
+            target = iota(s.shape, 0) + (step * BIG_TILE + (k - 1) * PART_TILE) == col_ref[0:1, :]
+            pick += jnp.sum(jnp.where(target, s, 0.0).reshape(PART_TILE // 8, 8, rows), axis=0)
+            best = jnp.max(jnp.max(s.reshape(PART_TILE // 8, 8, rows), axis=0), axis=0, keepdims=True)
             best = jnp.broadcast_to(best, (8, rows))
-            e = jnp.exp(s - best[None])
-            target = label_iota(rows) == (col_ref[...] - (step * BIG_TILE + (k - 1) * PART_TILE))[None]
-            p_ref[here, :] = jnp.where(target, 0.0, e).reshape(PART_TILE, rows).astype(BF16)
+            e = jnp.exp(s - best[0:1, :])
+            p_ref[here, :] = jnp.where(target, 0.0, e).astype(BF16)
             new = jnp.maximum(top, best)
-            tot = tot * jnp.exp(top - new) + jnp.sum(e, axis=0) * jnp.exp(best - new)
+            add = jnp.sum(e.reshape(PART_TILE // 8, 8, rows), axis=0)
+            tot = tot * jnp.exp(top - new) + add * jnp.exp(best - new)
             top = new
             top_ref[k - 1] = best
-    high[...], total[...] = top, tot
-
-    two = 2 * ROWS
-    mine = q_ref[pl.ds(pl.multiple_of(step * two, two), two), :].astype(F32) * r_ref[...].astype(F32)
-    folded = mine[:, :ROWS]
-    for c in range(1, FEAT // ROWS):
-        folded += mine[:, c * ROWS : (c + 1) * ROWS]
-    for i in range(2):
-        one = jnp.sum(folded[i * ROWS : (i + 1) * ROWS].T, axis=0, keepdims=True)
-        found[step, i : i + 1, :] = one
+    high[...], total[...], found[...] = top, tot, pick
 
     @pl.when(step == pl.num_programs(0) - 1)
     def _():
         lse = top[0:1, :] + jnp.log(jnp.sum(tot, axis=0, keepdims=True))
         row_ref[...] = jnp.broadcast_to(lse, (8, rows))
+        chosen = jnp.sum(pick, axis=0, keepdims=True)
         stat_ref[:, :SLOTS, :] = jnp.broadcast_to(by_slot(lse)[None], (NDEV, SLOTS, ROWS))
-        for i in range(SLOTS // 2):
-            here = slice(SLOTS + 2 * i, SLOTS + 2 * i + 2)
-            stat_ref[:, here, :] = jnp.broadcast_to(found[i][None], (NDEV, 2, ROWS))
+        stat_ref[:, SLOTS:, :] = jnp.broadcast_to(by_slot(chosen)[None], (NDEV, SLOTS, ROWS))
 
 
 def normal_kernel(stat_ref, mask_ref, norm_ref, rest_ref, slots_ref, loss_ref):
@@ -265,14 +258,14 @@
             out_ref[:, h, s * 8 : (s + 1) * 8, :] = part[:, :, h * HALF : (h + 1) * HALF]
 
 
-def table_grad_kernel(base, tiles_ref, q_ref, top_ref, norm_ref, rest_ref, col_ref, *refs):
-    n = len(refs) // 2
+def table_grad_kernel(base, tiles_ref, q_ref, norm_ref, rest_ref, col_ref, *refs):
+    n = len(refs) // 3
     for i in range(n):
-        p_ref, out_ref = refs[i], refs[n + i]
+        p_ref, top_ref, out_ref = refs[i], refs[n + i], refs[2 * n + i]
         tile = tiles_ref[base + i]
         for k in range(TILE // PART_TILE):
             here = slice(k * PART_TILE, (k + 1) * PART_TILE)
-            scale = jnp.exp(top_ref[tile * (TILE // PART_TILE) + k] - norm_ref[...])
+            scale = jnp.exp(top_ref[k] - norm_ref[...])
             rows = scale.shape[1]
             p = p_ref[here, :].astype(F32).reshape(PART_TILE // 8, 8, rows)
             target = label_iota(rows) == (col_ref[...] - (tile * TILE + k * PART_TILE))[None]
@@ -427,7 +420,7 @@
     p, q, tops, stats, lse_row = stepped(
         scores_kernel,
         steps,
-        [fixed((16, 2, SLOTS, 8, HALF)), fixed((8, rows)), w_spec, tiled((2 * ROWS, FEAT))],
+        [fixed((16, 2, SLOTS, 8, HALF)), fixed((8, rows)), w_spec],
         (
             pltpu.HBM((LABELS, rows), BF16),
             shape((rows, FEAT), BF16),
@@ -446,12 +439,11 @@
             pltpu.VMEM((BIG_TILE, rows), F32),
             pltpu.VMEM((8, rows), F32),
             pltpu.VMEM((8, rows), F32),
-            pltpu.VMEM((SLOTS // 2, 2, ROWS), F32),
+            pltpu.VMEM((8, rows), F32),
         ),
         pltpu.with_memory_space_constraint(arrived.reshape(16, 2, SLOTS, 8, HALF), pltpu.HBM),
         col,
         ranker,
-        positive_rows,
     )
     all_stats = swap(stats)
     p = pltpu.with_memory_space_constraint(p, pltpu.HBM)
@@ -490,22 +482,25 @@
             1,
             [
                 fixed((rows, FEAT)),
-                fixed((LABELS // PART_TILE, 8, rows)),
                 fixed((8, rows)),
                 fixed((8, rows)),
                 fixed((8, rows)),
                 *(pl.BlockSpec((TILE, rows), lambda _, t, i=i: (t[first + i], 0)) for i in range(n)),
+                *(
+                    pl.BlockSpec((TILE // PART_TILE, 8, rows), lambda _, t, i=i: (t[first + i], 0, 0))
+                    for i in range(n)
+                ),
             ],
             tuple(place((TILE, FEAT), d) for d in dtypes),
             tuple(fixed((TILE, FEAT)) for _ in dtypes),
             (),
             tiles,
             q,
-            tops,
             norm,
             rest,
             col,
             *([p] * n),
+            *([tops] * n),
             scalars=1,
         )
 

time: 156 us -> 154 us (0.987)
  Pallas kernels: 83.1 us -> 80.7 us
    pallas_call x7, Pallas kernels: 57.6 us -> 55.2 us  [stepped(): pl.pallas_call(kernel, grid_spec=spec, out_shape=outs, compiler_params=pl...]
  transfers between devices with their start and end apart: 11 -> 11, of which waited for: 3 -> 3; matrix products, arithmetic and copies ran while one was open for 1% -> 1% of each run, Pallas kernels for 35% -> 36%
where the time goes in v4:
time: 154 us; the launch traced here: 153 us
  Pallas kernels  80.7 us (52%)
  starting transfers between devices  43.2 us (28%)
  waiting for transfers between devices  21.8 us (14%)
  local copies, waits for them, and re-layouts  4.53 us (3%)
    pallas_call x7, Pallas kernels, stepped(): pl.pallas_call(kernel, grid_spec=spec, out_shape=outs, compiler_params=pl...  55.2 us
    all_to_all x5, starting transfers between devices, swap(): return lax.all_to_all(x, 'label', split_axis=0, concat_axis=0, tiled=True)  34.7 us
    pallas_call x10, Pallas kernels, whole(): pl.pallas_call(kernel, out_shape=outs, in_specs=[place(i, hbm, smem) for...  25.5 us
    all_to_all x5, waiting for transfers between devices, swap(): return lax.all_to_all(x, 'label', split_axis=0, concat_axis=0, tiled=True)  15 us
    ppermute x1, waiting for transfers between devices, per_device(): from_prev_a = lax.ppermute(relay_up, 'dp', up)  6.76 us
    unnamed x18, local copies, waits for them, and re-layouts  3.59 us
  transfers between devices with their start and end apart: 11, of which 3 were waited for; matrix products, arithmetic and copies ran while one was open for 1% of the time, Pallas kernels for 36%

profile of v4, /device:TPU:2, one launch (start us, length us, event | category | flops | bytes accessed | tf_op | source)
XLA Modules:
  0.0 152.5 jit_solution(694902404611394032)
XLA Ops:
  0.6 1.9 %shard_map.76 = bf16[16,2,8,896]{3,2,1,0:T(8,128)(2,1)} custom-call(bf16[2,16,8,768]{3,2,1,0:T(8,128)(2,1)} %bitcast.32, s32[2,128]{1,0:T(2,128)} %bitcast.33, s32[2,4]{1,0:T(2,128)} %beam_hbm.1), custom_call_target="tpu_custom_call" | custom-call | flops 1024 | bytes 1024 | tf_op jit(solution)/shard_map/pallas_call | solution.py:319
  2.5 8.5 %all-to-all-start = ((bf16[32,8,896]{2,1,0:T(8,128)(2,1)}), bf16[32,8,896]{2,1,0:T(8,128)(2,1)S(1)}, u32[]{:S(2)}, u32[]{:S(2)}) async-start(bf16[32,8,896]{2,1,0:T(8,128)(2,1)} %bitcast.30), calls=%async_computation | async-start | bytes 917504 | tf_op jit(solution)/shard_map/all_to_all | solution.py:366
  11.0 0.1 select_reduce_fusion
  11.1 0.1 broadcast_in_dim.42
  11.2 0.1 broadcast_in_dim.43
  11.3 9.5 %all-to-all-done = bf16[32,8,896]{2,1,0:T(8,128)(2,1)S(1)} async-done(((bf16[32,8,896]{2,1,0:T(8,128)(2,1)}), bf16[32,8,896]{2,1,0:T(8,128)(2,1)S(1)}, u32[]{:S(2)}, u32[]{:S(2)}) %all-to-all-start) | async-done | bytes 458784 | tf_op jit(solution)/shard_map/all_to_all | solution.py:366
  20.8 0.1 broadcast_in_dim.44.held_ref
  20.9 2.9 %shard_map.77 = bf16[2048,384]{1,0:T(8,128)(2,1)} custom-call(bf16[256,896]{1,0:T(8,128)(2,1)S(1)} %bitcast.22, f32[256,128]{1,0:T(8,128)S(1)} %broadcast_in_dim.44.held_ref), custom_call_target="tpu_custom_call" | custom-call | flops 1024 | bytes 1024 | tf_op jit(solution)/shard_map/pallas_call | solution.py:319
  23.8 5.7 %all-to-all-start.1 = ((bf16[32,64,384]{2,1,0:T(8,128)(2,1)}), bf16[32,64,384]{2,1,0:T(8,128)(2,1)}, u32[]{:S(2)}, u32[]{:S(2)}) async-start(bf16[32,64,384]{2,1,0:T(8,128)(2,1)} %bitcast.4), calls=%async_computation.1 | async-start | bytes 3145728 | tf_op jit(solution)/shard_map/all_to_all | solution.py:366
  29.6 0.6 fusion
  30.9 0.6 iota.17.mine_ref
  31.5 3.7 %shard_map.78 = (bf16[512,2048]{1,0:T(8,128)(2,1)}, f32[256,128]{1,0:T(8,128)}, s32[8,1024]{1,0:T(8,128)}, f32[8,128]{1,0:T(8,128)}) custom-call(bf16[256,896]{1,0:T(8,128)(2,1)} %bitcast.23, f32[256,128]{1,0:T(8,128)} %copy-done.4, f32[16,128]{1,0:T(8,128)} %iota.17.mine_ref), custom_call_target="tpu_custom_call" | custom-call | flops 1024 | bytes 1024 | tf_op jit(solution)/shard_map/pallas_call | solution.py:319
  35.2 0.8 copy-done.2
  35.9 10.4 %shard_map.79.r_ref = bf16[1024,768]{1,0:T(8,128)(2,1)S(1)} custom-call(s32[8,1024]{1,0:T(8,128)S(1)} %copy-done.2, bf16[4096,768]{1,0:T(8,128)(2,1)} %bitcast.25), custom_call_target="tpu_custom_call" | custom-call | flops 1024 | bytes 1024 | tf_op jit(solution)/shard_map/pallas_call | solution.py:346
  46.3 5.5 %all-to-all-done.1 = bf16[32,64,384]{2,1,0:T(8,128)(2,1)} async-done(((bf16[32,64,384]{2,1,0:T(8,128)(2,1)}), bf16[32,64,384]{2,1,0:T(8,128)(2,1)}, u32[]{:S(2)}, u32[]{:S(2)}) %all-to-all-start.1) | async-done | bytes 1572896 | tf_op jit(solution)/shard_map/all_to_all | solution.py:366
  51.8 13.6 %shard_map.80 = (bf16[4096,1024]{1,0:T(8,128)(2,1)}, bf16[1024,768]{1,0:T(8,128)(2,1)S(1)}, f32[16,8,1024]{2,1,0:T(8,128)}, f32[32,16,128]{2,1,0:T(8,128)}, f32[8,1024]{1,0:T(8,128)S(1)}) custom-call(bf16[16,2,8,8,384]{4,3,2,1,0:T(8,128)(2,1)} %bitcast.6.got_ref, s32[8,1024]{1,0:T(8,128)S(1)} %copy-done.3, bf16[4096,768]{1,0:T(8,128)(2,1)} %bitcast.26), custom_call_target="tpu_custom_call" | custom-call | flops 1024 | bytes 1024 | tf_op jit(solution)/shard_map/pallas_call | solution.py:346
  65.4 5.7 %all-to-all-start.2 = ((f32[32,16,128]{2,1,0:T(8,128)}), f32[32,16,128]{2,1,0:T(8,128)S(1)}, u32[]{:S(2)}, u32[]{:S(2)}) async-start(f32[32,16,128]{2,1,0:T(8,128)} %get-tuple-element.48.stat_ref), calls=%async_computation.2 | async-start | bytes 524288 | tf_op jit(solution)/shard_map/all_to_all | solution.py:366
  71.1 0.1 stack.35.tiles_ref
  71.2 12.2 %shard_map.81.u_ref = bf16[1024,768]{1,0:T(8,128)(2,1)} custom-call(f32[16,8,1024]{2,1,0:T(8,128)} %get-tuple-element.49.top_ref.refs_2_.refs_3_, f32[8,1024]{1,0:T(8,128)S(1)} %get-tuple-element.50.row_ref, bf16[4096,768]{1,0:T(8,128)(2,1)} %bitcast.27, bf16[4096,1024]{1,0:T(8,128)(2,1)} %get-tuple-element.51.p_ref.refs_0_.refs_1_), custom_call_target="tpu_custom_call" | custom-call | flops 1024 | bytes 1024 | tf_op jit(solution)/shard_map/pallas_call | solution.py:346
  83.4 0.0 all-to-all-done.2.stat_ref
  83.4 2.1 %shard_map.82 = (f32[8,1024]{1,0:T(8,128)S(1)}, f32[8,1024]{1,0:T(8,128)S(1)}, f32[8,128]{1,0:T(8,128)S(1)}, f32[2,128]{1,0:T(2,128)}) custom-call(f32[32,16,128]{2,1,0:T(8,128)S(1)} %all-to-all-done.2.stat_ref, f32[256,128]{1,0:T(8,128)} %get-tuple-element.53.mask_ref), custom_call_target="tpu_custom_call" | custom-call | flops 1024 | bytes 1024 | tf_op jit(solution)/shard_map/pallas_call | solution.py:319
  85.5 4.9 %shard_map.83 = (bf16[512,768]{1,0:T(8,128)(2,1)}, bf16[512,768]{1,0:T(8,128)(2,1)}) custom-call(s32[8]{0:T(128)S(1)} %stack.35.tiles_ref, bf16[1024,768]{1,0:T(8,128)(2,1)S(1)} %get-tuple-element.58.q_ref, f32[8,1024]{1,0:T(8,128)S(1)} %get-tuple-element.78.norm_ref, f32[8,1024]{1,0:T(8,128)S(1)} %get-tuple-element.60.rest_ref, s32[8,1024]{1,0:T(8,128)S(1)} %copy-done.3, ...), custom_call_target="tpu_custom_call" | custom-call | flops 1024 | bytes 1024 | tf_op jit(solution)/shard_map/pallas_call | solution.py:346
  90.4 1.6 %collective-permute-start = (bf16[512,768]{1,0:T(8,128)(2,1)}, bf16[512,768]{1,0:T(8,128)(2,1)}, u32[]{:S(2)}, u32[]{:S(2)}) collective-permute-start(bf16[512,768]{1,0:T(8,128)(2,1)} %get-tuple-element.74), channel_id=1, source_target_pairs={{0,32},{32,64},{64,96},{96,0},{1,33},{33,65},{65,97},{97,1},{2,34}... | collective-permute-start | bytes 2359304 | tf_op jit(solution)/shard_map/ppermute | solution.py:509
  92.0 1.7 %collective-permute-start.1 = (bf16[512,768]{1,0:T(8,128)(2,1)}, bf16[512,768]{1,0:T(8,128)(2,1)}, u32[]{:S(2)}, u32[]{:S(2)}) collective-permute-start(bf16[512,768]{1,0:T(8,128)(2,1)} %get-tuple-element.75), channel_id=1, source_target_pairs={{0,96},{32,0},{64,32},{96,64},{1,97},{33,1},{65,33},{97,65},{2,98}... | collective-permute-start | bytes 2359304 | tf_op jit(solution)/shard_map/ppermute | solution.py:510
  93.6 3.0 %shard_map.84 = bf16[16,2,64,384]{3,2,1,0:T(8,128)(2,1)} custom-call(bf16[1024,768]{1,0:T(8,128)(2,1)S(1)} %copy-done, bf16[1024,768]{1,0:T(8,128)(2,1)S(1)} %shard_map.79.r_ref, f32[32,16,128]{2,1,0:T(8,128)} %get-tuple-element.48.stat_ref, f32[8,128]{1,0:T(8,128)S(1)} %get-tuple-element.64.norm_ref, f32[8,128]{1,0:T(8,128)S(1)} %copy-done.5), custom_call_target="tpu_custom_call" | custom-call | flops 1024 | bytes 1024 | tf_op jit(solution)/shard_map/pallas_call | solution.py:319
  96.6 7.5 %all-to-all-start.3 = ((bf16[32,64,384]{2,1,0:T(8,128)(2,1)}), bf16[32,64,384]{2,1,0:T(8,128)(2,1)S(1)}, u32[]{:S(2)}, u32[]{:S(2)}) async-start(bf16[32,64,384]{2,1,0:T(8,128)(2,1)} %bitcast.28), calls=%async_computation.3 | async-start | bytes 3145728 | tf_op jit(solution)/shard_map/all_to_all | solution.py:366
  104.1 4.8 %shard_map.86 = (bf16[512,768]{1,0:T(8,128)(2,1)}, bf16[512,768]{1,0:T(8,128)(2,1)}) custom-call(s32[8]{0:T(128)S(1)} %stack.35.tiles_ref, bf16[1024,768]{1,0:T(8,128)(2,1)S(1)} %get-tuple-element.58.q_ref, f32[8,1024]{1,0:T(8,128)S(1)} %get-tuple-element.78.norm_ref, f32[8,1024]{1,0:T(8,128)S(1)} %get-tuple-element.60.rest_ref, s32[8,1024]{1,0:T(8,128)S(1)} %copy-done.3, ...), custom_call_target="tpu_custom_call" | custom-call | flops 1024 | bytes 1024 | tf_op jit(solution)/shard_map/pallas_call | solution.py:346
  108.9 1.8 %collective-permute-start.2 = (bf16[512,768]{1,0:T(8,128)(2,1)}, bf16[512,768]{1,0:T(8,128)(2,1)}, u32[]{:S(2)}, u32[]{:S(2)}) collective-permute-start(bf16[512,768]{1,0:T(8,128)(2,1)} %get-tuple-element.81), channel_id=1, source_target_pairs={{0,96},{32,0},{64,32},{96,64},{1,97},{33,1},{65,33},{97,65},{2,98}... | collective-permute-start | bytes 2359304 | tf_op jit(solution)/shard_map/ppermute | solution.py:526
  110.7 0.2 collective-permute-start.3
  110.9 3.9 %shard_map.87 = (f32[512,768]{1,0:T(8,128)S(1)}, f32[512,768]{1,0:T(8,128)S(1)}) custom-call(s32[8]{0:T(128)S(1)} %stack.35.tiles_ref, bf16[1024,768]{1,0:T(8,128)(2,1)S(1)} %get-tuple-element.58.q_ref, f32[8,1024]{1,0:T(8,128)S(1)} %get-tuple-element.78.norm_ref, f32[8,1024]{1,0:T(8,128)S(1)} %get-tuple-element.60.rest_ref, s32[8,1024]{1,0:T(8,128)S(1)} %copy-done.3, ...), custom_call_target="tpu_custom_call" | custom-call | flops 1024 | bytes 1024 | tf_op jit(solution)/shard_map/pallas_call | solution.py:346
  114.8 0.0 collective-permute-done.got_up_ref
  114.8 0.0 collective-permute-done.1.got_down_ref
  114.9 2.7 %shard_map.88 = (bf16[512,768]{1,0:T(8,128)(2,1)}, bf16[512,768]{1,0:T(8,128)(2,1)}) custom-call(f32[512,768]{1,0:T(8,128)S(1)} %get-tuple-element.72.up_ref, f32[512,768]{1,0:T(8,128)S(1)} %get-tuple-element.73.down_ref, bf16[512,768]{1,0:T(8,128)(2,1)} %collective-permute-done.got_up_ref, bf16[512,768]{1,0:T(8,128)(2,1)} %collective-permute-done.1.got_down_ref), custom_call_target="tpu_custom_call" | custom-call | flops 49999998976 | bytes 1024 | tf_op jit(solution)/shard_map/pallas_call | solution.py:319
  117.6 0.4 collective-permute-start.4
  117.9 2.9 %collective-permute-start.5 = (bf16[512,768]{1,0:T(8,128)(2,1)}, bf16[512,768]{1,0:T(8,128)(2,1)}, u32[]{:S(2)}, u32[]{:S(2)}) collective-permute-start(bf16[512,768]{1,0:T(8,128)(2,1)} %get-tuple-element.84), channel_id=1, source_target_pairs={{0,96},{32,0},{64,32},{96,64},{1,97},{33,1},{65,33},{97,65},{2,98}... | collective-permute-start | bytes 2359304 | tf_op jit(solution)/shard_map/ppermute | solution.py:542
  120.8 5.4 %shard_map.89 = (f32[512,768]{1,0:T(8,128)}, f32[512,768]{1,0:T(8,128)}) custom-call(s32[8]{0:T(128)S(1)} %stack.35.tiles_ref, bf16[1024,768]{1,0:T(8,128)(2,1)S(1)} %get-tuple-element.58.q_ref, f32[8,1024]{1,0:T(8,128)S(1)} %get-tuple-element.78.norm_ref, f32[8,1024]{1,0:T(8,128)S(1)} %get-tuple-element.60.rest_ref, s32[8,1024]{1,0:T(8,128)S(1)} %copy-done.3, ...), custom_call_target="tpu_custom_call" | custom-call | flops 1024 | bytes 1024 | tf_op jit(solution)/shard_map/pallas_call | solution.py:346
  126.2 0.0 all-to-all-done.3
  126.2 3.6 %shard_map.85 = bf16[32,8,768]{2,1,0:T(8,128)(2,1)} custom-call(bf16[512,2048]{1,0:T(8,128)(2,1)} %get-tuple-element.55.sel_ref, bf16[2048,384]{1,0:T(8,128)(2,1)S(1)} %bitcast.21), custom_call_target="tpu_custom_call" | custom-call | flops 1024 | bytes 1024 | tf_op jit(solution)/shard_map/pallas_call | solution.py:319
  129.8 7.4 %all-to-all-start.4 = ((bf16[32,8,768]{2,1,0:T(8,128)(2,1)}), bf16[32,8,768]{2,1,0:T(8,128)(2,1)S(1)}, u32[]{:S(2)}, u32[]{:S(2)}) async-start(bf16[32,8,768]{2,1,0:T(8,128)(2,1)} %shard_map.85), calls=%async_computation.4 | async-start | bytes 786432 | tf_op jit(solution)/shard_map/all_to_all | solution.py:366
  137.2 0.0 collective-permute-done.2.a_ref
  137.2 0.0 collective-permute-done.3.b_ref
  137.2 1.4 copy-done.6
  138.6 1.4 copy-done.7
  140.0 1.6 %shard_map.90.base_ref = f32[1024,768]{1,0:T(8,128)S(1)} custom-call(f32[512,768]{1,0:T(8,128)S(1)} %copy-done.6, f32[512,768]{1,0:T(8,128)S(1)} %copy-done.7, bf16[512,768]{1,0:T(8,128)(2,1)} %collective-permute-done.2.a_ref, bf16[512,768]{1,0:T(8,128)(2,1)} %collective-permute-done.3.b_ref), custom_call_target="tpu_custom_call" | custom-call | flops 8000000000 | bytes 1024 | tf_op jit(solution)/shard_map/pallas_call | solution.py:319
  141.6 6.8 %collective-permute-done.4.a_ref = bf16[512,768]{1,0:T(8,128)(2,1)} collective-permute-done((bf16[512,768]{1,0:T(8,128)(2,1)}, bf16[512,768]{1,0:T(8,128)(2,1)}, u32[]{:S(2)}, u32[]{:S(2)}) %collective-permute-start.4) | collective-permute-done | bytes 786464 | tf_op jit(solution)/shard_map/ppermute | solution.py:541
  148.4 0.0 collective-permute-done.5.b_ref
  148.4 3.2 %shard_map.91 = f32[1024,768]{1,0:T(8,128)} custom-call(f32[1024,768]{1,0:T(8,128)S(1)} %shard_map.90.base_ref, bf16[512,768]{1,0:T(8,128)(2,1)} %collective-permute-done.4.a_ref, bf16[512,768]{1,0:T(8,128)(2,1)} %collective-permute-done.5.b_ref), custom_call_target="tpu_custom_call" | custom-call | flops 1024 | bytes 1024 | tf_op jit(solution)/shard_map/pallas_call | solution.py:319
  151.6 0.9 shard_map.92
  (18 shorter events, 0.0 us)
Async XLA Ops:
  0.6 10.4 %copy-start.8 = (s32[32]{0:T(128)S(1)}, s32[32]{0:T(128)}, u32[]{:S(2)}) copy-start(s32[32]{0:T(128)} %param.9) | copy-start | bytes 388
  2.5 18.3 %all-to-all-start = ((bf16[32,8,896]{2,1,0:T(8,128)(2,1)}), bf16[32,8,896]{2,1,0:T(8,128)(2,1)S(1)}, u32[]{:S(2)}, u32[]{:S(2)}) async-start(bf16[32,8,896]{2,1,0:T(8,128)(2,1)} %bitcast.30), calls=%async_computation | async-start | bytes 917504 | tf_op jit(solution)/shard_map/all_to_all | solution.py:366
  20.8 3.0 %copy-start.1 = (bf16[32,8,896]{2,1,0:T(8,128)(2,1)}, bf16[32,8,896]{2,1,0:T(8,128)(2,1)S(1)}, u32[]{:S(2)}) copy-start(bf16[32,8,896]{2,1,0:T(8,128)(2,1)S(1)} %all-to-all-done) | copy-start | bytes 1376260
  20.9 2.9 %copy-start.4 = (f32[256,128]{1,0:T(8,128)}, f32[256,128]{1,0:T(8,128)S(1)}, u32[]{:S(2)}) copy-start(f32[256,128]{1,0:T(8,128)S(1)} %broadcast_in_dim.44.held_ref) | copy-start | bytes 393220
  23.8 28.0 %all-to-all-start.1 = ((bf16[32,64,384]{2,1,0:T(8,128)(2,1)}), bf16[32,64,384]{2,1,0:T(8,128)(2,1)}, u32[]{:S(2)}, u32[]{:S(2)}) async-start(bf16[32,64,384]{2,1,0:T(8,128)(2,1)} %bitcast.4), calls=%async_computation.1 | async-start | bytes 3145728 | tf_op jit(solution)/shard_map/all_to_all | solution.py:366
  35.2 0.8 copy-start.2
  35.9 15.9 %copy-start.3 = (s32[8,1024]{1,0:T(8,128)S(1)}, s32[8,1024]{1,0:T(8,128)}, u32[]{:S(2)}) copy-start(s32[8,1024]{1,0:T(8,128)} %get-tuple-element.47.col_ref) | copy-start | bytes 98308
  65.4 18.0 %all-to-all-start.2 = ((f32[32,16,128]{2,1,0:T(8,128)}), f32[32,16,128]{2,1,0:T(8,128)S(1)}, u32[]{:S(2)}, u32[]{:S(2)}) async-start(f32[32,16,128]{2,1,0:T(8,128)} %get-tuple-element.48.stat_ref), calls=%async_computation.2 | async-start | bytes 524288 | tf_op jit(solution)/shard_map/all_to_all | solution.py:366
  85.5 8.1 %copy-start = (bf16[1024,768]{1,0:T(8,128)(2,1)S(1)}, bf16[1024,768]{1,0:T(8,128)(2,1)}, u32[]{:S(2)}) copy-start(bf16[1024,768]{1,0:T(8,128)(2,1)} %shard_map.81.u_ref) | copy-start | bytes 4718596
  85.5 8.1 %copy-start.5 = (f32[8,128]{1,0:T(8,128)S(1)}, f32[8,128]{1,0:T(8,128)}, u32[]{:S(2)}) copy-start(f32[8,128]{1,0:T(8,128)} %get-tuple-element.65.col_ref) | copy-start | bytes 12292
  90.4 24.4 %collective-permute-start = (bf16[512,768]{1,0:T(8,128)(2,1)}, bf16[512,768]{1,0:T(8,128)(2,1)}, u32[]{:S(2)}, u32[]{:S(2)}) collective-permute-start(bf16[512,768]{1,0:T(8,128)(2,1)} %get-tuple-element.74), channel_id=1, source_target_pairs={{0,32},{32,64},{64,96},{96,0},{1,33},{33,65},{65,97},{97,1},{2,34}... | collective-permute-start | bytes 2359304 | tf_op jit(solution)/shard_map/ppermute | solution.py:509
  92.0 22.9 %collective-permute-start.1 = (bf16[512,768]{1,0:T(8,128)(2,1)}, bf16[512,768]{1,0:T(8,128)(2,1)}, u32[]{:S(2)}, u32[]{:S(2)}) collective-permute-start(bf16[512,768]{1,0:T(8,128)(2,1)} %get-tuple-element.75), channel_id=1, source_target_pairs={{0,96},{32,0},{64,32},{96,64},{1,97},{33,1},{65,33},{97,65},{2,98}... | collective-permute-start | bytes 2359304 | tf_op jit(solution)/shard_map/ppermute | solution.py:510
  96.6 29.6 %all-to-all-start.3 = ((bf16[32,64,384]{2,1,0:T(8,128)(2,1)}), bf16[32,64,384]{2,1,0:T(8,128)(2,1)S(1)}, u32[]{:S(2)}, u32[]{:S(2)}) async-start(bf16[32,64,384]{2,1,0:T(8,128)(2,1)} %bitcast.28), calls=%async_computation.3 | async-start | bytes 3145728 | tf_op jit(solution)/shard_map/all_to_all | solution.py:366
  108.9 28.3 %collective-permute-start.2 = (bf16[512,768]{1,0:T(8,128)(2,1)}, bf16[512,768]{1,0:T(8,128)(2,1)}, u32[]{:S(2)}, u32[]{:S(2)}) collective-permute-start(bf16[512,768]{1,0:T(8,128)(2,1)} %get-tuple-element.81), channel_id=1, source_target_pairs={{0,96},{32,0},{64,32},{96,64},{1,97},{33,1},{65,33},{97,65},{2,98}... | collective-permute-start | bytes 2359304 | tf_op jit(solution)/shard_map/ppermute | solution.py:526
  110.7 26.5 %collective-permute-start.3 = (bf16[512,768]{1,0:T(8,128)(2,1)}, bf16[512,768]{1,0:T(8,128)(2,1)}, u32[]{:S(2)}, u32[]{:S(2)}) collective-permute-start(bf16[512,768]{1,0:T(8,128)(2,1)} %get-tuple-element.82), channel_id=1, source_target_pairs={{0,32},{32,64},{64,96},{96,0},{1,33},{33,65},{65,97},{97,1},{2,34}... | collective-permute-start | bytes 2359304 | tf_op jit(solution)/shard_map/ppermute | solution.py:525
  117.6 30.8 %collective-permute-start.4 = (bf16[512,768]{1,0:T(8,128)(2,1)}, bf16[512,768]{1,0:T(8,128)(2,1)}, u32[]{:S(2)}, u32[]{:S(2)}) collective-permute-start(bf16[512,768]{1,0:T(8,128)(2,1)} %get-tuple-element.83), channel_id=1, source_target_pairs={{0,32},{32,64},{64,96},{96,0},{1,33},{33,65},{65,97},{97,1},{2,34}... | collective-permute-start | bytes 2359304 | tf_op jit(solution)/shard_map/ppermute | solution.py:541
  117.9 30.5 %collective-permute-start.5 = (bf16[512,768]{1,0:T(8,128)(2,1)}, bf16[512,768]{1,0:T(8,128)(2,1)}, u32[]{:S(2)}, u32[]{:S(2)}) collective-permute-start(bf16[512,768]{1,0:T(8,128)(2,1)} %get-tuple-element.84), channel_id=1, source_target_pairs={{0,96},{32,0},{64,32},{96,64},{1,97},{33,1},{65,33},{97,65},{2,98}... | collective-permute-start | bytes 2359304 | tf_op jit(solution)/shard_map/ppermute | solution.py:542
  129.8 21.8 %all-to-all-start.4 = ((bf16[32,8,768]{2,1,0:T(8,128)(2,1)}), bf16[32,8,768]{2,1,0:T(8,128)(2,1)S(1)}, u32[]{:S(2)}, u32[]{:S(2)}) async-start(bf16[32,8,768]{2,1,0:T(8,128)(2,1)} %shard_map.85), calls=%async_computation.4 | async-start | bytes 786432 | tf_op jit(solution)/shard_map/all_to_all | solution.py:366
  137.2 1.4 copy-start.6
  138.6 1.4 copy-start.7

commit v5 on v4

--- a/solution.py
+++ b/solution.py
@@ -58,9 +58,9 @@
     got = got_ref[...]
     table = slot_table(got[:, FEAT:], held_ref[...][:, :1])
     m = piece_matrix(table)
-    out = dot(m[:, :256], got[:, :HALF], ((1,), (0,)))
-    out += dot(m[:, 256:], got[:, HALF:FEAT], ((1,), (0,)))
-    out_ref[...] = out.astype(BF16)
+    x = jnp.concatenate([got[:, :HALF], got[:, HALF:FEAT]], axis=0)
+    out_ref[...] = dot(m, x, ((1,), (0,))).astype(BF16)
+
 
 def table_kernel(got_ref, held_ref, mine_ref, sel_ref, mask_ref, col_ref, slots_ref):
     meta = got_ref[...][:, FEAT:]
@@ -279,11 +279,6 @@
     for b in range(2):
         out_ref[:, :, b * HALF : (b + 1) * HALF] = out[b * 256 : (b + 1) * 256].reshape(NDEV, 8, HALF)
 
-def home_kernel(got_ref, out_ref):
-    for h in range(2):
-        for b in range(2):
-            out_ref[b, :, :, h * HALF : (h + 1) * HALF] = got_ref[:, h, :, b * HALF : (b + 1) * HALF].astype(F32)
-
 def relay_kernel(up_ref, down_ref, got_up_ref, got_down_ref, out_up_ref, out_down_ref):
     out_up_ref[...] = (up_ref[...] + got_up_ref[...].astype(F32)).astype(BF16)
     out_down_ref[...] = (down_ref[...] + got_down_ref[...].astype(F32)).astype(BF16)
@@ -294,15 +289,34 @@
     out_ref[TILE:, :] = own_b_ref[...] + b_ref[...].astype(F32)
 
 
-def finish_kernel(base_ref, a_ref, b_ref, out_hbm, out_v, out_sems):
-    copies = []
-    for i, ref in enumerate((a_ref, b_ref)):
-        here = pl.ds(i * TILE, TILE)
-        out_v[i * TILE : (i + 1) * TILE, :] = base_ref[i * TILE : (i + 1) * TILE, :] + ref[...].astype(F32)
-        c = pltpu.make_async_copy(out_v.at[here], out_hbm.at[here], out_sems.at[i])
+def finish_kernel(base_ref, a_hbm, b_hbm, home_ref, out_hbm, grad_hbm, got, out_v, grad_v, in_sems, out_sems, grad_sem):
+    tile = PART_TILE
+    per = TILE // tile
+    copies = start(
+        [
+            pltpu.make_async_copy(
+                src.at[pl.ds(k * tile, tile)], got.at[pl.ds((i * per + k) * tile, tile)], in_sems.at[i * per + k]
+            )
+            for i, src in enumerate((a_hbm, b_hbm))
+            for k in range(per)
+        ]
+    )
+    for h in range(2):
+        for b in range(2):
+            piece = home_ref[:, h, :, b * HALF : (b + 1) * HALF].astype(F32)
+            grad_v[b, :, :, h * HALF : (h + 1) * HALF] = piece
+    grad = pltpu.make_async_copy(grad_v, grad_hbm, grad_sem)
+    grad.start()
+    out = []
+    for j in range(2 * per):
+        here = slice(j * tile, (j + 1) * tile)
+        copies[j].wait()
+        out_v[here, :] = base_ref[here, :] + got[here, :].astype(F32)
+        c = pltpu.make_async_copy(out_v.at[pl.ds(j * tile, tile)], out_hbm.at[pl.ds(j * tile, tile)], out_sems.at[j])
         c.start()
-        copies.append(c)
-    for c in copies:
+        out.append(c)
+    grad.wait()
+    for c in out:
         c.wait()
 
 
@@ -554,20 +568,26 @@
         limit=16,
         cost=8_000_000_000,
     )
-    grad_table = whole(
+    grad_table, grad_queries = whole(
         finish_kernel,
-        shape((2 * TILE, FEAT), F32),
+        (shape((2 * TILE, FEAT), F32), shape((2, 16, 8, FEAT), F32)),
         base,
         from_prev_a,
         from_next_b,
-        hbm_out=(0,),
+        home.reshape(16, 2, 8, FEAT),
+        hbm=(1, 2),
+        hbm_out=(0, 1),
         limit=16,
-        scratch=(pltpu.VMEM((2 * TILE, FEAT), F32), sems(2)),
-    )
-    home, grad_table = lax.optimization_barrier((home, grad_table))
-    grad_queries = whole(
-        home_kernel, shape((2, 16, 8, FEAT), F32), home.reshape(16, 2, 8, FEAT), limit=16
-    ).reshape(256, FEAT)
+        scratch=(
+            pltpu.VMEM((2 * TILE, FEAT), BF16),
+            pltpu.VMEM((2 * TILE, FEAT), F32),
+            pltpu.VMEM((2, 16, 8, FEAT), F32),
+            sems(4),
+            sems(4),
+            pltpu.SemaphoreType.DMA,
+        ),
+    )
+    grad_queries = grad_queries.reshape(256, FEAT)
     return loss.reshape(256), grad_queries, grad_table[None]
 
 def solution(mesh):

time: 154 us -> 153 us (level)
    pallas_call x10 -> x9, Pallas kernels: 25.5 us -> 24.4 us  [whole(): pl.pallas_call(kernel, out_shape=outs, in_specs=[place(i, hbm, smem) for...]
  transfers between devices with their start and end apart: 11 -> 11, of which waited for: 3 -> 3; matrix products, arithmetic and copies ran while one was open for 1% -> 1% of each run, Pallas kernels for 36% -> 34%
where the time goes in v5:
time: 153 us; the launch traced here: 152 us
  Pallas kernels  79.6 us (52%)
  starting transfers between devices  43.3 us (28%)
  waiting for transfers between devices  21.8 us (14%)
  local copies, waits for them, and re-layouts  4.52 us (3%)
  between operations  1.67 us (1%)
    pallas_call x7, Pallas kernels, stepped(): pl.pallas_call(kernel, grid_spec=spec, out_shape=outs, compiler_params=pl...  55.2 us
    all_to_all x5, starting transfers between devices, swap(): return lax.all_to_all(x, 'label', split_axis=0, concat_axis=0, tiled=True)  34.8 us
    pallas_call x9, Pallas kernels, whole(): pl.pallas_call(kernel, out_shape=outs, in_specs=[place(i, hbm, smem) for...  24.4 us
    all_to_all x5, waiting for transfers between devices, swap(): return lax.all_to_all(x, 'label', split_axis=0, concat_axis=0, tiled=True)  15 us
    ppermute x1, waiting for transfers between devices, per_device(): from_prev_a = lax.ppermute(relay_up, 'dp', up)  6.75 us
    unnamed x18, local copies, waits for them, and re-layouts  3.59 us
  transfers between devices with their start and end apart: 11, of which 3 were waited for; matrix products, arithmetic and copies ran while one was open for 1% of the time, Pallas kernels for 34%

profile of v5, /device:TPU:2, one launch (start us, length us, event | category | flops | bytes accessed | tf_op | source)
XLA Modules:
  0.0 151.6 jit_solution(4391675603598142546)
XLA Ops:
  0.6 1.9 %shard_map.76 = bf16[16,2,8,896]{3,2,1,0:T(8,128)(2,1)} custom-call(bf16[2,16,8,768]{3,2,1,0:T(8,128)(2,1)} %bitcast.30, s32[2,128]{1,0:T(2,128)} %bitcast.31, s32[2,4]{1,0:T(2,128)} %beam_hbm.1), custom_call_target="tpu_custom_call" | custom-call | flops 1024 | bytes 1024 | tf_op jit(solution)/shard_map/pallas_call | solution.py:333
  2.5 8.5 %all-to-all-start = ((bf16[32,8,896]{2,1,0:T(8,128)(2,1)}), bf16[32,8,896]{2,1,0:T(8,128)(2,1)S(1)}, u32[]{:S(2)}, u32[]{:S(2)}) async-start(bf16[32,8,896]{2,1,0:T(8,128)(2,1)} %bitcast.29), calls=%async_computation | async-start | bytes 917504 | tf_op jit(solution)/shard_map/all_to_all | solution.py:380
  11.0 0.1 select_reduce_fusion
  11.1 0.1 broadcast_in_dim.42
  11.2 0.1 broadcast_in_dim.43
  11.3 9.5 %all-to-all-done = bf16[32,8,896]{2,1,0:T(8,128)(2,1)S(1)} async-done(((bf16[32,8,896]{2,1,0:T(8,128)(2,1)}), bf16[32,8,896]{2,1,0:T(8,128)(2,1)S(1)}, u32[]{:S(2)}, u32[]{:S(2)}) %all-to-all-start) | async-done | bytes 458784 | tf_op jit(solution)/shard_map/all_to_all | solution.py:380
  20.8 0.1 broadcast_in_dim.44.held_ref
  20.9 2.9 %shard_map.77 = bf16[2048,384]{1,0:T(8,128)(2,1)} custom-call(bf16[256,896]{1,0:T(8,128)(2,1)S(1)} %bitcast.22, f32[256,128]{1,0:T(8,128)S(1)} %broadcast_in_dim.44.held_ref), custom_call_target="tpu_custom_call" | custom-call | flops 1024 | bytes 1024 | tf_op jit(solution)/shard_map/pallas_call | solution.py:333
  23.8 5.7 %all-to-all-start.1 = ((bf16[32,64,384]{2,1,0:T(8,128)(2,1)}), bf16[32,64,384]{2,1,0:T(8,128)(2,1)}, u32[]{:S(2)}, u32[]{:S(2)}) async-start(bf16[32,64,384]{2,1,0:T(8,128)(2,1)} %bitcast.4), calls=%async_computation.1 | async-start | bytes 3145728 | tf_op jit(solution)/shard_map/all_to_all | solution.py:380
  29.6 0.6 fusion
  30.9 0.6 iota.17.mine_ref
  31.5 3.7 %shard_map.78 = (bf16[512,2048]{1,0:T(8,128)(2,1)}, f32[256,128]{1,0:T(8,128)}, s32[8,1024]{1,0:T(8,128)}, f32[8,128]{1,0:T(8,128)}) custom-call(bf16[256,896]{1,0:T(8,128)(2,1)} %bitcast.23, f32[256,128]{1,0:T(8,128)} %copy-done.4, f32[16,128]{1,0:T(8,128)} %iota.17.mine_ref), custom_call_target="tpu_custom_call" | custom-call | flops 1024 | bytes 1024 | tf_op jit(solution)/shard_map/pallas_call | solution.py:333
  35.2 0.8 copy-done.2
  35.9 10.4 %shard_map.79.r_ref = bf16[1024,768]{1,0:T(8,128)(2,1)S(1)} custom-call(s32[8,1024]{1,0:T(8,128)S(1)} %copy-done.2, bf16[4096,768]{1,0:T(8,128)(2,1)} %bitcast.25), custom_call_target="tpu_custom_call" | custom-call | flops 1024 | bytes 1024 | tf_op jit(solution)/shard_map/pallas_call | solution.py:360
  46.3 5.5 %all-to-all-done.1 = bf16[32,64,384]{2,1,0:T(8,128)(2,1)} async-done(((bf16[32,64,384]{2,1,0:T(8,128)(2,1)}), bf16[32,64,384]{2,1,0:T(8,128)(2,1)}, u32[]{:S(2)}, u32[]{:S(2)}) %all-to-all-start.1) | async-done | bytes 1572896 | tf_op jit(solution)/shard_map/all_to_all | solution.py:380
  51.8 13.6 %shard_map.80 = (bf16[4096,1024]{1,0:T(8,128)(2,1)}, bf16[1024,768]{1,0:T(8,128)(2,1)S(1)}, f32[16,8,1024]{2,1,0:T(8,128)}, f32[32,16,128]{2,1,0:T(8,128)}, f32[8,1024]{1,0:T(8,128)S(1)}) custom-call(bf16[16,2,8,8,384]{4,3,2,1,0:T(8,128)(2,1)} %bitcast.6.got_ref, s32[8,1024]{1,0:T(8,128)S(1)} %copy-done.3, bf16[4096,768]{1,0:T(8,128)(2,1)} %bitcast.26), custom_call_target="tpu_custom_call" | custom-call | flops 1024 | bytes 1024 | tf_op jit(solution)/shard_map/pallas_call | solution.py:360
  65.4 5.7 %all-to-all-start.2 = ((f32[32,16,128]{2,1,0:T(8,128)}), f32[32,16,128]{2,1,0:T(8,128)S(1)}, u32[]{:S(2)}, u32[]{:S(2)}) async-start(f32[32,16,128]{2,1,0:T(8,128)} %get-tuple-element.48.stat_ref), calls=%async_computation.2 | async-start | bytes 524288 | tf_op jit(solution)/shard_map/all_to_all | solution.py:380
  71.1 0.1 stack.35.tiles_ref
  71.2 12.3 %shard_map.81.u_ref = bf16[1024,768]{1,0:T(8,128)(2,1)} custom-call(f32[16,8,1024]{2,1,0:T(8,128)} %get-tuple-element.49.top_ref.refs_2_.refs_3_, f32[8,1024]{1,0:T(8,128)S(1)} %get-tuple-element.50.row_ref, bf16[4096,768]{1,0:T(8,128)(2,1)} %bitcast.27, bf16[4096,1024]{1,0:T(8,128)(2,1)} %get-tuple-element.51.p_ref.refs_0_.refs_1_), custom_call_target="tpu_custom_call" | custom-call | flops 1024 | bytes 1024 | tf_op jit(solution)/shard_map/pallas_call | solution.py:360
  83.4 0.0 all-to-all-done.2.stat_ref
  83.4 2.1 %shard_map.82 = (f32[8,1024]{1,0:T(8,128)S(1)}, f32[8,1024]{1,0:T(8,128)S(1)}, f32[8,128]{1,0:T(8,128)S(1)}, f32[2,128]{1,0:T(2,128)}) custom-call(f32[32,16,128]{2,1,0:T(8,128)S(1)} %all-to-all-done.2.stat_ref, f32[256,128]{1,0:T(8,128)} %get-tuple-element.53.mask_ref), custom_call_target="tpu_custom_call" | custom-call | flops 1024 | bytes 1024 | tf_op jit(solution)/shard_map/pallas_call | solution.py:333
  85.5 4.9 %shard_map.83 = (bf16[512,768]{1,0:T(8,128)(2,1)}, bf16[512,768]{1,0:T(8,128)(2,1)}) custom-call(s32[8]{0:T(128)S(1)} %stack.35.tiles_ref, bf16[1024,768]{1,0:T(8,128)(2,1)S(1)} %get-tuple-element.55.q_ref, f32[8,1024]{1,0:T(8,128)S(1)} %get-tuple-element.76.norm_ref, f32[8,1024]{1,0:T(8,128)S(1)} %get-tuple-element.59.rest_ref, s32[8,1024]{1,0:T(8,128)S(1)} %copy-done.3, ...), custom_call_target="tpu_custom_call" | custom-call | flops 1024 | bytes 1024 | tf_op jit(solution)/shard_map/pallas_call | solution.py:360
  90.4 1.6 %collective-permute-start = (bf16[512,768]{1,0:T(8,128)(2,1)}, bf16[512,768]{1,0:T(8,128)(2,1)}, u32[]{:S(2)}, u32[]{:S(2)}) collective-permute-start(bf16[512,768]{1,0:T(8,128)(2,1)} %get-tuple-element.72), channel_id=1, source_target_pairs={{0,32},{32,64},{64,96},{96,0},{1,33},{33,65},{65,97},{97,1},{2,34}... | collective-permute-start | bytes 2359304 | tf_op jit(solution)/shard_map/ppermute | solution.py:523
  92.0 1.7 %collective-permute-start.1 = (bf16[512,768]{1,0:T(8,128)(2,1)}, bf16[512,768]{1,0:T(8,128)(2,1)}, u32[]{:S(2)}, u32[]{:S(2)}) collective-permute-start(bf16[512,768]{1,0:T(8,128)(2,1)} %get-tuple-element.73), channel_id=1, source_target_pairs={{0,96},{32,0},{64,32},{96,64},{1,97},{33,1},{65,33},{97,65},{2,98}... | collective-permute-start | bytes 2359304 | tf_op jit(solution)/shard_map/ppermute | solution.py:524
  93.7 3.0 %shard_map.84 = bf16[16,2,64,384]{3,2,1,0:T(8,128)(2,1)} custom-call(bf16[1024,768]{1,0:T(8,128)(2,1)S(1)} %copy-done, bf16[1024,768]{1,0:T(8,128)(2,1)S(1)} %shard_map.79.r_ref, f32[32,16,128]{2,1,0:T(8,128)} %get-tuple-element.48.stat_ref, f32[8,128]{1,0:T(8,128)S(1)} %get-tuple-element.63.norm_ref, f32[8,128]{1,0:T(8,128)S(1)} %copy-done.5), custom_call_target="tpu_custom_call" | custom-call | flops 1024 | bytes 1024 | tf_op jit(solution)/shard_map/pallas_call | solution.py:333
  96.6 7.5 %all-to-all-start.3 = ((bf16[32,64,384]{2,1,0:T(8,128)(2,1)}), bf16[32,64,384]{2,1,0:T(8,128)(2,1)S(1)}, u32[]{:S(2)}, u32[]{:S(2)}) async-start(bf16[32,64,384]{2,1,0:T(8,128)(2,1)} %bitcast.28), calls=%async_computation.3 | async-start | bytes 3145728 | tf_op jit(solution)/shard_map/all_to_all | solution.py:380
  104.1 4.8 %shard_map.85 = (bf16[512,768]{1,0:T(8,128)(2,1)}, bf16[512,768]{1,0:T(8,128)(2,1)}) custom-call(s32[8]{0:T(128)S(1)} %stack.35.tiles_ref, bf16[1024,768]{1,0:T(8,128)(2,1)S(1)} %get-tuple-element.55.q_ref, f32[8,1024]{1,0:T(8,128)S(1)} %get-tuple-element.76.norm_ref, f32[8,1024]{1,0:T(8,128)S(1)} %get-tuple-element.59.rest_ref, s32[8,1024]{1,0:T(8,128)S(1)} %copy-done.3, ...), custom_call_target="tpu_custom_call" | custom-call | flops 1024 | bytes 1024 | tf_op jit(solution)/shard_map/pallas_call | solution.py:360
  109.0 1.8 %collective-permute-start.2 = (bf16[512,768]{1,0:T(8,128)(2,1)}, bf16[512,768]{1,0:T(8,128)(2,1)}, u32[]{:S(2)}, u32[]{:S(2)}) collective-permute-start(bf16[512,768]{1,0:T(8,128)(2,1)} %get-tuple-element.79), channel_id=1, source_target_pairs={{0,96},{32,0},{64,32},{96,64},{1,97},{33,1},{65,33},{97,65},{2,98}... | collective-permute-start | bytes 2359304 | tf_op jit(solution)/shard_map/ppermute | solution.py:540
  110.8 0.2 collective-permute-start.3
  111.0 3.9 %shard_map.86 = (f32[512,768]{1,0:T(8,128)S(1)}, f32[512,768]{1,0:T(8,128)S(1)}) custom-call(s32[8]{0:T(128)S(1)} %stack.35.tiles_ref, bf16[1024,768]{1,0:T(8,128)(2,1)S(1)} %get-tuple-element.55.q_ref, f32[8,1024]{1,0:T(8,128)S(1)} %get-tuple-element.76.norm_ref, f32[8,1024]{1,0:T(8,128)S(1)} %get-tuple-element.59.rest_ref, s32[8,1024]{1,0:T(8,128)S(1)} %copy-done.3, ...), custom_call_target="tpu_custom_call" | custom-call | flops 1024 | bytes 1024 | tf_op jit(solution)/shard_map/pallas_call | solution.py:360
  114.9 0.0 collective-permute-done.got_up_ref
  114.9 0.0 collective-permute-done.1.got_down_ref
  114.9 2.7 %shard_map.87 = (bf16[512,768]{1,0:T(8,128)(2,1)}, bf16[512,768]{1,0:T(8,128)(2,1)}) custom-call(f32[512,768]{1,0:T(8,128)S(1)} %get-tuple-element.70.up_ref, f32[512,768]{1,0:T(8,128)S(1)} %get-tuple-element.71.down_ref, bf16[512,768]{1,0:T(8,128)(2,1)} %collective-permute-done.got_up_ref, bf16[512,768]{1,0:T(8,128)(2,1)} %collective-permute-done.1.got_down_ref), custom_call_target="tpu_custom_call" | custom-call | flops 49999998976 | bytes 1024 | tf_op jit(solution)/shard_map/pallas_call | solution.py:333
  117.6 0.4 collective-permute-start.4
  118.0 2.8 %collective-permute-start.5 = (bf16[512,768]{1,0:T(8,128)(2,1)}, bf16[512,768]{1,0:T(8,128)(2,1)}, u32[]{:S(2)}, u32[]{:S(2)}) collective-permute-start(bf16[512,768]{1,0:T(8,128)(2,1)} %get-tuple-element.82), channel_id=1, source_target_pairs={{0,96},{32,0},{64,32},{96,64},{1,97},{33,1},{65,33},{97,65},{2,98}... | collective-permute-start | bytes 2359304 | tf_op jit(solution)/shard_map/ppermute | solution.py:556
  120.8 5.4 %shard_map.88 = (f32[512,768]{1,0:T(8,128)}, f32[512,768]{1,0:T(8,128)}) custom-call(s32[8]{0:T(128)S(1)} %stack.35.tiles_ref, bf16[1024,768]{1,0:T(8,128)(2,1)S(1)} %get-tuple-element.55.q_ref, f32[8,1024]{1,0:T(8,128)S(1)} %get-tuple-element.76.norm_ref, f32[8,1024]{1,0:T(8,128)S(1)} %get-tuple-element.59.rest_ref, s32[8,1024]{1,0:T(8,128)S(1)} %copy-done.3, ...), custom_call_target="tpu_custom_call" | custom-call | flops 1024 | bytes 1024 | tf_op jit(solution)/shard_map/pallas_call | solution.py:360
  126.2 0.0 all-to-all-done.3
  126.3 3.6 %shard_map.90 = bf16[32,8,768]{2,1,0:T(8,128)(2,1)} custom-call(bf16[512,2048]{1,0:T(8,128)(2,1)} %get-tuple-element.83.sel_ref, bf16[2048,384]{1,0:T(8,128)(2,1)S(1)} %bitcast.21), custom_call_target="tpu_custom_call" | custom-call | flops 1024 | bytes 1024 | tf_op jit(solution)/shard_map/pallas_call | solution.py:333
  129.8 7.4 %all-to-all-start.4 = ((bf16[32,8,768]{2,1,0:T(8,128)(2,1)}), bf16[32,8,768]{2,1,0:T(8,128)(2,1)S(1)}, u32[]{:S(2)}, u32[]{:S(2)}) async-start(bf16[32,8,768]{2,1,0:T(8,128)(2,1)} %shard_map.90), calls=%async_computation.4 | async-start | bytes 786432 | tf_op jit(solution)/shard_map/all_to_all | solution.py:380
  137.2 0.0 collective-permute-done.2.a_ref
  137.3 0.0 collective-permute-done.3.b_ref
  137.3 1.4 copy-done.6
  138.7 1.4 copy-done.7
  140.1 1.6 %shard_map.89.base_ref = f32[1024,768]{1,0:T(8,128)S(1)} custom-call(f32[512,768]{1,0:T(8,128)S(1)} %copy-done.6, f32[512,768]{1,0:T(8,128)S(1)} %copy-done.7, bf16[512,768]{1,0:T(8,128)(2,1)} %collective-permute-done.2.a_ref, bf16[512,768]{1,0:T(8,128)(2,1)} %collective-permute-done.3.b_ref), custom_call_target="tpu_custom_call" | custom-call | flops 8000000000 | bytes 1024 | tf_op jit(solution)/shard_map/pallas_call | solution.py:333
  141.7 6.7 %collective-permute-done.4.a_hbm = bf16[512,768]{1,0:T(8,128)(2,1)} collective-permute-done((bf16[512,768]{1,0:T(8,128)(2,1)}, bf16[512,768]{1,0:T(8,128)(2,1)}, u32[]{:S(2)}, u32[]{:S(2)}) %collective-permute-start.4) | collective-permute-done | bytes 786464 | tf_op jit(solution)/shard_map/ppermute | solution.py:555
  148.5 0.0 collective-permute-done.5.b_hbm
  148.5 0.0 all-to-all-done.4
  148.5 2.9 %shard_map.91 = (f32[1024,768]{1,0:T(8,128)}, f32[2,16,8,768]{3,2,1,0:T(8,128)}) custom-call(f32[1024,768]{1,0:T(8,128)S(1)} %shard_map.89.base_ref, bf16[512,768]{1,0:T(8,128)(2,1)} %collective-permute-done.4.a_hbm, bf16[512,768]{1,0:T(8,128)(2,1)} %collective-permute-done.5.b_hbm, bf16[16,2,8,768]{3,2,1,0:T(8,128)(2,1)S(1)} %bitcast.24), custom_call_target="tpu_custom_call" | custom-call | flops 1024 | bytes 1024 | tf_op jit(solution)/shard_map/pallas_call | solution.py:333
  (17 shorter events, 0.0 us)
Async XLA Ops:
  0.6 10.4 %copy-start.8 = (s32[32]{0:T(128)S(1)}, s32[32]{0:T(128)}, u32[]{:S(2)}) copy-start(s32[32]{0:T(128)} %param.9) | copy-start | bytes 388
  2.5 18.3 %all-to-all-start = ((bf16[32,8,896]{2,1,0:T(8,128)(2,1)}), bf16[32,8,896]{2,1,0:T(8,128)(2,1)S(1)}, u32[]{:S(2)}, u32[]{:S(2)}) async-start(bf16[32,8,896]{2,1,0:T(8,128)(2,1)} %bitcast.29), calls=%async_computation | async-start | bytes 917504 | tf_op jit(solution)/shard_map/all_to_all | solution.py:380
  20.8 3.0 %copy-start.1 = (bf16[32,8,896]{2,1,0:T(8,128)(2,1)}, bf16[32,8,896]{2,1,0:T(8,128)(2,1)S(1)}, u32[]{:S(2)}) copy-start(bf16[32,8,896]{2,1,0:T(8,128)(2,1)S(1)} %all-to-all-done) | copy-start | bytes 1376260
  20.9 2.9 %copy-start.4 = (f32[256,128]{1,0:T(8,128)}, f32[256,128]{1,0:T(8,128)S(1)}, u32[]{:S(2)}) copy-start(f32[256,128]{1,0:T(8,128)S(1)} %broadcast_in_dim.44.held_ref) | copy-start | bytes 393220
  23.8 28.0 %all-to-all-start.1 = ((bf16[32,64,384]{2,1,0:T(8,128)(2,1)}), bf16[32,64,384]{2,1,0:T(8,128)(2,1)}, u32[]{:S(2)}, u32[]{:S(2)}) async-start(bf16[32,64,384]{2,1,0:T(8,128)(2,1)} %bitcast.4), calls=%async_computation.1 | async-start | bytes 3145728 | tf_op jit(solution)/shard_map/all_to_all | solution.py:380
  35.1 0.8 copy-start.2
  35.9 15.9 %copy-start.3 = (s32[8,1024]{1,0:T(8,128)S(1)}, s32[8,1024]{1,0:T(8,128)}, u32[]{:S(2)}) copy-start(s32[8,1024]{1,0:T(8,128)} %get-tuple-element.47.col_ref) | copy-start | bytes 98308
  65.4 18.0 %all-to-all-start.2 = ((f32[32,16,128]{2,1,0:T(8,128)}), f32[32,16,128]{2,1,0:T(8,128)S(1)}, u32[]{:S(2)}, u32[]{:S(2)}) async-start(f32[32,16,128]{2,1,0:T(8,128)} %get-tuple-element.48.stat_ref), calls=%async_computation.2 | async-start | bytes 524288 | tf_op jit(solution)/shard_map/all_to_all | solution.py:380
  85.5 8.1 %copy-start = (bf16[1024,768]{1,0:T(8,128)(2,1)S(1)}, bf16[1024,768]{1,0:T(8,128)(2,1)}, u32[]{:S(2)}) copy-start(bf16[1024,768]{1,0:T(8,128)(2,1)} %shard_map.81.u_ref) | copy-start | bytes 4718596
  85.5 8.1 %copy-start.5 = (f32[8,128]{1,0:T(8,128)S(1)}, f32[8,128]{1,0:T(8,128)}, u32[]{:S(2)}) copy-start(f32[8,128]{1,0:T(8,128)} %get-tuple-element.64.col_ref) | copy-start | bytes 12292
  90.4 24.4 %collective-permute-start = (bf16[512,768]{1,0:T(8,128)(2,1)}, bf16[512,768]{1,0:T(8,128)(2,1)}, u32[]{:S(2)}, u32[]{:S(2)}) collective-permute-start(bf16[512,768]{1,0:T(8,128)(2,1)} %get-tuple-element.72), channel_id=1, source_target_pairs={{0,32},{32,64},{64,96},{96,0},{1,33},{33,65},{65,97},{97,1},{2,34}... | collective-permute-start | bytes 2359304 | tf_op jit(solution)/shard_map/ppermute | solution.py:523
  92.0 22.9 %collective-permute-start.1 = (bf16[512,768]{1,0:T(8,128)(2,1)}, bf16[512,768]{1,0:T(8,128)(2,1)}, u32[]{:S(2)}, u32[]{:S(2)}) collective-permute-start(bf16[512,768]{1,0:T(8,128)(2,1)} %get-tuple-element.73), channel_id=1, source_target_pairs={{0,96},{32,0},{64,32},{96,64},{1,97},{33,1},{65,33},{97,65},{2,98}... | collective-permute-start | bytes 2359304 | tf_op jit(solution)/shard_map/ppermute | solution.py:524
  96.6 29.6 %all-to-all-start.3 = ((bf16[32,64,384]{2,1,0:T(8,128)(2,1)}), bf16[32,64,384]{2,1,0:T(8,128)(2,1)S(1)}, u32[]{:S(2)}, u32[]{:S(2)}) async-start(bf16[32,64,384]{2,1,0:T(8,128)(2,1)} %bitcast.28), calls=%async_computation.3 | async-start | bytes 3145728 | tf_op jit(solution)/shard_map/all_to_all | solution.py:380
  109.0 28.3 %collective-permute-start.2 = (bf16[512,768]{1,0:T(8,128)(2,1)}, bf16[512,768]{1,0:T(8,128)(2,1)}, u32[]{:S(2)}, u32[]{:S(2)}) collective-permute-start(bf16[512,768]{1,0:T(8,128)(2,1)} %get-tuple-element.79), channel_id=1, source_target_pairs={{0,96},{32,0},{64,32},{96,64},{1,97},{33,1},{65,33},{97,65},{2,98}... | collective-permute-start | bytes 2359304 | tf_op jit(solution)/shard_map/ppermute | solution.py:540
  110.8 26.5 %collective-permute-start.3 = (bf16[512,768]{1,0:T(8,128)(2,1)}, bf16[512,768]{1,0:T(8,128)(2,1)}, u32[]{:S(2)}, u32[]{:S(2)}) collective-permute-start(bf16[512,768]{1,0:T(8,128)(2,1)} %get-tuple-element.80), channel_id=1, source_target_pairs={{0,32},{32,64},{64,96},{96,0},{1,33},{33,65},{65,97},{97,1},{2,34}... | collective-permute-start | bytes 2359304 | tf_op jit(solution)/shard_map/ppermute | solution.py:539
  117.6 30.9 %collective-permute-start.4 = (bf16[512,768]{1,0:T(8,128)(2,1)}, bf16[512,768]{1,0:T(8,128)(2,1)}, u32[]{:S(2)}, u32[]{:S(2)}) collective-permute-start(bf16[512,768]{1,0:T(8,128)(2,1)} %get-tuple-element.81), channel_id=1, source_target_pairs={{0,32},{32,64},{64,96},{96,0},{1,33},{33,65},{65,97},{97,1},{2,34}... | collective-permute-start | bytes 2359304 | tf_op jit(solution)/shard_map/ppermute | solution.py:555
  118.0 30.5 %collective-permute-start.5 = (bf16[512,768]{1,0:T(8,128)(2,1)}, bf16[512,768]{1,0:T(8,128)(2,1)}, u32[]{:S(2)}, u32[]{:S(2)}) collective-permute-start(bf16[512,768]{1,0:T(8,128)(2,1)} %get-tuple-element.82), channel_id=1, source_target_pairs={{0,96},{32,0},{64,32},{96,64},{1,97},{33,1},{65,33},{97,65},{2,98}... | collective-permute-start | bytes 2359304 | tf_op jit(solution)/shard_map/ppermute | solution.py:556
  129.8 18.6 %all-to-all-start.4 = ((bf16[32,8,768]{2,1,0:T(8,128)(2,1)}), bf16[32,8,768]{2,1,0:T(8,128)(2,1)S(1)}, u32[]{:S(2)}, u32[]{:S(2)}) async-start(bf16[32,8,768]{2,1,0:T(8,128)(2,1)} %shard_map.90), calls=%async_computation.4 | async-start | bytes 786432 | tf_op jit(solution)/shard_map/all_to_all | solution.py:380
  137.3 1.4 copy-start.6
  138.7 1.4 copy-start.7

commit v6 on v5

--- a/solution.py
+++ b/solution.py
@@ -50,9 +50,8 @@
     e = iota((64, 512), 1)
     spread = ones_where(iota((64, 512), 0) == e // 8)
     wide = dot(table.astype(BF16), spread, ((1,), (0,)))
-    full = jnp.broadcast_to(wide[:, None, :], (256, 8, 512))
-    same = iota((256, 8, 512), 1) == iota((256, 8, 512), 2) % 8
-    return jnp.where(same, full, 0.0).reshape(2048, 512).astype(BF16)
+    same = jnp.where(iota((8, 512), 0) == (iota((8, 512), 1) & 7), 1.0, 0.0)
+    return (wide[:, None, :] * same[None]).reshape(2048, 512).astype(BF16)
 
 def route_kernel(got_ref, held_ref, out_ref):
     got = got_ref[...]

time: 153 us -> 153 us (level)
  no operation moved by 1% of the time
where the time goes in v6:
time: 153 us; the launch traced here: 152 us
  Pallas kernels  79.6 us (52%)
  starting transfers between devices  43.2 us (28%)
  waiting for transfers between devices  21.8 us (14%)
  local copies, waits for them, and re-layouts  4.52 us (3%)
  between operations  1.67 us (1%)
    pallas_call x7, Pallas kernels, stepped(): pl.pallas_call(kernel, grid_spec=spec, out_shape=outs, compiler_params=pl...  55.2 us
    all_to_all x5, starting transfers between devices, swap(): return lax.all_to_all(x, 'label', split_axis=0, concat_axis=0, tiled=True)  34.7 us
    pallas_call x9, Pallas kernels, whole(): pl.pallas_call(kernel, out_shape=outs, in_specs=[place(i, hbm, smem) for...  24.4 us
    all_to_all x5, waiting for transfers between devices, swap(): return lax.all_to_all(x, 'label', split_axis=0, concat_axis=0, tiled=True)  15.1 us
    ppermute x1, waiting for transfers between devices, per_device(): from_prev_a = lax.ppermute(relay_up, 'dp', up)  6.76 us
    unnamed x18, local copies, waits for them, and re-layouts  3.59 us
  transfers between devices with their start and end apart: 11, of which 3 were waited for; matrix products, arithmetic and copies ran while one was open for 1% of the time, Pallas kernels for 34%

profile of v6, /device:TPU:2, one launch (start us, length us, event | category | flops | bytes accessed | tf_op | source)
XLA Modules:
  0.0 151.6 jit_solution(1211729513299336164)
XLA Ops:
  0.6 1.9 %shard_map.76 = bf16[16,2,8,896]{3,2,1,0:T(8,128)(2,1)} custom-call(bf16[2,16,8,768]{3,2,1,0:T(8,128)(2,1)} %bitcast.30, s32[2,128]{1,0:T(2,128)} %bitcast.31, s32[2,4]{1,0:T(2,128)} %beam_hbm.1), custom_call_target="tpu_custom_call" | custom-call | flops 1024 | bytes 1024 | tf_op jit(solution)/shard_map/pallas_call | solution.py:332
  2.5 8.5 %all-to-all-start = ((bf16[32,8,896]{2,1,0:T(8,128)(2,1)}), bf16[32,8,896]{2,1,0:T(8,128)(2,1)S(1)}, u32[]{:S(2)}, u32[]{:S(2)}) async-start(bf16[32,8,896]{2,1,0:T(8,128)(2,1)} %bitcast.29), calls=%async_computation | async-start | bytes 917504 | tf_op jit(solution)/shard_map/all_to_all | solution.py:379
  11.0 0.1 select_reduce_fusion
  11.1 0.1 broadcast_in_dim.42
  11.2 0.1 broadcast_in_dim.43
  11.3 9.5 %all-to-all-done = bf16[32,8,896]{2,1,0:T(8,128)(2,1)S(1)} async-done(((bf16[32,8,896]{2,1,0:T(8,128)(2,1)}), bf16[32,8,896]{2,1,0:T(8,128)(2,1)S(1)}, u32[]{:S(2)}, u32[]{:S(2)}) %all-to-all-start) | async-done | bytes 458784 | tf_op jit(solution)/shard_map/all_to_all | solution.py:379
  20.8 0.1 broadcast_in_dim.44.held_ref
  20.9 2.9 %shard_map.77 = bf16[2048,384]{1,0:T(8,128)(2,1)} custom-call(bf16[256,896]{1,0:T(8,128)(2,1)S(1)} %bitcast.22, f32[256,128]{1,0:T(8,128)S(1)} %broadcast_in_dim.44.held_ref), custom_call_target="tpu_custom_call" | custom-call | flops 1024 | bytes 1024 | tf_op jit(solution)/shard_map/pallas_call | solution.py:332
  23.8 5.7 %all-to-all-start.1 = ((bf16[32,64,384]{2,1,0:T(8,128)(2,1)}), bf16[32,64,384]{2,1,0:T(8,128)(2,1)}, u32[]{:S(2)}, u32[]{:S(2)}) async-start(bf16[32,64,384]{2,1,0:T(8,128)(2,1)} %bitcast.4), calls=%async_computation.1 | async-start | bytes 3145728 | tf_op jit(solution)/shard_map/all_to_all | solution.py:379
  29.6 0.6 fusion
  30.9 0.6 iota.17.mine_ref
  31.5 3.6 %shard_map.78 = (bf16[512,2048]{1,0:T(8,128)(2,1)}, f32[256,128]{1,0:T(8,128)}, s32[8,1024]{1,0:T(8,128)}, f32[8,128]{1,0:T(8,128)}) custom-call(bf16[256,896]{1,0:T(8,128)(2,1)} %bitcast.23, f32[256,128]{1,0:T(8,128)} %copy-done.4, f32[16,128]{1,0:T(8,128)} %iota.17.mine_ref), custom_call_target="tpu_custom_call" | custom-call | flops 1024 | bytes 1024 | tf_op jit(solution)/shard_map/pallas_call | solution.py:332
  35.1 0.8 copy-done.2
  35.9 10.4 %shard_map.79.r_ref = bf16[1024,768]{1,0:T(8,128)(2,1)S(1)} custom-call(s32[8,1024]{1,0:T(8,128)S(1)} %copy-done.2, bf16[4096,768]{1,0:T(8,128)(2,1)} %bitcast.25), custom_call_target="tpu_custom_call" | custom-call | flops 1024 | bytes 1024 | tf_op jit(solution)/shard_map/pallas_call | solution.py:359
  46.2 5.6 %all-to-all-done.1 = bf16[32,64,384]{2,1,0:T(8,128)(2,1)} async-done(((bf16[32,64,384]{2,1,0:T(8,128)(2,1)}), bf16[32,64,384]{2,1,0:T(8,128)(2,1)}, u32[]{:S(2)}, u32[]{:S(2)}) %all-to-all-start.1) | async-done | bytes 1572896 | tf_op jit(solution)/shard_map/all_to_all | solution.py:379
  51.8 13.6 %shard_map.80 = (bf16[4096,1024]{1,0:T(8,128)(2,1)}, bf16[1024,768]{1,0:T(8,128)(2,1)S(1)}, f32[16,8,1024]{2,1,0:T(8,128)}, f32[32,16,128]{2,1,0:T(8,128)}, f32[8,1024]{1,0:T(8,128)S(1)}) custom-call(bf16[16,2,8,8,384]{4,3,2,1,0:T(8,128)(2,1)} %bitcast.6.got_ref, s32[8,1024]{1,0:T(8,128)S(1)} %copy-done.3, bf16[4096,768]{1,0:T(8,128)(2,1)} %bitcast.26), custom_call_target="tpu_custom_call" | custom-call | flops 1024 | bytes 1024 | tf_op jit(solution)/shard_map/pallas_call | solution.py:359
  65.4 5.7 %all-to-all-start.2 = ((f32[32,16,128]{2,1,0:T(8,128)}), f32[32,16,128]{2,1,0:T(8,128)S(1)}, u32[]{:S(2)}, u32[]{:S(2)}) async-start(f32[32,16,128]{2,1,0:T(8,128)} %get-tuple-element.48.stat_ref), calls=%async_computation.2 | async-start | bytes 524288 | tf_op jit(solution)/shard_map/all_to_all | solution.py:379
  71.1 0.1 stack.35.tiles_ref
  71.2 12.3 %shard_map.81.u_ref = bf16[1024,768]{1,0:T(8,128)(2,1)} custom-call(f32[16,8,1024]{2,1,0:T(8,128)} %get-tuple-element.49.top_ref.refs_2_.refs_3_, f32[8,1024]{1,0:T(8,128)S(1)} %get-tuple-element.50.row_ref, bf16[4096,768]{1,0:T(8,128)(2,1)} %bitcast.27, bf16[4096,1024]{1,0:T(8,128)(2,1)} %get-tuple-element.51.p_ref.refs_0_.refs_1_), custom_call_target="tpu_custom_call" | custom-call | flops 1024 | bytes 1024 | tf_op jit(solution)/shard_map/pallas_call | solution.py:359
  83.4 0.0 all-to-all-done.2.stat_ref
  83.4 2.1 %shard_map.82 = (f32[8,1024]{1,0:T(8,128)S(1)}, f32[8,1024]{1,0:T(8,128)S(1)}, f32[8,128]{1,0:T(8,128)S(1)}, f32[2,128]{1,0:T(2,128)}) custom-call(f32[32,16,128]{2,1,0:T(8,128)S(1)} %all-to-all-done.2.stat_ref, f32[256,128]{1,0:T(8,128)} %get-tuple-element.53.mask_ref), custom_call_target="tpu_custom_call" | custom-call | flops 1024 | bytes 1024 | tf_op jit(solution)/shard_map/pallas_call | solution.py:332
  85.5 4.9 %shard_map.83 = (bf16[512,768]{1,0:T(8,128)(2,1)}, bf16[512,768]{1,0:T(8,128)(2,1)}) custom-call(s32[8]{0:T(128)S(1)} %stack.35.tiles_ref, bf16[1024,768]{1,0:T(8,128)(2,1)S(1)} %get-tuple-element.55.q_ref, f32[8,1024]{1,0:T(8,128)S(1)} %get-tuple-element.76.norm_ref, f32[8,1024]{1,0:T(8,128)S(1)} %get-tuple-element.59.rest_ref, s32[8,1024]{1,0:T(8,128)S(1)} %copy-done.3, ...), custom_call_target="tpu_custom_call" | custom-call | flops 1024 | bytes 1024 | tf_op jit(solution)/shard_map/pallas_call | solution.py:359
  90.4 1.6 %collective-permute-start = (bf16[512,768]{1,0:T(8,128)(2,1)}, bf16[512,768]{1,0:T(8,128)(2,1)}, u32[]{:S(2)}, u32[]{:S(2)}) collective-permute-start(bf16[512,768]{1,0:T(8,128)(2,1)} %get-tuple-element.72), channel_id=1, source_target_pairs={{0,32},{32,64},{64,96},{96,0},{1,33},{33,65},{65,97},{97,1},{2,34}... | collective-permute-start | bytes 2359304 | tf_op jit(solution)/shard_map/ppermute | solution.py:522
  92.0 1.7 %collective-permute-start.1 = (bf16[512,768]{1,0:T(8,128)(2,1)}, bf16[512,768]{1,0:T(8,128)(2,1)}, u32[]{:S(2)}, u32[]{:S(2)}) collective-permute-start(bf16[512,768]{1,0:T(8,128)(2,1)} %get-tuple-element.73), channel_id=1, source_target_pairs={{0,96},{32,0},{64,32},{96,64},{1,97},{33,1},{65,33},{97,65},{2,98}... | collective-permute-start | bytes 2359304 | tf_op jit(solution)/shard_map/ppermute | solution.py:523
  93.7 3.0 %shard_map.84 = bf16[16,2,64,384]{3,2,1,0:T(8,128)(2,1)} custom-call(bf16[1024,768]{1,0:T(8,128)(2,1)S(1)} %copy-done, bf16[1024,768]{1,0:T(8,128)(2,1)S(1)} %shard_map.79.r_ref, f32[32,16,128]{2,1,0:T(8,128)} %get-tuple-element.48.stat_ref, f32[8,128]{1,0:T(8,128)S(1)} %get-tuple-element.63.norm_ref, f32[8,128]{1,0:T(8,128)S(1)} %copy-done.5), custom_call_target="tpu_custom_call" | custom-call | flops 1024 | bytes 1024 | tf_op jit(solution)/shard_map/pallas_call | solution.py:332
  96.6 7.5 %all-to-all-start.3 = ((bf16[32,64,384]{2,1,0:T(8,128)(2,1)}), bf16[32,64,384]{2,1,0:T(8,128)(2,1)S(1)}, u32[]{:S(2)}, u32[]{:S(2)}) async-start(bf16[32,64,384]{2,1,0:T(8,128)(2,1)} %bitcast.28), calls=%async_computation.3 | async-start | bytes 3145728 | tf_op jit(solution)/shard_map/all_to_all | solution.py:379
  104.1 4.8 %shard_map.85 = (bf16[512,768]{1,0:T(8,128)(2,1)}, bf16[512,768]{1,0:T(8,128)(2,1)}) custom-call(s32[8]{0:T(128)S(1)} %stack.35.tiles_ref, bf16[1024,768]{1,0:T(8,128)(2,1)S(1)} %get-tuple-element.55.q_ref, f32[8,1024]{1,0:T(8,128)S(1)} %get-tuple-element.76.norm_ref, f32[8,1024]{1,0:T(8,128)S(1)} %get-tuple-element.59.rest_ref, s32[8,1024]{1,0:T(8,128)S(1)} %copy-done.3, ...), custom_call_target="tpu_custom_call" | custom-call | flops 1024 | bytes 1024 | tf_op jit(solution)/shard_map/pallas_call | solution.py:359
  109.0 1.8 %collective-permute-start.2 = (bf16[512,768]{1,0:T(8,128)(2,1)}, bf16[512,768]{1,0:T(8,128)(2,1)}, u32[]{:S(2)}, u32[]{:S(2)}) collective-permute-start(bf16[512,768]{1,0:T(8,128)(2,1)} %get-tuple-element.79), channel_id=1, source_target_pairs={{0,96},{32,0},{64,32},{96,64},{1,97},{33,1},{65,33},{97,65},{2,98}... | collective-permute-start | bytes 2359304 | tf_op jit(solution)/shard_map/ppermute | solution.py:539
  110.8 0.2 collective-permute-start.3
  111.0 3.9 %shard_map.86 = (f32[512,768]{1,0:T(8,128)S(1)}, f32[512,768]{1,0:T(8,128)S(1)}) custom-call(s32[8]{0:T(128)S(1)} %stack.35.tiles_ref, bf16[1024,768]{1,0:T(8,128)(2,1)S(1)} %get-tuple-element.55.q_ref, f32[8,1024]{1,0:T(8,128)S(1)} %get-tuple-element.76.norm_ref, f32[8,1024]{1,0:T(8,128)S(1)} %get-tuple-element.59.rest_ref, s32[8,1024]{1,0:T(8,128)S(1)} %copy-done.3, ...), custom_call_target="tpu_custom_call" | custom-call | flops 1024 | bytes 1024 | tf_op jit(solution)/shard_map/pallas_call | solution.py:359
  114.9 0.0 collective-permute-done.got_up_ref
  114.9 0.0 collective-permute-done.1.got_down_ref
  114.9 2.7 %shard_map.87 = (bf16[512,768]{1,0:T(8,128)(2,1)}, bf16[512,768]{1,0:T(8,128)(2,1)}) custom-call(f32[512,768]{1,0:T(8,128)S(1)} %get-tuple-element.70.up_ref, f32[512,768]{1,0:T(8,128)S(1)} %get-tuple-element.71.down_ref, bf16[512,768]{1,0:T(8,128)(2,1)} %collective-permute-done.got_up_ref, bf16[512,768]{1,0:T(8,128)(2,1)} %collective-permute-done.1.got_down_ref), custom_call_target="tpu_custom_call" | custom-call | flops 49999998976 | bytes 1024 | tf_op jit(solution)/shard_map/pallas_call | solution.py:332
  117.6 0.4 collective-permute-start.4
  118.0 2.8 %collective-permute-start.5 = (bf16[512,768]{1,0:T(8,128)(2,1)}, bf16[512,768]{1,0:T(8,128)(2,1)}, u32[]{:S(2)}, u32[]{:S(2)}) collective-permute-start(bf16[512,768]{1,0:T(8,128)(2,1)} %get-tuple-element.82), channel_id=1, source_target_pairs={{0,96},{32,0},{64,32},{96,64},{1,97},{33,1},{65,33},{97,65},{2,98}... | collective-permute-start | bytes 2359304 | tf_op jit(solution)/shard_map/ppermute | solution.py:555
  120.8 5.4 %shard_map.88 = (f32[512,768]{1,0:T(8,128)}, f32[512,768]{1,0:T(8,128)}) custom-call(s32[8]{0:T(128)S(1)} %stack.35.tiles_ref, bf16[1024,768]{1,0:T(8,128)(2,1)S(1)} %get-tuple-element.55.q_ref, f32[8,1024]{1,0:T(8,128)S(1)} %get-tuple-element.76.norm_ref, f32[8,1024]{1,0:T(8,128)S(1)} %get-tuple-element.59.rest_ref, s32[8,1024]{1,0:T(8,128)S(1)} %copy-done.3, ...), custom_call_target="tpu_custom_call" | custom-call | flops 1024 | bytes 1024 | tf_op jit(solution)/shard_map/pallas_call | solution.py:359
  126.2 0.0 all-to-all-done.3
  126.3 3.6 %shard_map.90 = bf16[32,8,768]{2,1,0:T(8,128)(2,1)} custom-call(bf16[512,2048]{1,0:T(8,128)(2,1)} %get-tuple-element.83.sel_ref, bf16[2048,384]{1,0:T(8,128)(2,1)S(1)} %bitcast.21), custom_call_target="tpu_custom_call" | custom-call | flops 1024 | bytes 1024 | tf_op jit(solution)/shard_map/pallas_call | solution.py:332
  129.8 7.4 %all-to-all-start.4 = ((bf16[32,8,768]{2,1,0:T(8,128)(2,1)}), bf16[32,8,768]{2,1,0:T(8,128)(2,1)S(1)}, u32[]{:S(2)}, u32[]{:S(2)}) async-start(bf16[32,8,768]{2,1,0:T(8,128)(2,1)} %shard_map.90), calls=%async_computation.4 | async-start | bytes 786432 | tf_op jit(solution)/shard_map/all_to_all | solution.py:379
  137.2 0.0 collective-permute-done.2.a_ref
  137.3 0.0 collective-permute-done.3.b_ref
  137.3 1.4 copy-done.6
  138.7 1.4 copy-done.7
  140.1 1.6 %shard_map.89.base_ref = f32[1024,768]{1,0:T(8,128)S(1)} custom-call(f32[512,768]{1,0:T(8,128)S(1)} %copy-done.6, f32[512,768]{1,0:T(8,128)S(1)} %copy-done.7, bf16[512,768]{1,0:T(8,128)(2,1)} %collective-permute-done.2.a_ref, bf16[512,768]{1,0:T(8,128)(2,1)} %collective-permute-done.3.b_ref), custom_call_target="tpu_custom_call" | custom-call | flops 8000000000 | bytes 1024 | tf_op jit(solution)/shard_map/pallas_call | solution.py:332
  141.7 6.8 %collective-permute-done.4.a_hbm = bf16[512,768]{1,0:T(8,128)(2,1)} collective-permute-done((bf16[512,768]{1,0:T(8,128)(2,1)}, bf16[512,768]{1,0:T(8,128)(2,1)}, u32[]{:S(2)}, u32[]{:S(2)}) %collective-permute-start.4) | collective-permute-done | bytes 786464 | tf_op jit(solution)/shard_map/ppermute | solution.py:554
  148.5 0.0 collective-permute-done.5.b_hbm
  148.5 0.0 all-to-all-done.4
  148.5 2.9 %shard_map.91 = (f32[1024,768]{1,0:T(8,128)}, f32[2,16,8,768]{3,2,1,0:T(8,128)}) custom-call(f32[1024,768]{1,0:T(8,128)S(1)} %shard_map.89.base_ref, bf16[512,768]{1,0:T(8,128)(2,1)} %collective-permute-done.4.a_hbm, bf16[512,768]{1,0:T(8,128)(2,1)} %collective-permute-done.5.b_hbm, bf16[16,2,8,768]{3,2,1,0:T(8,128)(2,1)S(1)} %bitcast.24), custom_call_target="tpu_custom_call" | custom-call | flops 1024 | bytes 1024 | tf_op jit(solution)/shard_map/pallas_call | solution.py:332
  (17 shorter events, 0.0 us)
Async XLA Ops:
  0.6 10.4 %copy-start.8 = (s32[32]{0:T(128)S(1)}, s32[32]{0:T(128)}, u32[]{:S(2)}) copy-start(s32[32]{0:T(128)} %param.9) | copy-start | bytes 388
  2.5 18.3 %all-to-all-start = ((bf16[32,8,896]{2,1,0:T(8,128)(2,1)}), bf16[32,8,896]{2,1,0:T(8,128)(2,1)S(1)}, u32[]{:S(2)}, u32[]{:S(2)}) async-start(bf16[32,8,896]{2,1,0:T(8,128)(2,1)} %bitcast.29), calls=%async_computation | async-start | bytes 917504 | tf_op jit(solution)/shard_map/all_to_all | solution.py:379
  20.8 3.0 %copy-start.1 = (bf16[32,8,896]{2,1,0:T(8,128)(2,1)}, bf16[32,8,896]{2,1,0:T(8,128)(2,1)S(1)}, u32[]{:S(2)}) copy-start(bf16[32,8,896]{2,1,0:T(8,128)(2,1)S(1)} %all-to-all-done) | copy-start | bytes 1376260
  20.9 2.9 %copy-start.4 = (f32[256,128]{1,0:T(8,128)}, f32[256,128]{1,0:T(8,128)S(1)}, u32[]{:S(2)}) copy-start(f32[256,128]{1,0:T(8,128)S(1)} %broadcast_in_dim.44.held_ref) | copy-start | bytes 393220
  23.8 28.0 %all-to-all-start.1 = ((bf16[32,64,384]{2,1,0:T(8,128)(2,1)}), bf16[32,64,384]{2,1,0:T(8,128)(2,1)}, u32[]{:S(2)}, u32[]{:S(2)}) async-start(bf16[32,64,384]{2,1,0:T(8,128)(2,1)} %bitcast.4), calls=%async_computation.1 | async-start | bytes 3145728 | tf_op jit(solution)/shard_map/all_to_all | solution.py:379
  35.1 0.8 copy-start.2
  35.9 15.9 %copy-start.3 = (s32[8,1024]{1,0:T(8,128)S(1)}, s32[8,1024]{1,0:T(8,128)}, u32[]{:S(2)}) copy-start(s32[8,1024]{1,0:T(8,128)} %get-tuple-element.47.col_ref) | copy-start | bytes 98308
  65.4 18.0 %all-to-all-start.2 = ((f32[32,16,128]{2,1,0:T(8,128)}), f32[32,16,128]{2,1,0:T(8,128)S(1)}, u32[]{:S(2)}, u32[]{:S(2)}) async-start(f32[32,16,128]{2,1,0:T(8,128)} %get-tuple-element.48.stat_ref), calls=%async_computation.2 | async-start | bytes 524288 | tf_op jit(solution)/shard_map/all_to_all | solution.py:379
  85.5 8.1 %copy-start = (bf16[1024,768]{1,0:T(8,128)(2,1)S(1)}, bf16[1024,768]{1,0:T(8,128)(2,1)}, u32[]{:S(2)}) copy-start(bf16[1024,768]{1,0:T(8,128)(2,1)} %shard_map.81.u_ref) | copy-start | bytes 4718596
  85.5 8.1 %copy-start.5 = (f32[8,128]{1,0:T(8,128)S(1)}, f32[8,128]{1,0:T(8,128)}, u32[]{:S(2)}) copy-start(f32[8,128]{1,0:T(8,128)} %get-tuple-element.64.col_ref) | copy-start | bytes 12292
  90.4 24.4 %collective-permute-start = (bf16[512,768]{1,0:T(8,128)(2,1)}, bf16[512,768]{1,0:T(8,128)(2,1)}, u32[]{:S(2)}, u32[]{:S(2)}) collective-permute-start(bf16[512,768]{1,0:T(8,128)(2,1)} %get-tuple-element.72), channel_id=1, source_target_pairs={{0,32},{32,64},{64,96},{96,0},{1,33},{33,65},{65,97},{97,1},{2,34}... | collective-permute-start | bytes 2359304 | tf_op jit(solution)/shard_map/ppermute | solution.py:522
  92.0 22.9 %collective-permute-start.1 = (bf16[512,768]{1,0:T(8,128)(2,1)}, bf16[512,768]{1,0:T(8,128)(2,1)}, u32[]{:S(2)}, u32[]{:S(2)}) collective-permute-start(bf16[512,768]{1,0:T(8,128)(2,1)} %get-tuple-element.73), channel_id=1, source_target_pairs={{0,96},{32,0},{64,32},{96,64},{1,97},{33,1},{65,33},{97,65},{2,98}... | collective-permute-start | bytes 2359304 | tf_op jit(solution)/shard_map/ppermute | solution.py:523
  96.6 29.6 %all-to-all-start.3 = ((bf16[32,64,384]{2,1,0:T(8,128)(2,1)}), bf16[32,64,384]{2,1,0:T(8,128)(2,1)S(1)}, u32[]{:S(2)}, u32[]{:S(2)}) async-start(bf16[32,64,384]{2,1,0:T(8,128)(2,1)} %bitcast.28), calls=%async_computation.3 | async-start | bytes 3145728 | tf_op jit(solution)/shard_map/all_to_all | solution.py:379
  109.0 28.3 %collective-permute-start.2 = (bf16[512,768]{1,0:T(8,128)(2,1)}, bf16[512,768]{1,0:T(8,128)(2,1)}, u32[]{:S(2)}, u32[]{:S(2)}) collective-permute-start(bf16[512,768]{1,0:T(8,128)(2,1)} %get-tuple-element.79), channel_id=1, source_target_pairs={{0,96},{32,0},{64,32},{96,64},{1,97},{33,1},{65,33},{97,65},{2,98}... | collective-permute-start | bytes 2359304 | tf_op jit(solution)/shard_map/ppermute | solution.py:539
  110.8 26.5 %collective-permute-start.3 = (bf16[512,768]{1,0:T(8,128)(2,1)}, bf16[512,768]{1,0:T(8,128)(2,1)}, u32[]{:S(2)}, u32[]{:S(2)}) collective-permute-start(bf16[512,768]{1,0:T(8,128)(2,1)} %get-tuple-element.80), channel_id=1, source_target_pairs={{0,32},{32,64},{64,96},{96,0},{1,33},{33,65},{65,97},{97,1},{2,34}... | collective-permute-start | bytes 2359304 | tf_op jit(solution)/shard_map/ppermute | solution.py:538
  117.6 30.9 %collective-permute-start.4 = (bf16[512,768]{1,0:T(8,128)(2,1)}, bf16[512,768]{1,0:T(8,128)(2,1)}, u32[]{:S(2)}, u32[]{:S(2)}) collective-permute-start(bf16[512,768]{1,0:T(8,128)(2,1)} %get-tuple-element.81), channel_id=1, source_target_pairs={{0,32},{32,64},{64,96},{96,0},{1,33},{33,65},{65,97},{97,1},{2,34}... | collective-permute-start | bytes 2359304 | tf_op jit(solution)/shard_map/ppermute | solution.py:554
  118.0 30.5 %collective-permute-start.5 = (bf16[512,768]{1,0:T(8,128)(2,1)}, bf16[512,768]{1,0:T(8,128)(2,1)}, u32[]{:S(2)}, u32[]{:S(2)}) collective-permute-start(bf16[512,768]{1,0:T(8,128)(2,1)} %get-tuple-element.82), channel_id=1, source_target_pairs={{0,96},{32,0},{64,32},{96,64},{1,97},{33,1},{65,33},{97,65},{2,98}... | collective-permute-start | bytes 2359304 | tf_op jit(solution)/shard_map/ppermute | solution.py:555
  129.8 18.6 %all-to-all-start.4 = ((bf16[32,8,768]{2,1,0:T(8,128)(2,1)}), bf16[32,8,768]{2,1,0:T(8,128)(2,1)S(1)}, u32[]{:S(2)}, u32[]{:S(2)}) async-start(bf16[32,8,768]{2,1,0:T(8,128)(2,1)} %shard_map.90), calls=%async_computation.4 | async-start | bytes 786432 | tf_op jit(solution)/shard_map/all_to_all | solution.py:379
  137.3 1.4 copy-start.6
  138.7 1.4 copy-start.7
